TPU v7x, 32 devices: a whole 2x2x4 slice. The times are simulated.
32 devices in a mesh: gx: 4 (over y, core), gy: 2 (over x), gz: 4 (over z).
Axes of the slice: x: 2, y: 2, z: 4, core: 2. Of those that a mesh axis runs over, the one named last changes fastest.
Arguments:
- warmth_values: float32 [256, 32, 512], P('gx', 'gy', 'gz'), may hold values from -4 to 4
- dissolved_sugar: float32 [256, 32, 512], P('gx', 'gy', 'gz'), may hold values from 0.5 to 2
- nucleus_population: float32 [8, 256, 32, 512], P(None, 'gx', 'gy', 'gz'), may hold values from 0.05 to 1
- enlarge_coefficient_grid: float32 [256, 32, 512], P('gx', 'gy', 'gz'), may hold values from 0.05 to 0.5
- sensor_readings: bfloat16 [2, 256, 32, 512], P(None, 'gx', 'gy', 'gz'), may hold values from -4 to 4
Outputs:
- sensitivity: float32 [256, 32, 512], P('gx', 'gy', 'gz')
- misfit: float32 [], replicated
- gradient: float32 [], replicated
All inputs are finite; a program needn't handle non-finite values.
Results may differ from a plain program's by a relative error of at most 0.0003.
Values sent between devices are 32-bit elements; how exact they have to be, the bound alone decides.
No kernel may reach another device: no remote copies, remote signals or barrier semaphores. Data moves between devices by JAX's collectives and lax.ppermute only.
A program may use at most 128 MiB of HBM per device.

v0:
```python
import functools

import jax
import jax.numpy as jnp
import numpy as np
from jax import lax
from jax.experimental import pallas as pl
from jax.experimental.pallas import tpu as pltpu
from jax.sharding import PartitionSpec as P

F32 = jnp.float32
AXES = ("gx", "gy", "gz")

SOLIDIFY_POINT = 0.5
LOWERING_COEF = 0.5
GROW = 0.3
NUCLEATE = 0.2
VOLUME = 0.005
WARMTH_ADVANCE = 0.08
STEP_SOLUTE = 0.1
HIDDEN_WARMTH = 0.5
REJECT = 0.3
LANES = 128


def volumes(bin_count):
    rank = np.arange(bin_count, dtype=np.float64) + 1.0
    return VOLUME * rank * rank


def functional_weights(bin_count):
    vol = volumes(bin_count)
    step = vol[1:] - vol[:-1]
    k = (1.0, vol)
    l = (NUCLEATE * vol[0], np.concatenate([GROW * step, [0.0]]))
    m_const = GROW * step[0] * NUCLEATE
    m = np.zeros(bin_count)
    for b in range(bin_count - 1):
        m[b] -= GROW * step[b] * GROW
        if b >= 1:
            m[b - 1] += GROW * step[b] * GROW
    return k, l, (m_const, m)


def swap_pairs(count, kind):
    if kind == 0:
        return [(i, i ^ 1) for i in range(count)]
    return [(i, (i + 1) % count if i % 2 else (i - 1) % count) for i in range(count)]


def swaps(count):
    return {1: 0, 2: 1}.get(count, 2)


def exchange(payloads, axis):
    count = lax.axis_size(axis)
    assert count == 1 or count % 2 == 0
    return [lax.ppermute(p, axis, swap_pairs(count, kind)) for kind, p in enumerate(payloads)]


class Side:
    def __init__(self, axis, count):
        self.count = count
        self.index = lax.axis_index(axis)
        self.odd = lax.rem(self.index, 2) == 1

    def outgoing(self, first, last):
        kinds = [jnp.where(self.odd, first, last), jnp.where(self.odd, last, first)]
        return kinds[: swaps(self.count)]

    def incoming(self, got):
        if self.count == 1:
            return None
        if self.count == 2:
            zero = jnp.zeros_like(got[0])
            return jnp.where(self.odd, got[0], zero), jnp.where(self.odd, zero, got[0])
        a, b = got
        zero = jnp.zeros_like(a)
        before = jnp.where(self.index > 0, jnp.where(self.odd, a, b), zero)
        after = jnp.where(self.index < self.count - 1, jnp.where(self.odd, b, a), zero)
        return before, after


def grid_iota(ny):
    row = lax.broadcasted_iota(jnp.int32, (ny, LANES), 0)
    lane = lax.broadcasted_iota(jnp.int32, (ny, LANES), 1)
    return row, lane


def pack_z(acc, value, x, lane):
    high = pltpu.roll(value, lax.rem(2 * x + 1, LANES), 1)
    low = pltpu.roll(value, lax.rem(2 * x + LANES - 1, LANES), 1)
    acc = jnp.where(lane == 2 * x, high, acc)
    return jnp.where(lane == lax.rem(2 * x + LANES - 1, LANES), low, acc)


class Halo:
    def __init__(self, dims, counts, fields, got, scratch):
        self.nx, self.ny = dims
        self.fields = fields
        self.xs, self.ys, self.zs = scratch
        nx, ny = dims
        gx, gy, gz = got
        sx, sy, sz = [Side(a, n) for a, n in zip(AXES, counts)]
        before, after = sx.incoming([r[...] for r in gx])
        self.xs[0], self.xs[1] = before, after
        before, after = sy.incoming([r[...] for r in gy])
        self.ys[0], self.ys[1] = before, after
        before, after = sz.incoming([r[...] for r in gz])
        lane = lax.broadcasted_iota(jnp.int32, before.shape, 1)
        self.zs[...] = jnp.where(lax.rem(lane, 2) == 0, before, after)

    def x(self, f, side):
        return self.xs[side, pl.ds(f * self.ny, self.ny), :]

    def y(self, f, side, x):
        return self.ys[side, pl.ds(f * self.nx + x, 1), :]

    def z(self, f, x):
        packed = self.zs[pl.ds(f * self.ny, self.ny), :]
        return pltpu.roll(packed, lax.rem(LANES - 2 * x + LANES, LANES), 1)


def halo_scratch(dims, fields):
    nx, ny = dims
    return [
        pltpu.VMEM((2, fields * ny, LANES), F32),
        pltpu.VMEM((2, fields * nx, LANES), F32),
        pltpu.VMEM((fields * ny, LANES), F32),
    ]


def around(cur, ym, yp, zr, row, lane):
    ny = cur.shape[0]
    return [
        jnp.where(row == 0, ym, pltpu.roll(cur, 1, 0)),
        jnp.where(row == ny - 1, yp, pltpu.roll(cur, ny - 1, 0)),
        jnp.where(lane == 0, zr, pltpu.roll(cur, 1, 1)),
        jnp.where(lane == LANES - 1, zr, pltpu.roll(cur, LANES - 1, 1)),
    ]


def put_faces(dims, counts, fields, outs, zaccs):
    nx, ny = dims
    ox, oy, oz = outs
    sx, sy, _ = [Side(a, n) for a, n in zip(AXES, counts)]
    for f, ref in enumerate(fields):
        first, last = ref[pl.ds(0, ny), :], ref[pl.ds((nx - 1) * ny, ny), :]
        for o, v in zip(ox, sx.outgoing(first, last)):
            o[pl.ds(f * ny, ny), :] = v
        first = ref[pl.ds(0, nx, stride=ny), :]
        last = ref[pl.ds(ny - 1, nx, stride=ny), :]
        for o, v in zip(oy, sy.outgoing(first, last)):
            o[pl.ds(f * nx, nx), :] = v
        for o in oz:
            o[pl.ds(f * ny, ny), :] = zaccs[f]


def face_shapes(dims, counts, fields):
    nx, ny = dims
    rows = (fields * ny, fields * nx, fields * ny)
    shapes = []
    for axis, (r, n) in enumerate(zip(rows, counts)):
        copies = min(swaps(n), 1) if axis == 2 else swaps(n)
        shapes += [((r, LANES), F32)] * copies
    return shapes


def split_faces(refs, counts):
    ax, ay = swaps(counts[0]), swaps(counts[1])
    return refs[:ax], refs[ax : ax + ay], refs[ax + ay :]


def send_faces(faces, counts):
    ox, oy, oz = split_faces(list(faces), counts)
    oz = [oz[0]] * swaps(counts[2])
    got = []
    for payload, axis in zip((ox, oy, oz), AXES):
        got += exchange(payload, axis)
    return got


def log1p_of(e, u, inv):
    return jnp.log(u) + (e - (u - 1.0)) * inv


def softplus_parts(v):
    e = jnp.exp(-jnp.abs(v))
    u = 1.0 + e
    inv = 1.0 / u
    soft = jnp.maximum(v, 0.0) + log1p_of(e, u, inv)
    return soft, jnp.where(v >= 0, inv, e * inv)


def prepare_kernel(dims, counts, bins, chunks, *refs):
    nx, ny = dims
    nface = len(face_shapes(dims, counts, 3))
    c_hbm, t_hbm, s_hbm = refs[:3]
    k_ref, l_ref, m_ref, t_ref, s_ref = refs[3:8]
    outs = split_faces(refs[8 : 8 + nface], counts)
    c_ref, sems = refs[8 + nface :]
    rows = nx * ny // chunks
    copies = [
        pltpu.make_async_copy(t_hbm, t_ref, sems.at[chunks]),
        pltpu.make_async_copy(s_hbm, s_ref, sems.at[chunks + 1]),
    ]
    for j in range(chunks):
        part = pl.ds(j * rows, rows)
        copies.append(pltpu.make_async_copy(c_hbm.at[:, part, :], c_ref.at[:, part, :], sems.at[j]))
    for copy in copies:
        copy.start()
    copies[0].wait()
    copies[1].wait()
    _, lane = grid_iota(ny)
    weights = functional_weights(bins)

    def plane(x, accs):
        here = pl.ds(x * ny, ny)
        c = [c_ref[b, here, :] for b in range(bins)]
        values = []
        for const, per_bin in weights:
            total = None
            for b in range(bins):
                if per_bin[b] != 0.0:
                    term = float(per_bin[b]) * c[b]
                    total = term if total is None else total + term
            values.append(float(const) + total)
        k_ref[here, :], l_ref[here, :], m_ref[here, :] = values
        faces = (t_ref[here, :], s_ref[here, :], values[0])
        return tuple(pack_z(a, v, x, lane) for a, v in zip(accs, faces))

    accs = tuple(jnp.zeros((ny, LANES), F32) for _ in range(3))
    planes = nx // chunks
    for j in range(chunks):
        copies[2 + j].wait()
        accs = lax.fori_loop(j * planes, (j + 1) * planes, plane, accs, unroll=2)
    put_faces(dims, counts, (t_ref, s_ref, k_ref), outs, accs)


def first_step_kernel(dims, counts, *refs):
    nx, ny = dims
    ngot = sum(swaps(n) for n in counts)
    nface = len(face_shapes(dims, counts, 4))
    t_ref, s_ref, g_ref, k_ref, l_ref, m_ref = refs[:6]
    got = refs[6 : 6 + ngot]
    t1, s1, k1, h0, l1, w0, v0 = refs[6 + ngot : 13 + ngot]
    outs = split_faces(refs[13 + ngot : 13 + ngot + nface], counts)
    scratch = refs[13 + ngot + nface :]
    a, b = swaps(counts[0]), swaps(counts[1])
    halo = Halo(dims, counts, 3, (got[:a], got[a : a + b], got[a + b :]), scratch)
    row, lane = grid_iota(ny)
    fields = (t_ref, s_ref, k_ref)

    def plane(x, carry):
        prev, cur, accs = carry
        here = pl.ds(x * ny, ny)
        ahead = pl.ds(jnp.minimum(x + 1, nx - 1) * ny, ny)
        nxt = tuple(
            jnp.where(x == nx - 1, halo.x(f, 1), r[ahead, :]) for f, r in enumerate(fields)
        )
        near = [
            [prev[f], nxt[f]]
            + around(cur[f], halo.y(f, 0, x), halo.y(f, 1, x), halo.z(f, x), row, lane)
            for f in range(3)
        ]
        t, s, k = cur
        heat = None
        for tn, kn in zip(near[0], near[2]):
            term = (k + kn) * (tn - t)
            heat = term if heat is None else heat + term
        heat = 0.5 * heat
        diff = near[1][0]
        for sn in near[1][1:]:
            diff = diff + sn
        diff = diff - 6.0 * s
        g, l, m = g_ref[here, :], l_ref[here, :], m_ref[here, :]
        soft, _ = softplus_parts(SOLIDIFY_POINT - LOWERING_COEF * s - t)
        w, v = soft * l, soft * m
        frost = g * w
        new_t = t + WARMTH_ADVANCE * heat + HIDDEN_WARMTH * frost
        new_s = s + STEP_SOLUTE * diff + REJECT * frost
        new_k = k + frost
        t1[here, :], s1[here, :], k1[here, :], h0[here, :] = new_t, new_s, new_k, heat
        l1[here, :], w0[here, :], v0[here, :] = l + g * v, w, v
        accs = tuple(
            pack_z(a, z, x, lane) for a, z in zip(accs, (new_t, new_s, new_k, heat))
        )
        return cur, nxt, accs

    prev = tuple(halo.x(f, 0) for f in range(3))
    cur = tuple(r[pl.ds(0, ny), :] for r in fields)
    accs = tuple(jnp.zeros((ny, LANES), F32) for _ in range(4))
    _, _, accs = lax.fori_loop(0, nx, plane, (prev, cur, accs), unroll=2)
    put_faces(dims, counts, (t1, s1, k1, h0), outs, accs)


def second_step_kernel(dims, counts, *refs):
    nx, ny = dims
    ngot = sum(swaps(n) for n in counts)
    nface = len(face_shapes(dims, counts, 2))
    t_ref, s_ref, k_ref, h_ref, l_ref, w_ref, v_ref, g_ref, r_ref = refs[:9]
    got = refs[9 : 9 + ngot]
    mt_ref, ms_ref, sense_ref, sums_ref = refs[9 + ngot : 13 + ngot]
    outs = split_faces(refs[13 + ngot : 13 + ngot + nface], counts)
    scratch = refs[13 + ngot + nface :]
    a, b = swaps(counts[0]), swaps(counts[1])
    halo = Halo(dims, counts, 4, (got[:a], got[a : a + b], got[a + b :]), scratch)
    row, lane = grid_iota(ny)
    fields = (t_ref, s_ref, k_ref, h_ref)

    def plane(x, carry):
        prev, cur, accs, sums = carry
        here = pl.ds(x * ny, ny)
        ahead = pl.ds(jnp.minimum(x + 1, nx - 1) * ny, ny)
        nxt = tuple(
            jnp.where(x == nx - 1, halo.x(f, 1), r[ahead, :]) for f, r in enumerate(fields)
        )
        near = [
            [prev[f], nxt[f]]
            + around(cur[f], halo.y(f, 0, x), halo.y(f, 1, x), halo.z(f, x), row, lane)
            for f in range(4)
        ]
        t, s, k, h = cur
        heat = again = None
        for tn, kn, hn in zip(near[0], near[2], near[3]):
            both = k + kn
            term, other = both * (tn - t), both * (hn - h)
            heat = term if heat is None else heat + term
            again = other if again is None else again + other
        heat = 0.5 * heat
        diff = near[1][0]
        for sn in near[1][1:]:
            diff = diff + sn
        diff = diff - 6.0 * s
        g, l = g_ref[here, :], l_ref[here, :]
        w, v = w_ref[here, :], v_ref[here, :]
        soft, slope = softplus_parts(SOLIDIFY_POINT - LOWERING_COEF * s - t)
        speed = g * soft
        frost = speed * l
        miss_t = (
            t + WARMTH_ADVANCE * heat + HIDDEN_WARMTH * frost - r_ref[0, here, :].astype(F32)
        )
        miss_s = s + STEP_SOLUTE * diff + REJECT * frost - r_ref[1, here, :].astype(F32)
        pull = HIDDEN_WARMTH * miss_t + REJECT * miss_s
        by_speed = pull * l
        below = by_speed * g * slope
        part_t = miss_t - below
        part_s = miss_s - LOWERING_COEF * below
        pull_0 = HIDDEN_WARMTH * part_t + REJECT * part_s
        mt_ref[here, :], ms_ref[here, :] = miss_t, miss_s
        sense_ref[here, :] = by_speed * soft + pull_0 * w + speed * pull * v
        misfit, part = sums
        misfit = misfit + (miss_t * miss_t + miss_s * miss_s)
        part = part + (
            miss_t * heat + part_t * h + (0.5 * WARMTH_ADVANCE) * miss_t * again
        )
        accs = tuple(pack_z(a, z, x, lane) for a, z in zip(accs, (miss_t, miss_s)))
        return cur, nxt, accs, (misfit, part)

    zero = jnp.zeros((ny, LANES), F32)
    prev = tuple(halo.x(f, 0) for f in range(4))
    cur = tuple(r[pl.ds(0, ny), :] for r in fields)
    _, _, accs, (misfit, part) = lax.fori_loop(
        0, nx, plane, (prev, cur, (zero, zero), (zero, zero)), unroll=2
    )
    put_faces(dims, counts, (mt_ref, ms_ref), outs, accs)
    lane_row = lax.broadcasted_iota(jnp.int32, (1, LANES), 1)
    line = jnp.where(lane_row == 0, 0.5 * jnp.sum(misfit), 0.0)
    line = jnp.where(lane_row == 1, WARMTH_ADVANCE * jnp.sum(part), line)
    sums_ref[...] = jnp.broadcast_to(line, sums_ref.shape)


def finish_kernel(dims, counts, cells, *refs):
    nx, ny = dims
    ngot = sum(swaps(n) for n in counts)
    t_ref, k_ref, mt_ref, ms_ref, w_ref, sense_ref, sums_ref = refs[:7]
    old = refs[7 : 7 + ngot]
    got = refs[7 + ngot : 7 + 2 * ngot]
    out_ref, misfit_ref, gradient_ref = refs[7 + 2 * ngot : 10 + 2 * ngot]
    scratch = refs[10 + 2 * ngot :]
    a, b = swaps(counts[0]), swaps(counts[1])
    before = Halo(dims, counts, 4, (old[:a], old[a : a + b], old[a + b :]), scratch[:3])
    halo = Halo(dims, counts, 2, (got[:a], got[a : a + b], got[a + b :]), scratch[3:])
    row, lane = grid_iota(ny)

    def edge(call):
        return 0.5 * call(before, 2) - call(before, 0), call(halo, 0), call(halo, 1)

    def load(here):
        return 0.5 * k_ref[here, :] - t_ref[here, :], mt_ref[here, :], ms_ref[here, :]

    def plane(x, carry):
        prev, cur = carry
        here = pl.ds(x * ny, ny)
        ahead = pl.ds(jnp.minimum(x + 1, nx - 1) * ny, ny)
        last = edge(lambda u, f: u.x(f, 1))
        nxt = tuple(jnp.where(x == nx - 1, e, v) for e, v in zip(last, load(ahead)))
        ym = edge(lambda u, f: u.y(f, 0, x))
        yp = edge(lambda u, f: u.y(f, 1, x))
        zr = edge(lambda u, f: u.z(f, x))
        near = [
            [prev[f], nxt[f]] + around(cur[f], ym[f], yp[f], zr[f], row, lane) for f in range(3)
        ]
        _, mt, ms = cur
        own = 0.5 * k_ref[here, :] + t_ref[here, :]
        flux = diff = None
        for qn, tn, sn in zip(*near):
            term = (tn - mt) * (own + qn)
            flux = term if flux is None else flux + term
            diff = sn if diff is None else diff + sn
        diff = diff - 6.0 * ms
        total = (0.5 * WARMTH_ADVANCE) * flux + (REJECT * STEP_SOLUTE) * diff
        out_ref[here, :] = sense_ref[here, :] + w_ref[here, :] * total
        return cur, nxt

    prev = edge(lambda u, f: u.x(f, 0))
    lax.fori_loop(0, nx, plane, (prev, load(pl.ds(0, ny))), unroll=2)
    sums = sums_ref[...]
    which = lax.broadcasted_iota(jnp.int32, sums.shape, 1)
    misfit_ref[0, 0] = jnp.sum(jnp.where(which == 0, sums, 0.0)) / cells
    gradient_ref[0, 0] = jnp.sum(jnp.where(which == 1, sums, 0.0)) / cells


VM = pl.BlockSpec(memory_space=pltpu.VMEM)
SM = pl.BlockSpec(memory_space=pltpu.SMEM)


def call(kernel, out, args, scratch=(), in_specs=None, out_specs=None, name=None):
    return pl.pallas_call(
        kernel,
        out_shape=[jax.ShapeDtypeStruct(s, d) for s, d in out],
        in_specs=in_specs or [VM] * len(args),
        out_specs=out_specs or [VM] * len(out),
        scratch_shapes=list(scratch),
        name=name,
        compiler_params=pltpu.CompilerParams(vmem_limit_bytes=32 << 20),
    )(*args)


def per_device(counts, warmth, sugar, population, coefficient, sensors):
    nx, ny, nz = warmth.shape
    assert nz == LANES and 2 * nx <= LANES
    bins = population.shape[0]
    dims = (nx, ny)
    cells = nx * ny
    t, s, g = [v.reshape(cells, nz) for v in (warmth, sugar, coefficient)]
    c = population.reshape(bins, cells, nz)
    r = sensors.reshape(2, cells, nz)
    field = ((cells, nz), F32)
    hbm = pl.BlockSpec(memory_space=pl.ANY)

    chunks = 8
    out = [field] * 5 + face_shapes(dims, counts, 3)
    res = call(
        functools.partial(prepare_kernel, dims, counts, bins, chunks),
        out,
        (c, t, s),
        [pltpu.VMEM((bins, cells, nz), F32), pltpu.SemaphoreType.DMA((chunks + 2,))],
        in_specs=[hbm] * 3,
        name="prepare",
    )
    k, l, m, t, s = res[:5]
    got = send_faces(res[5:], counts)

    out = [field] * 7 + face_shapes(dims, counts, 4)
    res = call(
        functools.partial(first_step_kernel, dims, counts),
        out,
        (t, s, g, k, l, m, *got),
        halo_scratch(dims, 3),
        name="first_step",
    )
    t1, s1, k1, h0, l1, w0, v0 = res[:7]
    got1 = send_faces(res[7:], counts)

    devices = int(np.prod(counts))
    out = [field] * 3 + [((devices, LANES), F32)] + face_shapes(dims, counts, 2)
    res = call(
        functools.partial(second_step_kernel, dims, counts),
        out,
        (t1, s1, k1, h0, l1, w0, v0, g, r, *got1),
        halo_scratch(dims, 4),
        name="second_step",
    )
    mt, ms, sense, sums = res[:4]
    got2 = send_faces(res[4:], counts)
    sums = lax.all_to_all(sums, AXES, 0, 0, tiled=True)

    sens, misfit, gradient = call(
        functools.partial(finish_kernel, dims, counts, float(cells * nz * devices)),
        [field, ((1, 1), F32), ((1, 1), F32)],
        (t1, k1, mt, ms, w0, sense, sums, *got1, *got2),
        halo_scratch(dims, 4) + halo_scratch(dims, 2),
        out_specs=[VM, SM, SM],
        name="finish",
    )
    return sens.reshape(nx, ny, nz), misfit.reshape(()), gradient.reshape(())


def solution(mesh):
    counts = tuple(mesh.shape[a] for a in AXES)
    placed = (
        P("gx", "gy", "gz"),
        P("gx", "gy", "gz"),
        P(None, "gx", "gy", "gz"),
        P("gx", "gy", "gz"),
        P(None, "gx", "gy", "gz"),
    )
    return jax.shard_map(
        functools.partial(per_device, counts),
        mesh=mesh,
        in_specs=placed,
        out_specs=(P("gx", "gy", "gz"), P(), P()),
        check_vma=False,
    )
```

profile of v0, /device:TPU:0, one launch (start us, length us, event | category | flops | bytes accessed | tf_op | source)
XLA Modules:
  0.0 60.0 jit_solution(2035947573917245530)
XLA Ops:
  0.6 2.2 %copy-done = f32[8,64,16,128]{3,2,1,0:T(8,128)S(1)} copy-done((f32[8,64,16,128]{3,2,1,0:T(8,128)S(1)}, f32[8,64,16,128]{3,2,1,0:T(8,128)}, u32[]{:S(2)}) %copy-start) | copy-done | bytes 4194328
  2.8 1.0 %copy-done.2 = f32[64,16,128]{2,1,0:T(8,128)S(1)} copy-done((f32[64,16,128]{2,1,0:T(8,128)S(1)}, f32[64,16,128]{2,1,0:T(8,128)}, u32[]{:S(2)}) %copy-start.2) | copy-done | bytes 524312
  3.9 1.0 %copy-done.3 = f32[64,16,128]{2,1,0:T(8,128)S(1)} copy-done((f32[64,16,128]{2,1,0:T(8,128)S(1)}, f32[64,16,128]{2,1,0:T(8,128)}, u32[]{:S(2)}) %copy-start.3) | copy-done | bytes 524312
  4.9 3.8 %prepare.1 = (f32[1024,128]{1,0:T(8,128)S(1)}, f32[1024,128]{1,0:T(8,128)S(1)}, f32[1024,128]{1,0:T(8,128)S(1)}, f32[1024,128]{1,0:T(8,128)S(1)}, f32[1024,128]{...) custom-call(f32[8,1024,128]{2,1,0:T(8,128)S(1)} %bitcast.12, ...), custom_call_target="tpu_custom_call" | custom-call | tf_op jit(solution)/shard_map/prepare/pallas_call | solution.py:429
  8.7 3.0 %collective-permute-start.2 = (f32[192,128]{1,0:T(8,128)S(1)}, f32[192,128]{1,0:T(8,128)S(1)}, u32[]{:S(2)}, u32[]{:S(2)}) collective-permute-start(f32[192,128]{1,0:T(8,128)S(1)} %get-tuple-element.41), channel_id=1, source_target_pairs={{0,4},{4,0},{1,5},{5,1},{2,6},{6,2},{3,7},{7,3},{8,12},{12,8},{9,1... | collective-permute-start | bytes 294920 | tf_op jit(solution)/shard_map/ppermute | solution.py:58
  11.7 1.6 %collective-permute-start.1 = (f32[48,128]{1,0:T(8,128)S(1)}, f32[48,128]{1,0:T(8,128)S(1)}, u32[]{:S(2)}, u32[]{:S(2)}) collective-permute-start(f32[48,128]{1,0:T(8,128)S(1)} %get-tuple-element.40), channel_id=1, source_target_pairs={{0,24},{8,16},{16,8},{24,0},{1,25},{9,17},{17,9},{25,1},{2,26},{10... | collective-permute-start | bytes 73736 | tf_op jit(solution)/shard_map/ppermute | solution.py:58
  13.4 3.6 %collective-permute-start.4 = (f32[48,128]{1,0:T(8,128)S(1)}, f32[48,128]{1,0:T(8,128)S(1)}, u32[]{:S(2)}, u32[]{:S(2)}) collective-permute-start(f32[48,128]{1,0:T(8,128)S(1)} %get-tuple-element.42), channel_id=1, source_target_pairs={{0,3},{1,2},{2,1},{3,0},{4,7},{5,6},{6,5},{7,4},{8,11},{9,10},{10,... | collective-permute-start | bytes 73736 | tf_op jit(solution)/shard_map/ppermute | solution.py:58
  17.0 2.0 %collective-permute-done.4.refs_10_ = f32[48,128]{1,0:T(8,128)S(1)} collective-permute-done((f32[48,128]{1,0:T(8,128)S(1)}, f32[48,128]{1,0:T(8,128)S(1)}, u32[]{:S(2)}, u32[]{:S(2)}) %collective-permute-start.4) | collective-permute-done | bytes 24608 | tf_op jit(solution)/shard_map/ppermute | solution.py:58
  19.0 1.8 %collective-permute-done.3.refs_9_ = f32[48,128]{1,0:T(8,128)S(1)} collective-permute-done((f32[48,128]{1,0:T(8,128)S(1)}, f32[48,128]{1,0:T(8,128)S(1)}, u32[]{:S(2)}, u32[]{:S(2)}) %collective-permute-start.3) | collective-permute-done | bytes 24608 | tf_op jit(solution)/shard_map/ppermute | solution.py:58
  20.8 6.3 %first_step.1 = (f32[1024,128]{1,0:T(8,128)S(1)}, f32[1024,128]{1,0:T(8,128)S(1)}, f32[1024,128]{1,0:T(8,128)S(1)}, f32[1024,128]{1,0:T(8,128)S(1)}, f32[1024,12...) custom-call(f32[1024,128]{1,0:T(8,128)S(1)} %get-tuple-element.34.re, ...), custom_call_target="tpu_custom_call" | custom-call | tf_op jit(solution)/shard_map/first_step/pallas_call | solution.py:429
  27.1 0.6 collective-permute-start.7
  27.7 0.6 %collective-permute-start.6 = (f32[64,128]{1,0:T(8,128)S(1)}, f32[64,128]{1,0:T(8,128)S(1)}, u32[]{:S(2)}, u32[]{:S(2)}) collective-permute-start(f32[64,128]{1,0:T(8,128)S(1)} %get-tuple-element.51), channel_id=1, source_target_pairs={{0,24},{8,16},{16,8},{24,0},{1,25},{9,17},{17,9},{25,1},{2,26},{10... | collective-permute-start | bytes 98312 | tf_op jit(solution)/shard_map/ppermute | solution.py:58
  28.3 1.8 %collective-permute-start.9 = (f32[64,128]{1,0:T(8,128)S(1)}, f32[64,128]{1,0:T(8,128)S(1)}, u32[]{:S(2)}, u32[]{:S(2)}) collective-permute-start(f32[64,128]{1,0:T(8,128)S(1)} %get-tuple-element.53), channel_id=1, source_target_pairs={{0,3},{1,2},{2,1},{3,0},{4,7},{5,6},{6,5},{7,4},{8,11},{9,10},{10,... | collective-permute-start | bytes 98312 | tf_op jit(solution)/shard_map/ppermute | solution.py:58
  30.2 0.9 %collective-permute-done.6.refs_10_.refs_8_ = f32[64,128]{1,0:T(8,128)S(1)} collective-permute-done((f32[64,128]{1,0:T(8,128)S(1)}, f32[64,128]{1,0:T(8,128)S(1)}, u32[]{:S(2)}, u32[]{:S(2)}) %collective-permute-start.6) | collective-permute-done | bytes 32800 | tf_op jit(solution)/shard_map/ppermute | solution.py:58
  31.1 3.0 %collective-permute-done.9.refs_13_.refs_11_ = f32[64,128]{1,0:T(8,128)S(1)} collective-permute-done((f32[64,128]{1,0:T(8,128)S(1)}, f32[64,128]{1,0:T(8,128)S(1)}, u32[]{:S(2)}, u32[]{:S(2)}) %collective-permute-start.9) | collective-permute-done | bytes 32800 | tf_op jit(solution)/shard_map/ppermute | solution.py:58
  34.1 0.3 collective-permute-done.8.refs_12_.refs_10_
  34.4 7.1 %second_step.1 = (f32[1024,128]{1,0:T(8,128)S(1)}, f32[1024,128]{1,0:T(8,128)S(1)}, f32[1024,128]{1,0:T(8,128)S(1)}, f32[32,128]{1,0:T(8,128)}, f32[32,128]{1,0:...) custom-call(f32[1024,128]{1,0:T(8,128)S(1)} %get-tuple-element.43.refs_0_, ...), custom_call_target="tpu_custom_call" | custom-call | tf_op jit(solution)/shard_map/second_step/pallas_call | solution.py:429
  41.5 1.5 %collective-permute-start.12 = (f32[128,128]{1,0:T(8,128)}, f32[128,128]{1,0:T(8,128)S(1)}, u32[]{:S(2)}, u32[]{:S(2)}) collective-permute-start(f32[128,128]{1,0:T(8,128)} %get-tuple-element.60), channel_id=1, source_target_pairs={{0,4},{4,0},{1,5},{5,1},{2,6},{6,2},{3,7},{7,3},{8,12},{12,8},{9,1... | collective-permute-start | bytes 196616 | tf_op jit(solution)/shard_map/ppermute | solution.py:58
  43.0 3.1 %all-to-all-start = ((f32[32,1,128]{2,1,0:T(1,128)}), f32[32,1,128]{2,1,0:T(1,128)S(1)}, u32[]{:S(2)}, u32[]{:S(2)}) async-start(f32[32,1,128]{2,1,0:T(1,128)} %bitcast.6), calls=%async_computation | async-start | bytes 32768 | tf_op jit(solution)/shard_map/all_to_all | solution.py:487
  46.4 1.6 %collective-permute-start.11 = (f32[32,128]{1,0:T(8,128)}, f32[32,128]{1,0:T(8,128)S(1)}, u32[]{:S(2)}, u32[]{:S(2)}) collective-permute-start(f32[32,128]{1,0:T(8,128)} %get-tuple-element.59), channel_id=1, source_target_pairs={{0,24},{8,16},{16,8},{24,0},{1,25},{9,17},{17,9},{25,1},{2,26},{10... | collective-permute-start | bytes 49160 | tf_op jit(solution)/shard_map/ppermute | solution.py:58
  48.1 3.3 %collective-permute-start.14 = (f32[32,128]{1,0:T(8,128)}, f32[32,128]{1,0:T(8,128)S(1)}, u32[]{:S(2)}, u32[]{:S(2)}) collective-permute-start(f32[32,128]{1,0:T(8,128)} %get-tuple-element.61), channel_id=1, source_target_pairs={{0,3},{1,2},{2,1},{3,0},{4,7},{5,6},{6,5},{7,4},{8,11},{9,10},{10,... | collective-permute-start | bytes 49160 | tf_op jit(solution)/shard_map/ppermute | solution.py:58
  51.4 2.4 %collective-permute-done.14.refs_16_ = f32[32,128]{1,0:T(8,128)S(1)} collective-permute-done((f32[32,128]{1,0:T(8,128)}, f32[32,128]{1,0:T(8,128)S(1)}, u32[]{:S(2)}, u32[]{:S(2)}) %collective-permute-start.14) | collective-permute-done | bytes 16416 | tf_op jit(solution)/shard_map/ppermute | solution.py:58
  53.8 1.5 %collective-permute-done.13.refs_15_ = f32[32,128]{1,0:T(8,128)S(1)} collective-permute-done((f32[32,128]{1,0:T(8,128)}, f32[32,128]{1,0:T(8,128)S(1)}, u32[]{:S(2)}, u32[]{:S(2)}) %collective-permute-start.13) | collective-permute-done | bytes 16416 | tf_op jit(solution)/shard_map/ppermute | solution.py:58
  55.4 4.7 %finish.1 = (f32[1024,128]{1,0:T(8,128)}, f32[1,1]{1,0:T(1,128)}, f32[1,1]{1,0:T(1,128)}) custom-call(f32[1024,128]{1,0:T(8,128)S(1)} %get-tuple-element.43.refs_0_, f32[1024,128]{1,0:T(8,128)S(1)} %get-tuple-element.44.refs_2_.refs_1_, f32[1024,128]{1,0:T(8,128)S(1)} %get-tuple-element.54.refs_2_, f32[1024,128]{1,0:T(8,128)S(1)} %get-tuple-element.55.refs_3_, ...), custom_call_target="tpu_custom_call" | custom-call | tf_op jit(solution)/shard_map/finish/pallas_call | solution.py:429
  (22 shorter events, 0.4 us)
Async XLA Ops:
  0.6 2.2 %copy-start = (f32[8,64,16,128]{3,2,1,0:T(8,128)S(1)}, f32[8,64,16,128]{3,2,1,0:T(8,128)}, u32[]{:S(2)}) copy-start(f32[8,64,16,128]{3,2,1,0:T(8,128)} %param.7) | copy-start | bytes 12582916
  2.8 1.0 %copy-start.2 = (f32[64,16,128]{2,1,0:T(8,128)S(1)}, f32[64,16,128]{2,1,0:T(8,128)}, u32[]{:S(2)}) copy-start(f32[64,16,128]{2,1,0:T(8,128)} %param.5) | copy-start | bytes 1572868
  3.9 1.0 %copy-start.3 = (f32[64,16,128]{2,1,0:T(8,128)S(1)}, f32[64,16,128]{2,1,0:T(8,128)}, u32[]{:S(2)}) copy-start(f32[64,16,128]{2,1,0:T(8,128)} %param.6) | copy-start | bytes 1572868
  4.9 15.9 %copy-start.1 = (f32[64,16,128]{2,1,0:T(8,128)S(1)}, f32[64,16,128]{2,1,0:T(8,128)}, u32[]{:S(2)}) copy-start(f32[64,16,128]{2,1,0:T(8,128)} %param.8) | copy-start | bytes 1572868
  4.9 29.5 %copy-start.4 = (bf16[2,64,16,128]{3,2,1,0:T(8,128)(2,1)S(1)}, bf16[2,64,16,128]{3,2,1,0:T(8,128)(2,1)}, u32[]{:S(2)}) copy-start(bf16[2,64,16,128]{3,2,1,0:T(8,128)(2,1)} %param.9) | copy-start | bytes 1572868
  8.7 12.1 %collective-permute-start.2 = (f32[192,128]{1,0:T(8,128)S(1)}, f32[192,128]{1,0:T(8,128)S(1)}, u32[]{:S(2)}, u32[]{:S(2)}) collective-permute-start(f32[192,128]{1,0:T(8,128)S(1)} %get-tuple-element.41), channel_id=1, source_target_pairs={{0,4},{4,0},{1,5},{5,1},{2,6},{6,2},{3,7},{7,3},{8,12},{12,8},{9,1... | collective-permute-start | bytes 294920 | tf_op jit(solution)/shard_map/ppermute | solution.py:58
  11.7 5.2 %collective-permute-start = (f32[48,128]{1,0:T(8,128)S(1)}, f32[48,128]{1,0:T(8,128)S(1)}, u32[]{:S(2)}, u32[]{:S(2)}) collective-permute-start(f32[48,128]{1,0:T(8,128)S(1)} %get-tuple-element.39), channel_id=1, source_target_pairs={{0,8},{8,0},{16,24},{24,16},{1,9},{9,1},{17,25},{25,17},{2,10},{10... | collective-permute-start | bytes 73736 | tf_op jit(solution)/shard_map/ppermute | solution.py:58
  11.7 5.2 %collective-permute-start.1 = (f32[48,128]{1,0:T(8,128)S(1)}, f32[48,128]{1,0:T(8,128)S(1)}, u32[]{:S(2)}, u32[]{:S(2)}) collective-permute-start(f32[48,128]{1,0:T(8,128)S(1)} %get-tuple-element.40), channel_id=1, source_target_pairs={{0,24},{8,16},{16,8},{24,0},{1,25},{9,17},{17,9},{25,1},{2,26},{10... | collective-permute-start | bytes 73736 | tf_op jit(solution)/shard_map/ppermute | solution.py:58
  13.4 5.6 %collective-permute-start.4 = (f32[48,128]{1,0:T(8,128)S(1)}, f32[48,128]{1,0:T(8,128)S(1)}, u32[]{:S(2)}, u32[]{:S(2)}) collective-permute-start(f32[48,128]{1,0:T(8,128)S(1)} %get-tuple-element.42), channel_id=1, source_target_pairs={{0,3},{1,2},{2,1},{3,0},{4,7},{5,6},{6,5},{7,4},{8,11},{9,10},{10,... | collective-permute-start | bytes 73736 | tf_op jit(solution)/shard_map/ppermute | solution.py:58
  17.0 3.8 %collective-permute-start.3 = (f32[48,128]{1,0:T(8,128)S(1)}, f32[48,128]{1,0:T(8,128)S(1)}, u32[]{:S(2)}, u32[]{:S(2)}) collective-permute-start(f32[48,128]{1,0:T(8,128)S(1)} %get-tuple-element.42), channel_id=1, source_target_pairs={{0,1},{1,0},{2,3},{3,2},{4,5},{5,4},{6,7},{7,6},{8,9},{9,8},{10,11... | collective-permute-start | bytes 73736 | tf_op jit(solution)/shard_map/ppermute | solution.py:58
  27.1 7.3 %collective-permute-start.7 = (f32[256,128]{1,0:T(8,128)S(1)}, f32[256,128]{1,0:T(8,128)S(1)}, u32[]{:S(2)}, u32[]{:S(2)}) collective-permute-start(f32[256,128]{1,0:T(8,128)S(1)} %get-tuple-element.52), channel_id=1, source_target_pairs={{0,4},{4,0},{1,5},{5,1},{2,6},{6,2},{3,7},{7,3},{8,12},{12,8},{9,1... | collective-permute-start | bytes 393224 | tf_op jit(solution)/shard_map/ppermute | solution.py:58
  27.7 2.4 %collective-permute-start.5 = (f32[64,128]{1,0:T(8,128)S(1)}, f32[64,128]{1,0:T(8,128)S(1)}, u32[]{:S(2)}, u32[]{:S(2)}) collective-permute-start(f32[64,128]{1,0:T(8,128)S(1)} %get-tuple-element.50), channel_id=1, source_target_pairs={{0,8},{8,0},{16,24},{24,16},{1,9},{9,1},{17,25},{25,17},{2,10},{10... | collective-permute-start | bytes 98312 | tf_op jit(solution)/shard_map/ppermute | solution.py:58
  27.7 3.3 %collective-permute-start.6 = (f32[64,128]{1,0:T(8,128)S(1)}, f32[64,128]{1,0:T(8,128)S(1)}, u32[]{:S(2)}, u32[]{:S(2)}) collective-permute-start(f32[64,128]{1,0:T(8,128)S(1)} %get-tuple-element.51), channel_id=1, source_target_pairs={{0,24},{8,16},{16,8},{24,0},{1,25},{9,17},{17,9},{25,1},{2,26},{10... | collective-permute-start | bytes 98312 | tf_op jit(solution)/shard_map/ppermute | solution.py:58
  28.3 5.7 %collective-permute-start.9 = (f32[64,128]{1,0:T(8,128)S(1)}, f32[64,128]{1,0:T(8,128)S(1)}, u32[]{:S(2)}, u32[]{:S(2)}) collective-permute-start(f32[64,128]{1,0:T(8,128)S(1)} %get-tuple-element.53), channel_id=1, source_target_pairs={{0,3},{1,2},{2,1},{3,0},{4,7},{5,6},{6,5},{7,4},{8,11},{9,10},{10,... | collective-permute-start | bytes 98312 | tf_op jit(solution)/shard_map/ppermute | solution.py:58
  30.2 4.3 %collective-permute-start.8 = (f32[64,128]{1,0:T(8,128)S(1)}, f32[64,128]{1,0:T(8,128)S(1)}, u32[]{:S(2)}, u32[]{:S(2)}) collective-permute-start(f32[64,128]{1,0:T(8,128)S(1)} %get-tuple-element.53), channel_id=1, source_target_pairs={{0,1},{1,0},{2,3},{3,2},{4,5},{5,4},{6,7},{7,6},{8,9},{9,8},{10,11... | collective-permute-start | bytes 98312 | tf_op jit(solution)/shard_map/ppermute | solution.py:58
  41.5 13.9 %collective-permute-start.12 = (f32[128,128]{1,0:T(8,128)}, f32[128,128]{1,0:T(8,128)S(1)}, u32[]{:S(2)}, u32[]{:S(2)}) collective-permute-start(f32[128,128]{1,0:T(8,128)} %get-tuple-element.60), channel_id=1, source_target_pairs={{0,4},{4,0},{1,5},{5,1},{2,6},{6,2},{3,7},{7,3},{8,12},{12,8},{9,1... | collective-permute-start | bytes 196616 | tf_op jit(solution)/shard_map/ppermute | solution.py:58
  43.0 12.4 %all-to-all-start = ((f32[32,1,128]{2,1,0:T(1,128)}), f32[32,1,128]{2,1,0:T(1,128)S(1)}, u32[]{:S(2)}, u32[]{:S(2)}) async-start(f32[32,1,128]{2,1,0:T(1,128)} %bitcast.6), calls=%async_computation | async-start | bytes 32768 | tf_op jit(solution)/shard_map/all_to_all | solution.py:487
  46.1 5.3 %collective-permute-start.10 = (f32[32,128]{1,0:T(8,128)}, f32[32,128]{1,0:T(8,128)S(1)}, u32[]{:S(2)}, u32[]{:S(2)}) collective-permute-start(f32[32,128]{1,0:T(8,128)} %get-tuple-element.58), channel_id=1, source_target_pairs={{0,8},{8,0},{16,24},{24,16},{1,9},{9,1},{17,25},{25,17},{2,10},{10... | collective-permute-start | bytes 49160 | tf_op jit(solution)/shard_map/ppermute | solution.py:58
  46.4 5.0 %collective-permute-start.11 = (f32[32,128]{1,0:T(8,128)}, f32[32,128]{1,0:T(8,128)S(1)}, u32[]{:S(2)}, u32[]{:S(2)}) collective-permute-start(f32[32,128]{1,0:T(8,128)} %get-tuple-element.59), channel_id=1, source_target_pairs={{0,24},{8,16},{16,8},{24,0},{1,25},{9,17},{17,9},{25,1},{2,26},{10... | collective-permute-start | bytes 49160 | tf_op jit(solution)/shard_map/ppermute | solution.py:58
  48.1 5.7 %collective-permute-start.14 = (f32[32,128]{1,0:T(8,128)}, f32[32,128]{1,0:T(8,128)S(1)}, u32[]{:S(2)}, u32[]{:S(2)}) collective-permute-start(f32[32,128]{1,0:T(8,128)} %get-tuple-element.61), channel_id=1, source_target_pairs={{0,3},{1,2},{2,1},{3,0},{4,7},{5,6},{6,5},{7,4},{8,11},{9,10},{10,... | collective-permute-start | bytes 49160 | tf_op jit(solution)/shard_map/ppermute | solution.py:58
  51.4 3.9 %collective-permute-start.13 = (f32[32,128]{1,0:T(8,128)}, f32[32,128]{1,0:T(8,128)S(1)}, u32[]{:S(2)}, u32[]{:S(2)}) collective-permute-start(f32[32,128]{1,0:T(8,128)} %get-tuple-element.61), channel_id=1, source_target_pairs={{0,1},{1,0},{2,3},{3,2},{4,5},{5,4},{6,7},{7,6},{8,9},{9,8},{10,11... | collective-permute-start | bytes 49160 | tf_op jit(solution)/shard_map/ppermute | solution.py:58
where the time goes:
time: 60.3 us; the launch traced here: 60 us
  Pallas kernels  21.9 us (36%)
  starting transfers between devices  21.2 us (35%)
  waiting for transfers between devices  12 us (20%)
  local copies, waits for them, and re-layouts  4.27 us (7%)
  between operations  0.69 us (1%)
    pallas_call x4, Pallas kernels, call(): pl.pallas_call(kernel, out_shape=[jax.ShapeDtypeStruct(s, d) for s, d in...  21.9 us
    ppermute x15, starting transfers between devices, exchange(): lax.ppermute(p, axis, swap_pairs(count, kind))  18.1 us
    ppermute x15, waiting for transfers between devices, exchange(): lax.ppermute(p, axis, swap_pairs(count, kind))  12 us
    unnamed x10, local copies, waits for them, and re-layouts  4.27 us
    all_to_all x1, starting transfers between devices, per_device(): sums = lax.all_to_all(sums, AXES, 0, 0, tiled=True)  3.13 us
  transfers between devices with their start and end apart: 16, of which 7 were waited for; matrix products, arithmetic and copies ran while one was open for 0% of the time, Pallas kernels for 0%

commit v1 on v0

--- a/solution.py
+++ b/solution.py
@@ -233,7 +233,7 @@
     planes = nx // chunks
     for j in range(chunks):
         copies[2 + j].wait()
-        accs = lax.fori_loop(j * planes, (j + 1) * planes, plane, accs, unroll=2)
+        accs = lax.fori_loop(j * planes, (j + 1) * planes, plane, accs, unroll=8)
     put_faces(dims, counts, (t_ref, s_ref, k_ref), outs, accs)
 
 
@@ -290,7 +290,7 @@
     prev = tuple(halo.x(f, 0) for f in range(3))
     cur = tuple(r[pl.ds(0, ny), :] for r in fields)
     accs = tuple(jnp.zeros((ny, LANES), F32) for _ in range(4))
-    _, _, accs = lax.fori_loop(0, nx, plane, (prev, cur, accs), unroll=2)
+    _, _, accs = lax.fori_loop(0, nx, plane, (prev, cur, accs), unroll=4)
     put_faces(dims, counts, (t1, s1, k1, h0), outs, accs)
 
 
@@ -361,7 +361,7 @@
     prev = tuple(halo.x(f, 0) for f in range(4))
     cur = tuple(r[pl.ds(0, ny), :] for r in fields)
     _, _, accs, (misfit, part) = lax.fori_loop(
-        0, nx, plane, (prev, cur, (zero, zero), (zero, zero)), unroll=2
+        0, nx, plane, (prev, cur, (zero, zero), (zero, zero)), unroll=4
     )
     put_faces(dims, counts, (mt_ref, ms_ref), outs, accs)
     lane_row = lax.broadcasted_iota(jnp.int32, (1, LANES), 1)
@@ -414,7 +414,7 @@
         return cur, nxt
 
     prev = edge(lambda u, f: u.x(f, 0))
-    lax.fori_loop(0, nx, plane, (prev, load(pl.ds(0, ny))), unroll=2)
+    lax.fori_loop(0, nx, plane, (prev, load(pl.ds(0, ny))), unroll=8)
     sums = sums_ref[...]
     which = lax.broadcasted_iota(jnp.int32, sums.shape, 1)
     misfit_ref[0, 0] = jnp.sum(jnp.where(which == 0, sums, 0.0)) / cells
@@ -425,7 +425,7 @@
 SM = pl.BlockSpec(memory_space=pltpu.SMEM)
 
 
-def call(kernel, out, args, scratch=(), in_specs=None, out_specs=None, name=None):
+def call(kernel, out, args, scratch=(), in_specs=None, out_specs=None, name=None, vmem=32):
     return pl.pallas_call(
         kernel,
         out_shape=[jax.ShapeDtypeStruct(s, d) for s, d in out],
@@ -433,7 +433,7 @@
         out_specs=out_specs or [VM] * len(out),
         scratch_shapes=list(scratch),
         name=name,
-        compiler_params=pltpu.CompilerParams(vmem_limit_bytes=32 << 20),
+        compiler_params=pltpu.CompilerParams(vmem_limit_bytes=vmem << 20),
     )(*args)
 
 
@@ -458,6 +458,7 @@
         [pltpu.VMEM((bins, cells, nz), F32), pltpu.SemaphoreType.DMA((chunks + 2,))],
         in_specs=[hbm] * 3,
         name="prepare",
+        vmem=51,
     )
     k, l, m, t, s = res[:5]
     got = send_faces(res[5:], counts)

time: 60.3 us -> 50 us (0.83)
  Pallas kernels: 21.9 us -> 15.9 us
  local copies, waits for them, and re-layouts: 4.27 us -> 0.01 us
    pallas_call x4, Pallas kernels: 21.9 us -> 15.9 us  [call(): pl.pallas_call(kernel, out_shape=[jax.ShapeDtypeStruct(s, d) for s, d in...]
    unnamed x10 -> x4, local copies, waits for them, and re-layouts: 4.27 us -> 0.01 us
where the time goes in v1:
time: 50 us; the launch traced here: 49.8 us
  starting transfers between devices  21.2 us (42%)
  Pallas kernels  15.9 us (32%)
  waiting for transfers between devices  12 us (24%)
  between operations  0.69 us (1%)
    ppermute x15, starting transfers between devices, exchange(): lax.ppermute(p, axis, swap_pairs(count, kind))  18.1 us
    pallas_call x4, Pallas kernels, call(): pl.pallas_call(kernel, out_shape=[jax.ShapeDtypeStruct(s, d) for s, d in...  15.9 us
    ppermute x15, waiting for transfers between devices, exchange(): lax.ppermute(p, axis, swap_pairs(count, kind))  12 us
    all_to_all x1, starting transfers between devices, per_device(): sums = lax.all_to_all(sums, AXES, 0, 0, tiled=True)  3.13 us
  transfers between devices with their start and end apart: 16, of which 7 were waited for; matrix products, arithmetic and copies ran while one was open for 0% of the time, Pallas kernels for 0%

profile of v1, /device:TPU:0, one launch (start us, length us, event | category | flops | bytes accessed | tf_op | source)
XLA Modules:
  0.0 49.8 jit_solution(14902861031152245891)
XLA Ops:
  0.7 3.0 %prepare.1 = (f32[1024,128]{1,0:T(8,128)S(1)}, f32[1024,128]{1,0:T(8,128)S(1)}, f32[1024,128]{1,0:T(8,128)S(1)}, f32[1024,128]{1,0:T(8,128)S(1)}, f32[1024,128]{...) custom-call(f32[8,1024,128]{2,1,0:T(8,128)} %bitcast.16, ...), custom_call_target="tpu_custom_call" | custom-call | tf_op jit(solution)/shard_map/prepare/pallas_call | solution.py:429
  3.7 3.0 %collective-permute-start.2 = (f32[192,128]{1,0:T(8,128)S(1)}, f32[192,128]{1,0:T(8,128)S(1)}, u32[]{:S(2)}, u32[]{:S(2)}) collective-permute-start(f32[192,128]{1,0:T(8,128)S(1)} %get-tuple-element.41), channel_id=1, source_target_pairs={{0,4},{4,0},{1,5},{5,1},{2,6},{6,2},{3,7},{7,3},{8,12},{12,8},{9,1... | collective-permute-start | bytes 294920 | tf_op jit(solution)/shard_map/ppermute | solution.py:58
  6.7 1.6 %collective-permute-start.1 = (f32[48,128]{1,0:T(8,128)S(1)}, f32[48,128]{1,0:T(8,128)S(1)}, u32[]{:S(2)}, u32[]{:S(2)}) collective-permute-start(f32[48,128]{1,0:T(8,128)S(1)} %get-tuple-element.40), channel_id=1, source_target_pairs={{0,24},{8,16},{16,8},{24,0},{1,25},{9,17},{17,9},{25,1},{2,26},{10... | collective-permute-start | bytes 73736 | tf_op jit(solution)/shard_map/ppermute | solution.py:58
  8.3 3.6 %collective-permute-start.4 = (f32[48,128]{1,0:T(8,128)S(1)}, f32[48,128]{1,0:T(8,128)S(1)}, u32[]{:S(2)}, u32[]{:S(2)}) collective-permute-start(f32[48,128]{1,0:T(8,128)S(1)} %get-tuple-element.42), channel_id=1, source_target_pairs={{0,3},{1,2},{2,1},{3,0},{4,7},{5,6},{6,5},{7,4},{8,11},{9,10},{10,... | collective-permute-start | bytes 73736 | tf_op jit(solution)/shard_map/ppermute | solution.py:58
  11.9 0.0 collective-permute-start.3
  11.9 0.0 collective-permute-done.refs_6_
  11.9 2.0 %collective-permute-done.4.refs_10_ = f32[48,128]{1,0:T(8,128)S(1)} collective-permute-done((f32[48,128]{1,0:T(8,128)S(1)}, f32[48,128]{1,0:T(8,128)S(1)}, u32[]{:S(2)}, u32[]{:S(2)}) %collective-permute-start.4) | collective-permute-done | bytes 24608 | tf_op jit(solution)/shard_map/ppermute | solution.py:58
  13.9 1.8 %collective-permute-done.3.refs_9_ = f32[48,128]{1,0:T(8,128)S(1)} collective-permute-done((f32[48,128]{1,0:T(8,128)S(1)}, f32[48,128]{1,0:T(8,128)S(1)}, u32[]{:S(2)}, u32[]{:S(2)}) %collective-permute-start.3) | collective-permute-done | bytes 24608 | tf_op jit(solution)/shard_map/ppermute | solution.py:58
  15.7 5.0 %first_step.1 = (f32[1024,128]{1,0:T(8,128)S(1)}, f32[1024,128]{1,0:T(8,128)S(1)}, f32[1024,128]{1,0:T(8,128)S(1)}, f32[1024,128]{1,0:T(8,128)S(1)}, f32[1024,12...) custom-call(f32[1024,128]{1,0:T(8,128)S(1)} %get-tuple-element.34.re, ...), custom_call_target="tpu_custom_call" | custom-call | tf_op jit(solution)/shard_map/first_step/pallas_call | solution.py:429
  20.8 0.6 %collective-permute-start.7 = (f32[256,128]{1,0:T(8,128)S(1)}, f32[256,128]{1,0:T(8,128)S(1)}, u32[]{:S(2)}, u32[]{:S(2)}) collective-permute-start(f32[256,128]{1,0:T(8,128)S(1)} %get-tuple-element.52), channel_id=1, source_target_pairs={{0,4},{4,0},{1,5},{5,1},{2,6},{6,2},{3,7},{7,3},{8,12},{12,8},{9,1... | collective-permute-start | bytes 393224 | tf_op jit(solution)/shard_map/ppermute | solution.py:58
  21.4 0.6 %collective-permute-start.6 = (f32[64,128]{1,0:T(8,128)S(1)}, f32[64,128]{1,0:T(8,128)S(1)}, u32[]{:S(2)}, u32[]{:S(2)}) collective-permute-start(f32[64,128]{1,0:T(8,128)S(1)} %get-tuple-element.51), channel_id=1, source_target_pairs={{0,24},{8,16},{16,8},{24,0},{1,25},{9,17},{17,9},{25,1},{2,26},{10... | collective-permute-start | bytes 98312 | tf_op jit(solution)/shard_map/ppermute | solution.py:58
  22.0 1.8 %collective-permute-start.9 = (f32[64,128]{1,0:T(8,128)S(1)}, f32[64,128]{1,0:T(8,128)S(1)}, u32[]{:S(2)}, u32[]{:S(2)}) collective-permute-start(f32[64,128]{1,0:T(8,128)S(1)} %get-tuple-element.53), channel_id=1, source_target_pairs={{0,3},{1,2},{2,1},{3,0},{4,7},{5,6},{6,5},{7,4},{8,11},{9,10},{10,... | collective-permute-start | bytes 98312 | tf_op jit(solution)/shard_map/ppermute | solution.py:58
  23.8 0.9 %collective-permute-done.6.refs_10_.refs_8_ = f32[64,128]{1,0:T(8,128)S(1)} collective-permute-done((f32[64,128]{1,0:T(8,128)S(1)}, f32[64,128]{1,0:T(8,128)S(1)}, u32[]{:S(2)}, u32[]{:S(2)}) %collective-permute-start.6) | collective-permute-done | bytes 32800 | tf_op jit(solution)/shard_map/ppermute | solution.py:58
  24.7 3.0 %collective-permute-done.9.refs_13_.refs_11_ = f32[64,128]{1,0:T(8,128)S(1)} collective-permute-done((f32[64,128]{1,0:T(8,128)S(1)}, f32[64,128]{1,0:T(8,128)S(1)}, u32[]{:S(2)}, u32[]{:S(2)}) %collective-permute-start.9) | collective-permute-done | bytes 32800 | tf_op jit(solution)/shard_map/ppermute | solution.py:58
  27.7 0.3 collective-permute-done.8.refs_12_.refs_10_
  28.0 5.0 %second_step.1 = (f32[1024,128]{1,0:T(8,128)S(1)}, f32[1024,128]{1,0:T(8,128)S(1)}, f32[1024,128]{1,0:T(8,128)S(1)}, f32[32,128]{1,0:T(8,128)}, f32[32,128]{1,0:...) custom-call(f32[1024,128]{1,0:T(8,128)S(1)} %get-tuple-element.43.refs_0_, ...), custom_call_target="tpu_custom_call" | custom-call | tf_op jit(solution)/shard_map/second_step/pallas_call | solution.py:429
  33.0 1.5 %collective-permute-start.12 = (f32[128,128]{1,0:T(8,128)}, f32[128,128]{1,0:T(8,128)S(1)}, u32[]{:S(2)}, u32[]{:S(2)}) collective-permute-start(f32[128,128]{1,0:T(8,128)} %get-tuple-element.60), channel_id=1, source_target_pairs={{0,4},{4,0},{1,5},{5,1},{2,6},{6,2},{3,7},{7,3},{8,12},{12,8},{9,1... | collective-permute-start | bytes 196616 | tf_op jit(solution)/shard_map/ppermute | solution.py:58
  34.5 3.1 %all-to-all-start = ((f32[32,1,128]{2,1,0:T(1,128)}), f32[32,1,128]{2,1,0:T(1,128)S(1)}, u32[]{:S(2)}, u32[]{:S(2)}) async-start(f32[32,1,128]{2,1,0:T(1,128)} %bitcast.6), calls=%async_computation | async-start | bytes 32768 | tf_op jit(solution)/shard_map/all_to_all | solution.py:488
  37.7 0.3 collective-permute-start.10
  38.0 1.6 %collective-permute-start.11 = (f32[32,128]{1,0:T(8,128)}, f32[32,128]{1,0:T(8,128)S(1)}, u32[]{:S(2)}, u32[]{:S(2)}) collective-permute-start(f32[32,128]{1,0:T(8,128)} %get-tuple-element.59), channel_id=1, source_target_pairs={{0,24},{8,16},{16,8},{24,0},{1,25},{9,17},{17,9},{25,1},{2,26},{10... | collective-permute-start | bytes 49160 | tf_op jit(solution)/shard_map/ppermute | solution.py:58
  39.6 3.3 %collective-permute-start.14 = (f32[32,128]{1,0:T(8,128)}, f32[32,128]{1,0:T(8,128)S(1)}, u32[]{:S(2)}, u32[]{:S(2)}) collective-permute-start(f32[32,128]{1,0:T(8,128)} %get-tuple-element.61), channel_id=1, source_target_pairs={{0,3},{1,2},{2,1},{3,0},{4,7},{5,6},{6,5},{7,4},{8,11},{9,10},{10,... | collective-permute-start | bytes 49160 | tf_op jit(solution)/shard_map/ppermute | solution.py:58
  43.0 2.4 %collective-permute-done.14.refs_16_ = f32[32,128]{1,0:T(8,128)S(1)} collective-permute-done((f32[32,128]{1,0:T(8,128)}, f32[32,128]{1,0:T(8,128)S(1)}, u32[]{:S(2)}, u32[]{:S(2)}) %collective-permute-start.14) | collective-permute-done | bytes 16416 | tf_op jit(solution)/shard_map/ppermute | solution.py:58
  45.4 1.5 %collective-permute-done.13.refs_15_ = f32[32,128]{1,0:T(8,128)S(1)} collective-permute-done((f32[32,128]{1,0:T(8,128)}, f32[32,128]{1,0:T(8,128)S(1)}, u32[]{:S(2)}, u32[]{:S(2)}) %collective-permute-start.13) | collective-permute-done | bytes 16416 | tf_op jit(solution)/shard_map/ppermute | solution.py:58
  46.9 2.9 %finish.1 = (f32[1024,128]{1,0:T(8,128)}, f32[1,1]{1,0:T(1,128)}, f32[1,1]{1,0:T(1,128)}) custom-call(f32[1024,128]{1,0:T(8,128)S(1)} %get-tuple-element.43.refs_0_, f32[1024,128]{1,0:T(8,128)S(1)} %get-tuple-element.44.refs_2_.refs_1_, f32[1024,128]{1,0:T(8,128)S(1)} %get-tuple-element.54.refs_2_, f32[1024,128]{1,0:T(8,128)S(1)} %get-tuple-element.55.refs_3_, ...), custom_call_target="tpu_custom_call" | custom-call | tf_op jit(solution)/shard_map/finish/pallas_call | solution.py:429
  (16 shorter events, 0.0 us)
Async XLA Ops:
  0.6 15.1 %copy-start = (f32[64,16,128]{2,1,0:T(8,128)S(1)}, f32[64,16,128]{2,1,0:T(8,128)}, u32[]{:S(2)}) copy-start(f32[64,16,128]{2,1,0:T(8,128)} %param.8) | copy-start | bytes 1572868
  0.6 27.4 %copy-start.1 = (bf16[2,64,16,128]{3,2,1,0:T(8,128)(2,1)S(1)}, bf16[2,64,16,128]{3,2,1,0:T(8,128)(2,1)}, u32[]{:S(2)}) copy-start(bf16[2,64,16,128]{3,2,1,0:T(8,128)(2,1)} %param.9) | copy-start | bytes 1572868
  3.7 12.1 %collective-permute-start.2 = (f32[192,128]{1,0:T(8,128)S(1)}, f32[192,128]{1,0:T(8,128)S(1)}, u32[]{:S(2)}, u32[]{:S(2)}) collective-permute-start(f32[192,128]{1,0:T(8,128)S(1)} %get-tuple-element.41), channel_id=1, source_target_pairs={{0,4},{4,0},{1,5},{5,1},{2,6},{6,2},{3,7},{7,3},{8,12},{12,8},{9,1... | collective-permute-start | bytes 294920 | tf_op jit(solution)/shard_map/ppermute | solution.py:58
  6.7 5.2 %collective-permute-start = (f32[48,128]{1,0:T(8,128)S(1)}, f32[48,128]{1,0:T(8,128)S(1)}, u32[]{:S(2)}, u32[]{:S(2)}) collective-permute-start(f32[48,128]{1,0:T(8,128)S(1)} %get-tuple-element.39), channel_id=1, source_target_pairs={{0,8},{8,0},{16,24},{24,16},{1,9},{9,1},{17,25},{25,17},{2,10},{10... | collective-permute-start | bytes 73736 | tf_op jit(solution)/shard_map/ppermute | solution.py:58
  6.7 5.2 %collective-permute-start.1 = (f32[48,128]{1,0:T(8,128)S(1)}, f32[48,128]{1,0:T(8,128)S(1)}, u32[]{:S(2)}, u32[]{:S(2)}) collective-permute-start(f32[48,128]{1,0:T(8,128)S(1)} %get-tuple-element.40), channel_id=1, source_target_pairs={{0,24},{8,16},{16,8},{24,0},{1,25},{9,17},{17,9},{25,1},{2,26},{10... | collective-permute-start | bytes 73736 | tf_op jit(solution)/shard_map/ppermute | solution.py:58
  8.3 5.6 %collective-permute-start.4 = (f32[48,128]{1,0:T(8,128)S(1)}, f32[48,128]{1,0:T(8,128)S(1)}, u32[]{:S(2)}, u32[]{:S(2)}) collective-permute-start(f32[48,128]{1,0:T(8,128)S(1)} %get-tuple-element.42), channel_id=1, source_target_pairs={{0,3},{1,2},{2,1},{3,0},{4,7},{5,6},{6,5},{7,4},{8,11},{9,10},{10,... | collective-permute-start | bytes 73736 | tf_op jit(solution)/shard_map/ppermute | solution.py:58
  11.9 3.8 %collective-permute-start.3 = (f32[48,128]{1,0:T(8,128)S(1)}, f32[48,128]{1,0:T(8,128)S(1)}, u32[]{:S(2)}, u32[]{:S(2)}) collective-permute-start(f32[48,128]{1,0:T(8,128)S(1)} %get-tuple-element.42), channel_id=1, source_target_pairs={{0,1},{1,0},{2,3},{3,2},{4,5},{5,4},{6,7},{7,6},{8,9},{9,8},{10,11... | collective-permute-start | bytes 73736 | tf_op jit(solution)/shard_map/ppermute | solution.py:58
  20.8 7.3 %collective-permute-start.7 = (f32[256,128]{1,0:T(8,128)S(1)}, f32[256,128]{1,0:T(8,128)S(1)}, u32[]{:S(2)}, u32[]{:S(2)}) collective-permute-start(f32[256,128]{1,0:T(8,128)S(1)} %get-tuple-element.52), channel_id=1, source_target_pairs={{0,4},{4,0},{1,5},{5,1},{2,6},{6,2},{3,7},{7,3},{8,12},{12,8},{9,1... | collective-permute-start | bytes 393224 | tf_op jit(solution)/shard_map/ppermute | solution.py:58
  21.4 2.4 %collective-permute-start.5 = (f32[64,128]{1,0:T(8,128)S(1)}, f32[64,128]{1,0:T(8,128)S(1)}, u32[]{:S(2)}, u32[]{:S(2)}) collective-permute-start(f32[64,128]{1,0:T(8,128)S(1)} %get-tuple-element.50), channel_id=1, source_target_pairs={{0,8},{8,0},{16,24},{24,16},{1,9},{9,1},{17,25},{25,17},{2,10},{10... | collective-permute-start | bytes 98312 | tf_op jit(solution)/shard_map/ppermute | solution.py:58
  21.4 3.3 %collective-permute-start.6 = (f32[64,128]{1,0:T(8,128)S(1)}, f32[64,128]{1,0:T(8,128)S(1)}, u32[]{:S(2)}, u32[]{:S(2)}) collective-permute-start(f32[64,128]{1,0:T(8,128)S(1)} %get-tuple-element.51), channel_id=1, source_target_pairs={{0,24},{8,16},{16,8},{24,0},{1,25},{9,17},{17,9},{25,1},{2,26},{10... | collective-permute-start | bytes 98312 | tf_op jit(solution)/shard_map/ppermute | solution.py:58
  22.0 5.7 %collective-permute-start.9 = (f32[64,128]{1,0:T(8,128)S(1)}, f32[64,128]{1,0:T(8,128)S(1)}, u32[]{:S(2)}, u32[]{:S(2)}) collective-permute-start(f32[64,128]{1,0:T(8,128)S(1)} %get-tuple-element.53), channel_id=1, source_target_pairs={{0,3},{1,2},{2,1},{3,0},{4,7},{5,6},{6,5},{7,4},{8,11},{9,10},{10,... | collective-permute-start | bytes 98312 | tf_op jit(solution)/shard_map/ppermute | solution.py:58
  23.8 4.3 %collective-permute-start.8 = (f32[64,128]{1,0:T(8,128)S(1)}, f32[64,128]{1,0:T(8,128)S(1)}, u32[]{:S(2)}, u32[]{:S(2)}) collective-permute-start(f32[64,128]{1,0:T(8,128)S(1)} %get-tuple-element.53), channel_id=1, source_target_pairs={{0,1},{1,0},{2,3},{3,2},{4,5},{5,4},{6,7},{7,6},{8,9},{9,8},{10,11... | collective-permute-start | bytes 98312 | tf_op jit(solution)/shard_map/ppermute | solution.py:58
  33.0 13.9 %collective-permute-start.12 = (f32[128,128]{1,0:T(8,128)}, f32[128,128]{1,0:T(8,128)S(1)}, u32[]{:S(2)}, u32[]{:S(2)}) collective-permute-start(f32[128,128]{1,0:T(8,128)} %get-tuple-element.60), channel_id=1, source_target_pairs={{0,4},{4,0},{1,5},{5,1},{2,6},{6,2},{3,7},{7,3},{8,12},{12,8},{9,1... | collective-permute-start | bytes 196616 | tf_op jit(solution)/shard_map/ppermute | solution.py:58
  34.5 12.4 %all-to-all-start = ((f32[32,1,128]{2,1,0:T(1,128)}), f32[32,1,128]{2,1,0:T(1,128)S(1)}, u32[]{:S(2)}, u32[]{:S(2)}) async-start(f32[32,1,128]{2,1,0:T(1,128)} %bitcast.6), calls=%async_computation | async-start | bytes 32768 | tf_op jit(solution)/shard_map/all_to_all | solution.py:488
  37.7 5.3 %collective-permute-start.10 = (f32[32,128]{1,0:T(8,128)}, f32[32,128]{1,0:T(8,128)S(1)}, u32[]{:S(2)}, u32[]{:S(2)}) collective-permute-start(f32[32,128]{1,0:T(8,128)} %get-tuple-element.58), channel_id=1, source_target_pairs={{0,8},{8,0},{16,24},{24,16},{1,9},{9,1},{17,25},{25,17},{2,10},{10... | collective-permute-start | bytes 49160 | tf_op jit(solution)/shard_map/ppermute | solution.py:58
  38.0 5.0 %collective-permute-start.11 = (f32[32,128]{1,0:T(8,128)}, f32[32,128]{1,0:T(8,128)S(1)}, u32[]{:S(2)}, u32[]{:S(2)}) collective-permute-start(f32[32,128]{1,0:T(8,128)} %get-tuple-element.59), channel_id=1, source_target_pairs={{0,24},{8,16},{16,8},{24,0},{1,25},{9,17},{17,9},{25,1},{2,26},{10... | collective-permute-start | bytes 49160 | tf_op jit(solution)/shard_map/ppermute | solution.py:58
  39.6 5.7 %collective-permute-start.14 = (f32[32,128]{1,0:T(8,128)}, f32[32,128]{1,0:T(8,128)S(1)}, u32[]{:S(2)}, u32[]{:S(2)}) collective-permute-start(f32[32,128]{1,0:T(8,128)} %get-tuple-element.61), channel_id=1, source_target_pairs={{0,3},{1,2},{2,1},{3,0},{4,7},{5,6},{6,5},{7,4},{8,11},{9,10},{10,... | collective-permute-start | bytes 49160 | tf_op jit(solution)/shard_map/ppermute | solution.py:58
  43.0 3.9 %collective-permute-start.13 = (f32[32,128]{1,0:T(8,128)}, f32[32,128]{1,0:T(8,128)S(1)}, u32[]{:S(2)}, u32[]{:S(2)}) collective-permute-start(f32[32,128]{1,0:T(8,128)} %get-tuple-element.61), channel_id=1, source_target_pairs={{0,1},{1,0},{2,3},{3,2},{4,5},{5,4},{6,7},{7,6},{8,9},{9,8},{10,11... | collective-permute-start | bytes 49160 | tf_op jit(solution)/shard_map/ppermute | solution.py:58

commit v2 on v1

v2 whole, which is shorter than its diff:
```python
import functools

import jax
import jax.numpy as jnp
import numpy as np
from jax import lax
from jax.experimental import pallas as pl
from jax.experimental.pallas import tpu as pltpu
from jax.sharding import PartitionSpec as P

F32 = jnp.float32
AXES = ("gx", "gy", "gz")

SOLIDIFY_POINT = 0.5
LOWERING_COEF = 0.5
GROW = 0.3
NUCLEATE = 0.2
VOLUME = 0.005
WARMTH_ADVANCE = 0.08
STEP_SOLUTE = 0.1
HIDDEN_WARMTH = 0.5
REJECT = 0.3
LANES = 128


def volumes(bin_count):
    rank = np.arange(bin_count, dtype=np.float64) + 1.0
    return VOLUME * rank * rank


def functional_weights(bin_count):
    vol = volumes(bin_count)
    step = vol[1:] - vol[:-1]
    k = (1.0, vol)
    l = (NUCLEATE * vol[0], np.concatenate([GROW * step, [0.0]]))
    m_const = GROW * step[0] * NUCLEATE
    m = np.zeros(bin_count)
    for b in range(bin_count - 1):
        m[b] -= GROW * step[b] * GROW
        if b >= 1:
            m[b - 1] += GROW * step[b] * GROW
    return k, l, (m_const, m)


def swap_pairs(count, kind):
    if kind == 0:
        return [(i, i ^ 1) for i in range(count)]
    return [(i, (i + 1) % count if i % 2 else (i - 1) % count) for i in range(count)]


def swaps(count):
    return {1: 0, 2: 1}.get(count, 2)


def exchange(payloads, axis):
    count = lax.axis_size(axis)
    assert count == 1 or count % 2 == 0
    return [lax.ppermute(p, axis, swap_pairs(count, kind)) for kind, p in enumerate(payloads)]


class Side:
    def __init__(self, axis, count):
        self.count = count
        self.index = lax.axis_index(axis)
        self.odd = lax.rem(self.index, 2) == 1

    def outgoing(self, first, last):
        kinds = [jnp.where(self.odd, first, last), jnp.where(self.odd, last, first)]
        return kinds[: swaps(self.count)]

    def incoming(self, got):
        if self.count == 1:
            return None
        if self.count == 2:
            zero = jnp.zeros_like(got[0])
            return jnp.where(self.odd, got[0], zero), jnp.where(self.odd, zero, got[0])
        a, b = got
        zero = jnp.zeros_like(a)
        before = jnp.where(self.index > 0, jnp.where(self.odd, a, b), zero)
        after = jnp.where(self.index < self.count - 1, jnp.where(self.odd, b, a), zero)
        return before, after


def grid_iota(ny):
    row = lax.broadcasted_iota(jnp.int32, (ny, LANES), 0)
    lane = lax.broadcasted_iota(jnp.int32, (ny, LANES), 1)
    return row, lane


def pack_z(acc, value, x, lane):
    return jnp.where(lane // 2 == x, pltpu.roll(value, lax.rem(2 * x + 1, LANES), 1), acc)


class Faces:
    def __init__(self, dims, counts, own, got):
        self.nx, self.ny = dims
        self.sides = [Side(a, n) for a, n in zip(AXES, counts)]
        self.mine = own
        a, b = swaps(counts[0]), swaps(counts[1])
        self.got = (got[:a], got[a : a + b], got[a + b :])

    def _part(self, axis, f):
        rows = self.nx if axis == 1 else self.ny
        return pl.ds(f * rows, rows)

    def near(self, axis, f):
        part = [r[self._part(axis, f), :] for r in self.got[axis]]
        before, after = self.sides[axis].incoming(part)
        if axis < 2:
            return before, after
        lane = lax.broadcasted_iota(jnp.int32, before.shape, 1)
        return jnp.where(lax.rem(lane, 2) == 0, before, after)

    def own(self, axis, f):
        if axis < 2:
            return [self.mine[axis][side, self._part(axis, f), :] for side in (0, 1)]
        return turn_z(self.mine[2][self._part(2, f), :])


def turn_z(pack):
    lane = lax.broadcasted_iota(jnp.int32, pack.shape, 1)
    even = lax.rem(lane, 2) == 0
    return jnp.where(even, pltpu.roll(pack, LANES - 1, 1), pltpu.roll(pack, 1, 1))


class Own:
    def __init__(self, dims, counts, refs):
        self.nx, self.ny = dims
        self.counts = counts
        self.x, self.y, self.z = refs[:3]
        a = swaps(counts[0])
        self.out = (refs[3 : 3 + a], refs[3 + a :])

    def rows(self, f, x, value):
        self.y[0, pl.ds(f * self.nx + x, 1), :] = value[:1, :]
        self.y[1, pl.ds(f * self.nx + x, 1), :] = value[self.ny - 1 :, :]

    def finish(self, fields, packs):
        nx, ny = self.nx, self.ny
        for f, (ref, pack) in enumerate(zip(fields, packs)):
            part = pl.ds(f * ny, ny)
            self.x[0, part, :] = ref[pl.ds(0, ny), :]
            self.x[1, part, :] = ref[pl.ds((nx - 1) * ny, ny), :]
            self.z[part, :] = pack
        for axis, own in enumerate((self.x, self.y)):
            side = Side(AXES[axis], self.counts[axis])
            for o, v in zip(self.out[axis], side.outgoing(own[0], own[1])):
                o[...] = v


def own_shapes(dims, counts, fields):
    nx, ny = dims
    x, y = (fields * ny, LANES), (fields * nx, LANES)
    shapes = [(2, *x), (2, *y), x] + [x] * swaps(counts[0]) + [y] * swaps(counts[1])
    return [(v, F32) for v in shapes]


def send_faces(own, counts):
    a = swaps(counts[0])
    payloads = (own[3 : 3 + a], own[3 + a :], [own[2]] * swaps(counts[2]))
    got = []
    for payload, axis in zip(payloads, AXES):
        got += exchange(payload, axis)
    return got


def at_plane(x, nx, pair):
    return jnp.where(x == 0, pair[0], jnp.where(x == nx - 1, pair[1], 0.0))


def at_rows(x, ref, f, nx, row, ny):
    part = pl.ds(f * nx + x, 1)
    return jnp.where(row == 0, ref[0, part, :], jnp.where(row == ny - 1, ref[1, part, :], 0.0))


def ready_z(value):
    lane = lax.broadcasted_iota(jnp.int32, value.shape, 1)
    return jnp.where(lax.rem(lane, 2) == 0, value, pltpu.roll(value, LANES - 2, 1))


def unpack_z(value, x):
    return pltpu.roll(value, lax.rem(LANES - 2 * x, LANES), 1)


def half_flux(k, t, kn, tn):
    return 0.5 * (k + kn) * (tn - t)


def divergence(flux_up, axis, index):
    size = flux_up.shape[axis]
    flux_up = jnp.where(index == size - 1, 0.0, flux_up)
    return flux_up - pltpu.roll(flux_up, 1, axis)


def ahead(value, axis):
    return pltpu.roll(value, value.shape[axis] - 1, axis)


def neighbour_sum(value, axis, index):
    size = value.shape[axis]
    up = jnp.where(index == size - 1, 0.0, ahead(value, axis))
    return up + jnp.where(index == 0, 0.0, pltpu.roll(value, 1, axis))


def log1p_of(e, u, inv):
    return jnp.log(u) + (e - (u - 1.0)) * inv


def softplus_parts(v):
    e = jnp.exp(-jnp.abs(v))
    u = 1.0 + e
    inv = 1.0 / u
    soft = jnp.maximum(v, 0.0) + log1p_of(e, u, inv)
    return soft, jnp.where(v >= 0, inv, e * inv)


def prepare_kernel(dims, counts, bins, chunks, *refs):
    nx, ny = dims
    c_hbm, t_hbm, s_hbm = refs[:3]
    k_ref, l_ref, m_ref, t_ref, s_ref = refs[3:8]
    own = Own(dims, counts, refs[8:-2])
    c_ref, sems = refs[-2:]
    rows = nx * ny // chunks
    copies = [
        pltpu.make_async_copy(t_hbm, t_ref, sems.at[chunks]),
        pltpu.make_async_copy(s_hbm, s_ref, sems.at[chunks + 1]),
    ]
    for j in range(chunks):
        part = pl.ds(j * rows, rows)
        copies.append(pltpu.make_async_copy(c_hbm.at[:, part, :], c_ref.at[:, part, :], sems.at[j]))
    for copy in copies:
        copy.start()
    copies[0].wait()
    copies[1].wait()
    _, lane = grid_iota(ny)
    weights = functional_weights(bins)

    def plane(x, accs):
        here = pl.ds(x * ny, ny)
        c = [c_ref[b, here, :] for b in range(bins)]
        values = []
        for const, per_bin in weights:
            total = None
            for b in range(bins):
                if per_bin[b] != 0.0:
                    term = float(per_bin[b]) * c[b]
                    total = term if total is None else total + term
            values.append(float(const) + total)
        k_ref[here, :], l_ref[here, :], m_ref[here, :] = values
        faces = (t_ref[here, :], s_ref[here, :], values[0])
        for f, v in enumerate(faces):
            own.rows(f, x, v)
        return tuple(pack_z(a, v, x, lane) for a, v in zip(accs, faces))

    accs = tuple(jnp.zeros((ny, LANES), F32) for _ in range(3))
    planes = nx // chunks
    for j in range(chunks):
        copies[2 + j].wait()
        accs = lax.fori_loop(j * planes, (j + 1) * planes, plane, accs, unroll=8)
    own.finish((t_ref, s_ref, k_ref), accs)


def first_inner_kernel(dims, unroll, *refs):
    nx, ny = dims
    t_ref, s_ref, k_ref, l_ref, m_ref, g_ref = refs[:6]
    t1, s1, h0, k1, l1, w0, v0, kpack = refs[6:]
    row, lane = grid_iota(ny)

    def plane(x, carry):
        t, s, k, s_prev, flux_prev, acc = carry
        here = pl.ds(x * ny, ny)
        then = pl.ds(jnp.minimum(x + 1, nx - 1) * ny, ny)
        tn, sn, kn = t_ref[then, :], s_ref[then, :], k_ref[then, :]
        flux = half_flux(k, t, kn, tn)
        heat = (flux - flux_prev) + divergence(
            half_flux(k, t, ahead(k, 0), ahead(t, 0)), 0, row
        )
        heat = heat + divergence(half_flux(k, t, ahead(k, 1), ahead(t, 1)), 1, lane)
        s_next = jnp.where(x == nx - 1, 0.0, sn)
        diff = (s_prev + s_next) + neighbour_sum(s, 0, row)
        diff = diff + neighbour_sum(s, 1, lane) - 6.0 * s
        g, l, m = g_ref[here, :], l_ref[here, :], m_ref[here, :]
        soft, _ = softplus_parts(SOLIDIFY_POINT - LOWERING_COEF * s - t)
        w, v = soft * l, soft * m
        frost = g * w
        t1[here, :] = t + WARMTH_ADVANCE * heat + HIDDEN_WARMTH * frost
        s1[here, :] = s + STEP_SOLUTE * diff + REJECT * frost
        h0[here, :] = heat
        new_k = k + frost
        k1[here, :] = new_k
        l1[here, :], w0[here, :], v0[here, :] = l + g * v, w, v
        return tn, sn, kn, s, flux, pack_z(acc, new_k, x, lane)

    top = pl.ds(0, ny)
    zero = jnp.zeros((ny, LANES), F32)
    carry = (t_ref[top, :], s_ref[top, :], k_ref[top, :], zero, zero, zero)
    kpack[...] = lax.fori_loop(0, nx, plane, carry, unroll=unroll)[-1]


def first_edge_kernel(dims, counts, unroll, *refs):
    nx, ny = dims
    ngot = sum(swaps(n) for n in counts)
    tp_ref, sp_ref, hp_ref, k1_ref, kpack_ref = refs[:5]
    faces = Faces(dims, counts, refs[5:8], refs[8 : 8 + ngot])
    t1, s1, h0 = refs[8 + ngot : 11 + ngot]
    own = Own(dims, counts, refs[11 + ngot : -1])
    rows_ref = refs[-1]
    row, lane = grid_iota(ny)
    edge = (lane == 0) | (lane == LANES - 1)

    def flux_in(axis):
        tn, sn, kn = [faces.near(axis, f) for f in range(3)]
        to, ko = faces.own(axis, 0), faces.own(axis, 2)
        if axis == 2:
            return half_flux(ko, to, kn, tn), sn
        return [half_flux(*v) for v in zip(ko, to, kn, tn)], sn

    heat_x, sugar_x = flux_in(0)
    heat_y, sugar_y = flux_in(1)
    for side in (0, 1):
        rows_ref[side, pl.ds(0, nx), :] = heat_y[side]
        rows_ref[side, pl.ds(nx, nx), :] = sugar_y[side]
    heat_z, sugar_z = flux_in(2)
    in_heat, in_sugar = ready_z(heat_z), ready_z(sugar_z)

    def plane(x, accs):
        here = pl.ds(x * ny, ny)
        heat = at_plane(x, nx, heat_x) + at_rows(x, rows_ref, 0, nx, row, ny)
        diff = at_plane(x, nx, sugar_x) + at_rows(x, rows_ref, 1, nx, row, ny)
        some_t = tp_ref[here, :] + WARMTH_ADVANCE * heat
        some_s = sp_ref[here, :] + STEP_SOLUTE * diff
        some_h = hp_ref[here, :] + heat
        heat = jnp.where(edge, unpack_z(in_heat, x), 0.0)
        diff = jnp.where(edge, unpack_z(in_sugar, x), 0.0)
        new_t = some_t + WARMTH_ADVANCE * heat
        new_s = some_s + STEP_SOLUTE * diff
        new_h = some_h + heat
        t1[here, :], s1[here, :], h0[here, :] = new_t, new_s, new_h
        for f, v in enumerate((new_t, new_s, k1_ref[here, :], new_h)):
            own.rows(f, x, v)
        return tuple(pack_z(a, v, x, lane) for a, v in zip(accs, (some_t, some_s, some_h)))

    accs = tuple(jnp.zeros((ny, LANES), F32) for _ in range(3))
    accs = lax.fori_loop(0, nx, plane, accs, unroll=unroll)
    heat_z, sugar_z = turn_z(heat_z), turn_z(sugar_z)
    packs = (
        accs[0] + WARMTH_ADVANCE * heat_z,
        accs[1] + STEP_SOLUTE * sugar_z,
        kpack_ref[...],
        accs[2] + heat_z,
    )
    own.finish((t1, s1, k1_ref, h0), packs)


def second_inner_kernel(dims, unroll, *refs):
    nx, ny = dims
    t_ref, s_ref, k_ref, h_ref, l_ref, g_ref, r_ref = refs[:7]
    mt_ref, ms_ref, inner_ref, soft_ref, slope_ref = refs[7:]
    row, lane = grid_iota(ny)

    def plane(x, carry):
        t, s, k, h, s_prev, flux_prev, other_prev = carry
        here = pl.ds(x * ny, ny)
        then = pl.ds(jnp.minimum(x + 1, nx - 1) * ny, ny)
        tn, sn, kn, hn = t_ref[then, :], s_ref[then, :], k_ref[then, :], h_ref[then, :]
        both = 0.5 * (k + kn)
        flux, other = both * (tn - t), both * (hn - h)
        heat, again = flux - flux_prev, other - other_prev
        for axis, index in ((0, row), (1, lane)):
            both = 0.5 * (k + ahead(k, axis))
            heat = heat + divergence(both * (ahead(t, axis) - t), axis, index)
            again = again + divergence(both * (ahead(h, axis) - h), axis, index)
        s_next = jnp.where(x == nx - 1, 0.0, sn)
        diff = (s_prev + s_next) + neighbour_sum(s, 0, row)
        diff = diff + neighbour_sum(s, 1, lane) - 6.0 * s
        g, l = g_ref[here, :], l_ref[here, :]
        soft, slope = softplus_parts(SOLIDIFY_POINT - LOWERING_COEF * s - t)
        frost = g * soft * l
        mt_ref[here, :] = (
            t + WARMTH_ADVANCE * heat + HIDDEN_WARMTH * frost - r_ref[0, here, :].astype(F32)
        )
        ms_ref[here, :] = s + STEP_SOLUTE * diff + REJECT * frost - r_ref[1, here, :].astype(F32)
        inner_ref[here, :] = heat + WARMTH_ADVANCE * again
        soft_ref[here, :], slope_ref[here, :] = soft, slope
        return tn, sn, kn, hn, s, flux, other

    top = pl.ds(0, ny)
    zero = jnp.zeros((ny, LANES), F32)
    start = [r[top, :] for r in (t_ref, s_ref, k_ref, h_ref)]
    lax.fori_loop(0, nx, plane, (*start, zero, zero, zero), unroll=unroll)


def second_edge_kernel(dims, counts, unroll, *refs):
    nx, ny = dims
    ngot = sum(swaps(n) for n in counts)
    h_ref, l_ref, w_ref, v_ref, g_ref = refs[:5]
    mtp_ref, msp_ref, inner_ref, soft_ref, slope_ref = refs[5:10]
    faces = Faces(dims, counts, refs[10:13], refs[13 : 13 + ngot])
    mt_ref, ms_ref, sense_ref, sums_ref = refs[13 + ngot : 17 + ngot]
    meet = refs[17 + ngot : 20 + ngot]
    own = Own(dims, counts, refs[20 + ngot : -1])
    rows_ref = refs[-1]
    row, lane = grid_iota(ny)
    edge = (lane == 0) | (lane == LANES - 1)

    def flux_in(axis):
        tn, sn, kn, hn = [faces.near(axis, f) for f in range(4)]
        to, ko, ho = [faces.own(axis, f) for f in (0, 2, 3)]
        if axis == 2:
            meet[2][...] = (0.5 * ko + to) + (0.5 * kn - tn)
            return half_flux(ko, to, kn, tn), sn, half_flux(ko, ho, kn, hn)
        for side in (0, 1):
            meet[axis][side] = (0.5 * ko[side] + to[side]) + (0.5 * kn[side] - tn[side])
        heat = [half_flux(*v) for v in zip(ko, to, kn, tn)]
        return heat, sn, [half_flux(*v) for v in zip(ko, ho, kn, hn)]

    heat_x, sugar_x, again_x = flux_in(0)
    for f, pair in enumerate(flux_in(1)):
        for side in (0, 1):
            rows_ref[side, pl.ds(f * nx, nx), :] = pair[side]
    heat_z, sugar_z, again_z = flux_in(2)
    in_heat, in_sugar = ready_z(heat_z), ready_z(sugar_z)

    def plane(x, carry):
        accs, misfit, part = carry
        here = pl.ds(x * ny, ny)
        heat = at_plane(x, nx, heat_x) + at_rows(x, rows_ref, 0, nx, row, ny)
        diff = at_plane(x, nx, sugar_x) + at_rows(x, rows_ref, 1, nx, row, ny)
        some_t = mtp_ref[here, :] + WARMTH_ADVANCE * heat
        some_s = msp_ref[here, :] + STEP_SOLUTE * diff
        heat_in = jnp.where(edge, unpack_z(in_heat, x), 0.0)
        diff = jnp.where(edge, unpack_z(in_sugar, x), 0.0)
        heat = heat + heat_in
        again = at_plane(x, nx, again_x) + at_rows(x, rows_ref, 2, nx, row, ny)
        mt = some_t + WARMTH_ADVANCE * heat_in
        ms = some_s + STEP_SOLUTE * diff
        h, l, soft, g = h_ref[here, :], l_ref[here, :], soft_ref[here, :], g_ref[here, :]
        pull = HIDDEN_WARMTH * mt + REJECT * ms
        by_speed = pull * l
        below = by_speed * g * slope_ref[here, :]
        part_t = mt - below
        pull_0 = HIDDEN_WARMTH * part_t + REJECT * (ms - LOWERING_COEF * below)
        mt_ref[here, :], ms_ref[here, :] = mt, ms
        sense_ref[here, :] = (
            by_speed * soft + pull_0 * w_ref[here, :] + g * soft * pull * v_ref[here, :]
        )
        misfit = misfit + (mt * mt + ms * ms)
        inner = inner_ref[here, :] + heat + WARMTH_ADVANCE * again
        part = part + (mt * inner + part_t * h)
        for f, v in enumerate((mt, ms)):
            own.rows(f, x, v)
        accs = tuple(pack_z(a, z, x, lane) for a, z in zip(accs, (some_t, some_s)))
        return accs, misfit, part

    zero = jnp.zeros((ny, LANES), F32)
    accs, misfit, part = lax.fori_loop(
        0, nx, plane, ((zero, zero), zero, zero), unroll=unroll
    )
    packs = (
        accs[0] + WARMTH_ADVANCE * turn_z(heat_z),
        accs[1] + STEP_SOLUTE * turn_z(sugar_z),
    )
    own.finish((mt_ref, ms_ref), packs)
    part = part + WARMTH_ADVANCE * turn_z(packs[0]) * again_z
    lane_row = lax.broadcasted_iota(jnp.int32, (1, LANES), 1)
    line = jnp.where(lane_row == 0, 0.5 * jnp.sum(misfit), 0.0)
    line = jnp.where(lane_row == 1, WARMTH_ADVANCE * jnp.sum(part), line)
    sums_ref[...] = jnp.broadcast_to(line, sums_ref.shape)


FLUX_WEIGHT = 0.5 * WARMTH_ADVANCE
SUGAR_WEIGHT = REJECT * STEP_SOLUTE


def crossing(k, t, mt, kn, tn, mtn, msn):
    return FLUX_WEIGHT * (mtn - mt) * (0.5 * (k + kn) + (t - tn)) + SUGAR_WEIGHT * msn


def third_inner_kernel(dims, unroll, *refs):
    nx, ny = dims
    t_ref, k_ref, mt_ref, ms_ref, w_ref, sense_ref = refs[:6]
    out_ref = refs[6]
    row, lane = grid_iota(ny)

    def plane(x, carry):
        t, k, mt, ms, from_prev = carry
        here = pl.ds(x * ny, ny)
        then = pl.ds(jnp.minimum(x + 1, nx - 1) * ny, ny)
        tn, kn, mtn, msn = [r[then, :] for r in (t_ref, k_ref, mt_ref, ms_ref)]
        total = from_prev - (6.0 * SUGAR_WEIGHT) * ms
        total = total + jnp.where(x == nx - 1, 0.0, crossing(k, t, mt, kn, tn, mtn, msn))
        to_next = crossing(kn, tn, mtn, k, t, mt, ms)
        for axis, index in ((0, row), (1, lane)):
            size = ny if axis == 0 else LANES
            ta, ka, mta, msa = [ahead(v, axis) for v in (t, k, mt, ms)]
            up = crossing(k, t, mt, ka, ta, mta, msa)
            down = crossing(ka, ta, mta, k, t, mt, ms)
            total = total + jnp.where(index == size - 1, 0.0, up)
            total = total + jnp.where(index == 0, 0.0, pltpu.roll(down, 1, axis))
        out_ref[here, :] = sense_ref[here, :] + w_ref[here, :] * total
        return tn, kn, mtn, msn, to_next

    top = pl.ds(0, ny)
    start = [r[top, :] for r in (t_ref, k_ref, mt_ref, ms_ref)]
    lax.fori_loop(0, nx, plane, (*start, jnp.zeros((ny, LANES), F32)), unroll=unroll)


def finish_kernel(dims, counts, cells, unroll, *refs):
    nx, ny = dims
    ngot = sum(swaps(n) for n in counts)
    w_ref, sense_ref, sums_ref = refs[:3]
    meet = refs[3:6]
    faces = Faces(dims, counts, refs[6:9], refs[9 : 9 + ngot])
    out_ref, misfit_ref, gradient_ref, rows_ref = refs[9 + ngot :]
    row, lane = grid_iota(ny)
    edge = (lane == 0) | (lane == LANES - 1)

    def into(axis):
        own, near, sugar = faces.own(axis, 0), faces.near(axis, 0), faces.near(axis, 1)
        if axis == 2:
            return FLUX_WEIGHT * (near - own) * meet[2][...] + SUGAR_WEIGHT * sugar
        return [
            FLUX_WEIGHT * (near[side] - own[side]) * meet[axis][side] + SUGAR_WEIGHT * sugar[side]
            for side in (0, 1)
        ]

    into_x, into_y, into_z = into(0), into(1), ready_z(into(2))
    rows_ref[0], rows_ref[1] = into_y

    def plane(x, _):
        here = pl.ds(x * ny, ny)
        value = jnp.where(edge, unpack_z(into_z, x), 0.0) + at_plane(x, nx, into_x)
        value = value + at_rows(x, rows_ref, 0, nx, row, ny)
        out_ref[here, :] = sense_ref[here, :] + w_ref[here, :] * value
        return 0

    lax.fori_loop(0, nx, plane, 0, unroll=unroll)
    sums = sums_ref[...]
    which = lax.broadcasted_iota(jnp.int32, sums.shape, 1)
    misfit_ref[0, 0] = jnp.sum(jnp.where(which == 0, sums, 0.0)) / cells
    gradient_ref[0, 0] = jnp.sum(jnp.where(which == 1, sums, 0.0)) / cells


VM = pl.BlockSpec(memory_space=pltpu.VMEM)
SM = pl.BlockSpec(memory_space=pltpu.SMEM)


def call(kernel, out, args, name, scratch=(), in_specs=None, out_specs=None, vmem=32, flops=0):
    size = sum(int(np.prod(a.shape)) * a.dtype.itemsize for a in args)
    return pl.pallas_call(
        kernel,
        out_shape=[jax.ShapeDtypeStruct(s, d) for s, d in out],
        in_specs=in_specs or [VM] * len(args),
        out_specs=out_specs or [VM] * len(out),
        scratch_shapes=list(scratch),
        name=name,
        cost_estimate=pl.CostEstimate(flops=flops, bytes_accessed=size, transcendentals=0),
        compiler_params=pltpu.CompilerParams(vmem_limit_bytes=vmem << 20),
    )(*args)


def per_device(counts, warmth, sugar, population, coefficient, sensors):
    nx, ny, nz = warmth.shape
    assert nz == LANES and 2 * nx <= LANES
    bins = population.shape[0]
    dims = (nx, ny)
    cells = nx * ny
    t, s, g = [v.reshape(cells, nz) for v in (warmth, sugar, coefficient)]
    c = population.reshape(bins, cells, nz)
    r = sensors.reshape(2, cells, nz)
    field = ((cells, nz), F32)
    hbm = pl.BlockSpec(memory_space=pl.ANY)
    work = cells * nz * 100

    chunks = 8
    res = call(
        functools.partial(prepare_kernel, dims, counts, bins, chunks),
        [field] * 5 + own_shapes(dims, counts, 3),
        (c, t, s),
        "prepare",
        [pltpu.VMEM((bins, cells, nz), F32), pltpu.SemaphoreType.DMA((chunks + 2,))],
        in_specs=[hbm] * 3,
        vmem=51,
    )
    k, l, m, t, s = res[:5]
    own = res[5:]
    got = send_faces(own, counts)
    pack = ((ny, nz), F32)
    tp, sp, hp, k1, l1, w, v, kpack = call(
        functools.partial(first_inner_kernel, dims, 8),
        [field] * 7 + [pack],
        (t, s, k, l, m, g),
        "first_inner",
        flops=work,
    )
    res = call(
        functools.partial(first_edge_kernel, dims, counts, 32),
        [field] * 3 + own_shapes(dims, counts, 4),
        (tp, sp, hp, k1, kpack, *own[:3], *got),
        "first_edge",
        [pltpu.VMEM((2, 2 * nx, nz), F32)],
    )
    t1, s1, h0 = res[:3]
    own1 = res[3:]
    got1 = send_faces(own1, counts)
    inner = call(
        functools.partial(second_inner_kernel, dims, 8),
        [field] * 5,
        (t1, s1, k1, h0, l1, g, r),
        "second_inner",
        flops=work,
    )
    devices = int(np.prod(counts))
    line = ((devices, LANES), F32)
    meet_shapes = own_shapes(dims, counts, 1)[:3]
    res = call(
        functools.partial(second_edge_kernel, dims, counts, 32),
        [field] * 3 + [line] + meet_shapes + own_shapes(dims, counts, 2),
        (h0, l1, w, v, g, *inner, *own1[:3], *got1),
        "second_edge",
        [pltpu.VMEM((2, 3 * nx, nz), F32)],
    )
    mt, ms, sense, sums = res[:4]
    meet, own2 = res[4:7], res[7:]
    got2 = send_faces(own2, counts)
    sums = lax.all_to_all(sums, AXES, 0, 0, tiled=True)
    (sense,) = call(
        functools.partial(third_inner_kernel, dims, 8),
        [field],
        (t1, k1, mt, ms, w, sense),
        "third_inner",
        flops=work,
    )
    sens, misfit, gradient = call(
        functools.partial(finish_kernel, dims, counts, float(cells * nz * devices), 64),
        [field, ((1, 1), F32), ((1, 1), F32)],
        (w, sense, sums, *meet, *own2[:3], *got2),
        "finish",
        [pltpu.VMEM((2, nx, nz), F32)],
        out_specs=[VM, SM, SM],
    )
    return sens.reshape(nx, ny, nz), misfit.reshape(()), gradient.reshape(())


def solution(mesh):
    counts = tuple(mesh.shape[a] for a in AXES)
    placed = (
        P("gx", "gy", "gz"),
        P("gx", "gy", "gz"),
        P(None, "gx", "gy", "gz"),
        P("gx", "gy", "gz"),
        P(None, "gx", "gy", "gz"),
    )
    return jax.shard_map(
        functools.partial(per_device, counts),
        mesh=mesh,
        in_specs=placed,
        out_specs=(P("gx", "gy", "gz"), P(), P()),
        check_vma=False,
    )
```

time: 50 us -> 43.2 us (0.86)
  waiting for transfers between devices: 12 us -> 5.39 us
  Pallas kernels: 15.9 us -> 12.5 us
  local copies, waits for them, and re-layouts: 0.01 us -> 3.14 us
    ppermute x15, waiting for transfers between devices: 12 us -> 5.39 us  [exchange(): lax.ppermute(p, axis, swap_pairs(count, kind))]
    pallas_call x4 -> x7, Pallas kernels: 15.9 us -> 12.5 us  [call(): pl.pallas_call(kernel, out_shape=[jax.ShapeDtypeStruct(s, d) for s, d in...]
    unnamed x4 -> x12, local copies, waits for them, and re-layouts: 0.01 us -> 3.14 us
  transfers between devices with their start and end apart: 16 -> 16, of which waited for: 7 -> 5; matrix products, arithmetic and copies ran while one was open for 0% -> 0% of each run, Pallas kernels for 0% -> 12%
where the time goes in v2:
time: 43.2 us; the launch traced here: 43 us
  starting transfers between devices  21.1 us (49%)
  Pallas kernels  12.5 us (29%)
  waiting for transfers between devices  5.39 us (12%)
  local copies, waits for them, and re-layouts  3.14 us (7%)
  between operations  0.76 us (2%)
    ppermute x15, starting transfers between devices, exchange(): lax.ppermute(p, axis, swap_pairs(count, kind))  18 us
    pallas_call x7, Pallas kernels, call(): pl.pallas_call(kernel, out_shape=[jax.ShapeDtypeStruct(s, d) for s, d in...  12.5 us
    ppermute x15, waiting for transfers between devices, exchange(): lax.ppermute(p, axis, swap_pairs(count, kind))  5.39 us
    unnamed x12, local copies, waits for them, and re-layouts  3.14 us
    all_to_all x1, starting transfers between devices, per_device(): sums = lax.all_to_all(sums, AXES, 0, 0, tiled=True)  3.12 us
  transfers between devices with their start and end apart: 16, of which 5 were waited for; matrix products, arithmetic and copies ran while one was open for 0% of the time, Pallas kernels for 12%

profile of v2, /device:TPU:0, one launch (start us, length us, event | category | flops | bytes accessed | tf_op | source)
XLA Modules:
  0.0 43.0 jit_solution(5060966275999925205)
XLA Ops:
  0.6 2.9 %prepare.1 = (f32[1024,128]{1,0:T(8,128)S(1)}, f32[1024,128]{1,0:T(8,128)S(1)}, f32[1024,128]{1,0:T(8,128)S(1)}, f32[1024,128]{1,0:T(8,128)S(1)}, f32[1024,128]{...) custom-call(f32[8,1024,128]{2,1,0:T(8,128)} %bitcast.17, ...), custom_call_target="tpu_custom_call" | custom-call | bytes 5242880 | tf_op jit(solution)/shard_map/prepare/pallas_call | solution.py:550
  3.6 3.0 %collective-permute-start.2 = (f32[192,128]{1,0:T(8,128)S(1)}, f32[192,128]{1,0:T(8,128)S(1)}, u32[]{:S(2)}, u32[]{:S(2)}) collective-permute-start(f32[192,128]{1,0:T(8,128)S(1)} %get-tuple-element.68), channel_id=1, source_target_pairs={{0,4},{4,0},{1,5},{5,1},{2,6},{6,2},{3,7},{7,3},{8,12},{12,8},{9,1... | collective-permute-start | bytes 294920 | tf_op jit(solution)/shard_map/ppermute | solution.py:58
  6.6 1.6 %collective-permute-start.1 = (f32[48,128]{1,0:T(8,128)S(1)}, f32[48,128]{1,0:T(8,128)S(1)}, u32[]{:S(2)}, u32[]{:S(2)}) collective-permute-start(f32[48,128]{1,0:T(8,128)S(1)} %get-tuple-element.67), channel_id=1, source_target_pairs={{0,24},{8,16},{16,8},{24,0},{1,25},{9,17},{17,9},{25,1},{2,26},{10... | collective-permute-start | bytes 73736 | tf_op jit(solution)/shard_map/ppermute | solution.py:58
  8.2 3.6 %collective-permute-start.4 = (f32[48,128]{1,0:T(8,128)S(1)}, f32[48,128]{1,0:T(8,128)S(1)}, u32[]{:S(2)}, u32[]{:S(2)}) collective-permute-start(f32[48,128]{1,0:T(8,128)S(1)} %get-tuple-element.65.refs_7_), channel_id=1, source_target_pairs={{0,3},{1,2},{2,1},{3,0},{4,7},{5,6},{6,5},{7,4},{8,11},{9,10},{10,... | collective-permute-start | bytes 73736 | tf_op jit(solution)/shard_map/ppermute | solution.py:58
  11.8 1.6 %first_inner.1 = (f32[1024,128]{1,0:T(8,128)S(1)}, f32[1024,128]{1,0:T(8,128)S(1)}, f32[1024,128]{1,0:T(8,128)S(1)}, f32[1024,128]{1,0:T(8,128)S(1)}, f32[1024,1...) custom-call(f32[1024,128]{1,0:T(8,128)S(1)} %get-tuple-element.52.refs_0_, ...), custom_call_target="tpu_custom_call" | custom-call | flops 13107200 | bytes 3145728 | tf_op jit(solution)/shard_map/first_inner/pallas_call | solution.py:550
  13.8 1.8 %collective-permute-done.3.refs_11_ = f32[48,128]{1,0:T(8,128)S(1)} collective-permute-done((f32[48,128]{1,0:T(8,128)S(1)}, f32[48,128]{1,0:T(8,128)S(1)}, u32[]{:S(2)}, u32[]{:S(2)}) %collective-permute-start.3) | collective-permute-done | bytes 24608 | tf_op jit(solution)/shard_map/ppermute | solution.py:58
  15.6 1.0 %first_edge.1 = (f32[1024,128]{1,0:T(8,128)S(1)}, f32[1024,128]{1,0:T(8,128)S(1)}, f32[1024,128]{1,0:T(8,128)S(1)}, f32[2,64,128]{2,1,0:T(8,128)S(1)}, f32[2,256...) custom-call(f32[1024,128]{1,0:T(8,128)S(1)} %get-tuple-element.58.re, ...), custom_call_target="tpu_custom_call" | custom-call | bytes 2572288 | tf_op jit(solution)/shard_map/first_edge/pallas_call | solution.py:550
  16.7 0.6 %collective-permute-start.7 = (f32[256,128]{1,0:T(8,128)S(1)}, f32[256,128]{1,0:T(8,128)S(1)}, u32[]{:S(2)}, u32[]{:S(2)}) collective-permute-start(f32[256,128]{1,0:T(8,128)S(1)} %get-tuple-element.84), channel_id=1, source_target_pairs={{0,4},{4,0},{1,5},{5,1},{2,6},{6,2},{3,7},{7,3},{8,12},{12,8},{9,1... | collective-permute-start | bytes 393224 | tf_op jit(solution)/shard_map/ppermute | solution.py:58
  17.2 0.6 %collective-permute-start.6 = (f32[64,128]{1,0:T(8,128)S(1)}, f32[64,128]{1,0:T(8,128)S(1)}, u32[]{:S(2)}, u32[]{:S(2)}) collective-permute-start(f32[64,128]{1,0:T(8,128)S(1)} %get-tuple-element.83), channel_id=1, source_target_pairs={{0,24},{8,16},{16,8},{24,0},{1,25},{9,17},{17,9},{25,1},{2,26},{10... | collective-permute-start | bytes 98312 | tf_op jit(solution)/shard_map/ppermute | solution.py:58
  17.9 1.8 %collective-permute-start.9 = (f32[64,128]{1,0:T(8,128)S(1)}, f32[64,128]{1,0:T(8,128)S(1)}, u32[]{:S(2)}, u32[]{:S(2)}) collective-permute-start(f32[64,128]{1,0:T(8,128)S(1)} %get-tuple-element.81.refs_12_), channel_id=1, source_target_pairs={{0,3},{1,2},{2,1},{3,0},{4,7},{5,6},{6,5},{7,4},{8,11},{9,10},{10,... | collective-permute-start | bytes 98312 | tf_op jit(solution)/shard_map/ppermute | solution.py:58
  19.7 2.1 %second_inner.1 = (f32[1024,128]{1,0:T(8,128)S(1)}, f32[1024,128]{1,0:T(8,128)S(1)}, f32[1024,128]{1,0:T(8,128)S(1)}, f32[1024,128]{1,0:T(8,128)S(1)}, f32[1024,128]{1,0:T(8,128)S(1)}) custom-call(f32[1024,128]{1,0:T(8,128)S(1)} %get-tuple-element.69.refs_0_, f32[1024,128]{1,0:T(8,128)S(1)} %get-tuple-element.73.refs_1_, ...), custom_call_target="tpu_custom_call" | custom-call | flops 13107200 | bytes 3670016 | tf_op jit(solution)/shard_map/second_inner/pallas_call | solution.py:550
  21.8 1.8 %collective-permute-done.9.refs_17_ = f32[64,128]{1,0:T(8,128)S(1)} collective-permute-done((f32[64,128]{1,0:T(8,128)S(1)}, f32[64,128]{1,0:T(8,128)S(1)}, u32[]{:S(2)}, u32[]{:S(2)}) %collective-permute-start.9) | collective-permute-done | bytes 32800 | tf_op jit(solution)/shard_map/ppermute | solution.py:58
  23.9 2.1 %second_edge.1 = (f32[1024,128]{1,0:T(8,128)S(1)}, f32[1024,128]{1,0:T(8,128)S(1)}, f32[1024,128]{1,0:T(8,128)S(1)}, f32[32,128]{1,0:T(8,128)}, f32[2,16,128]{2,...) custom-call(f32[1024,128]{1,0:T(8,128)S(1)} %get-tuple-element.70.re, ...), custom_call_target="tpu_custom_call" | custom-call | bytes 5865472 | tf_op jit(solution)/shard_map/second_edge/pallas_call | solution.py:550
  26.1 0.8 %copy-done.2 = f32[1024,128]{1,0:T(8,128)} copy-done((f32[1024,128]{1,0:T(8,128)}, f32[1024,128]{1,0:T(8,128)S(1)}, u32[]{:S(2)}) %copy-start.2) | copy-done | bytes 524312
  26.9 0.6 %copy-done.4 = f32[16,128]{1,0:T(8,128)} copy-done((f32[16,128]{1,0:T(8,128)}, f32[16,128]{1,0:T(8,128)S(1)}, u32[]{:S(2)}) %copy-start.4) | copy-done | bytes 8216
  27.5 1.5 %collective-permute-start.12 = (f32[128,128]{1,0:T(8,128)}, f32[128,128]{1,0:T(8,128)S(1)}, u32[]{:S(2)}, u32[]{:S(2)}) collective-permute-start(f32[128,128]{1,0:T(8,128)} %get-tuple-element.97), channel_id=1, source_target_pairs={{0,4},{4,0},{1,5},{5,1},{2,6},{6,2},{3,7},{7,3},{8,12},{12,8},{9,1... | collective-permute-start | bytes 196616 | tf_op jit(solution)/shard_map/ppermute | solution.py:58
  29.0 3.1 %all-to-all-start = ((f32[32,1,128]{2,1,0:T(1,128)}), f32[32,1,128]{2,1,0:T(1,128)S(1)}, u32[]{:S(2)}, u32[]{:S(2)}) async-start(f32[32,1,128]{2,1,0:T(1,128)} %bitcast.6), calls=%async_computation | async-start | bytes 32768 | tf_op jit(solution)/shard_map/all_to_all | solution.py:626
  32.4 1.6 %collective-permute-start.11 = (f32[32,128]{1,0:T(8,128)}, f32[32,128]{1,0:T(8,128)S(1)}, u32[]{:S(2)}, u32[]{:S(2)}) collective-permute-start(f32[32,128]{1,0:T(8,128)} %get-tuple-element.96), channel_id=1, source_target_pairs={{0,24},{8,16},{16,8},{24,0},{1,25},{9,17},{17,9},{25,1},{2,26},{10... | collective-permute-start | bytes 49160 | tf_op jit(solution)/shard_map/ppermute | solution.py:58
  34.0 3.3 %collective-permute-start.14 = (f32[32,128]{1,0:T(8,128)S(1)}, f32[32,128]{1,0:T(8,128)S(1)}, u32[]{:S(2)}, u32[]{:S(2)}) collective-permute-start(f32[32,128]{1,0:T(8,128)S(1)} %get-tuple-element.94.refs_8_), channel_id=1, source_target_pairs={{0,3},{1,2},{2,1},{3,0},{4,7},{5,6},{6,5},{7,4},{8,11},{9,10},{10,... | collective-permute-start | bytes 49160 | tf_op jit(solution)/shard_map/ppermute | solution.py:58
  37.4 1.0 %copy-done.3 = f32[1024,128]{1,0:T(8,128)S(1)} copy-done((f32[1024,128]{1,0:T(8,128)S(1)}, f32[1024,128]{1,0:T(8,128)}, u32[]{:S(2)}) %copy-start.3) | copy-done | bytes 524312
  38.4 1.6 %third_inner.1.refs_1_ = f32[1024,128]{1,0:T(8,128)S(1)} custom-call(f32[1024,128]{1,0:T(8,128)S(1)} %get-tuple-element.69.refs_0_, f32[1024,128]{1,0:T(8,128)S(1)} %get-tuple-element.61.refs_3_.refs_2_.refs_1_, f32[1024,128]{1,0:T(8,128)S(1)} %get-tuple-element.85.refs_2_, f32[1024,128]{1,0:T(8,128)S(1)} %get-tuple-element.86.refs_3_, ...), custom_call_target="tpu_custom_call" | custom-call | flops 13107200 | bytes 3145728 | tf_op jit(solution)/shard_map/third_inner/pallas_call | solution.py:550
  40.1 1.0 %collective-permute-done.13.refs_12_ = f32[32,128]{1,0:T(8,128)S(1)} collective-permute-done((f32[32,128]{1,0:T(8,128)S(1)}, f32[32,128]{1,0:T(8,128)S(1)}, u32[]{:S(2)}, u32[]{:S(2)}) %collective-permute-start.13) | collective-permute-done | bytes 16416 | tf_op jit(solution)/shard_map/ppermute | solution.py:58
  41.1 0.7 %copy-done.5 = f32[16,128]{1,0:T(8,128)S(1)} copy-done((f32[16,128]{1,0:T(8,128)S(1)}, f32[16,128]{1,0:T(8,128)}, u32[]{:S(2)}) %copy-start.5) | copy-done | bytes 8216
  41.8 1.1 %finish.1 = (f32[1024,128]{1,0:T(8,128)}, f32[1,1]{1,0:T(1,128)}, f32[1,1]{1,0:T(1,128)}) custom-call(f32[1024,128]{1,0:T(8,128)S(1)} %get-tuple-element.57.refs_2_.refs_4_.refs_0_, f32[1024,128]{1,0:T(8,128)S(1)} %third_inner.1.refs_1_, f32[32,128]{1,0:T(8,128)S(1)} %bitcast.16, f32[2,16,128]{2,1,0:T(8,128)S(1)} %get-tuple-element.89.refs_3_, ...), custom_call_target="tpu_custom_call" | custom-call | bytes 1466368 | tf_op jit(solution)/shard_map/finish/pallas_call | solution.py:550
  (27 shorter events, 1.1 us)
Async XLA Ops:
  0.6 11.2 %copy-start = (f32[64,16,128]{2,1,0:T(8,128)S(1)}, f32[64,16,128]{2,1,0:T(8,128)}, u32[]{:S(2)}) copy-start(f32[64,16,128]{2,1,0:T(8,128)} %param.8) | copy-start | bytes 1572868
  3.6 16.1 %copy-start.1 = (bf16[2,64,16,128]{3,2,1,0:T(8,128)(2,1)S(1)}, bf16[2,64,16,128]{3,2,1,0:T(8,128)(2,1)}, u32[]{:S(2)}) copy-start(bf16[2,64,16,128]{3,2,1,0:T(8,128)(2,1)} %param.9) | copy-start | bytes 1572868
  3.6 12.1 %collective-permute-start.2 = (f32[192,128]{1,0:T(8,128)S(1)}, f32[192,128]{1,0:T(8,128)S(1)}, u32[]{:S(2)}, u32[]{:S(2)}) collective-permute-start(f32[192,128]{1,0:T(8,128)S(1)} %get-tuple-element.68), channel_id=1, source_target_pairs={{0,4},{4,0},{1,5},{5,1},{2,6},{6,2},{3,7},{7,3},{8,12},{12,8},{9,1... | collective-permute-start | bytes 294920 | tf_op jit(solution)/shard_map/ppermute | solution.py:58
  6.6 6.8 %collective-permute-start = (f32[48,128]{1,0:T(8,128)S(1)}, f32[48,128]{1,0:T(8,128)S(1)}, u32[]{:S(2)}, u32[]{:S(2)}) collective-permute-start(f32[48,128]{1,0:T(8,128)S(1)} %get-tuple-element.66), channel_id=1, source_target_pairs={{0,8},{8,0},{16,24},{24,16},{1,9},{9,1},{17,25},{25,17},{2,10},{10... | collective-permute-start | bytes 73736 | tf_op jit(solution)/shard_map/ppermute | solution.py:58
  6.6 6.9 %collective-permute-start.1 = (f32[48,128]{1,0:T(8,128)S(1)}, f32[48,128]{1,0:T(8,128)S(1)}, u32[]{:S(2)}, u32[]{:S(2)}) collective-permute-start(f32[48,128]{1,0:T(8,128)S(1)} %get-tuple-element.67), channel_id=1, source_target_pairs={{0,24},{8,16},{16,8},{24,0},{1,25},{9,17},{17,9},{25,1},{2,26},{10... | collective-permute-start | bytes 73736 | tf_op jit(solution)/shard_map/ppermute | solution.py:58
  8.2 5.6 %collective-permute-start.4 = (f32[48,128]{1,0:T(8,128)S(1)}, f32[48,128]{1,0:T(8,128)S(1)}, u32[]{:S(2)}, u32[]{:S(2)}) collective-permute-start(f32[48,128]{1,0:T(8,128)S(1)} %get-tuple-element.65.refs_7_), channel_id=1, source_target_pairs={{0,3},{1,2},{2,1},{3,0},{4,7},{5,6},{6,5},{7,4},{8,11},{9,10},{10,... | collective-permute-start | bytes 73736 | tf_op jit(solution)/shard_map/ppermute | solution.py:58
  11.8 3.8 %collective-permute-start.3 = (f32[48,128]{1,0:T(8,128)S(1)}, f32[48,128]{1,0:T(8,128)S(1)}, u32[]{:S(2)}, u32[]{:S(2)}) collective-permute-start(f32[48,128]{1,0:T(8,128)S(1)} %get-tuple-element.65.refs_7_), channel_id=1, source_target_pairs={{0,1},{1,0},{2,3},{3,2},{4,5},{5,4},{6,7},{7,6},{8,9},{9,8},{10,11... | collective-permute-start | bytes 73736 | tf_op jit(solution)/shard_map/ppermute | solution.py:58
  16.7 7.3 %collective-permute-start.7 = (f32[256,128]{1,0:T(8,128)S(1)}, f32[256,128]{1,0:T(8,128)S(1)}, u32[]{:S(2)}, u32[]{:S(2)}) collective-permute-start(f32[256,128]{1,0:T(8,128)S(1)} %get-tuple-element.84), channel_id=1, source_target_pairs={{0,4},{4,0},{1,5},{5,1},{2,6},{6,2},{3,7},{7,3},{8,12},{12,8},{9,1... | collective-permute-start | bytes 393224 | tf_op jit(solution)/shard_map/ppermute | solution.py:58
  17.2 4.5 %collective-permute-start.5 = (f32[64,128]{1,0:T(8,128)S(1)}, f32[64,128]{1,0:T(8,128)S(1)}, u32[]{:S(2)}, u32[]{:S(2)}) collective-permute-start(f32[64,128]{1,0:T(8,128)S(1)} %get-tuple-element.82), channel_id=1, source_target_pairs={{0,8},{8,0},{16,24},{24,16},{1,9},{9,1},{17,25},{25,17},{2,10},{10... | collective-permute-start | bytes 98312 | tf_op jit(solution)/shard_map/ppermute | solution.py:58
  17.2 4.5 %collective-permute-start.6 = (f32[64,128]{1,0:T(8,128)S(1)}, f32[64,128]{1,0:T(8,128)S(1)}, u32[]{:S(2)}, u32[]{:S(2)}) collective-permute-start(f32[64,128]{1,0:T(8,128)S(1)} %get-tuple-element.83), channel_id=1, source_target_pairs={{0,24},{8,16},{16,8},{24,0},{1,25},{9,17},{17,9},{25,1},{2,26},{10... | collective-permute-start | bytes 98312 | tf_op jit(solution)/shard_map/ppermute | solution.py:58
  17.9 5.7 %collective-permute-start.9 = (f32[64,128]{1,0:T(8,128)S(1)}, f32[64,128]{1,0:T(8,128)S(1)}, u32[]{:S(2)}, u32[]{:S(2)}) collective-permute-start(f32[64,128]{1,0:T(8,128)S(1)} %get-tuple-element.81.refs_12_), channel_id=1, source_target_pairs={{0,3},{1,2},{2,1},{3,0},{4,7},{5,6},{6,5},{7,4},{8,11},{9,10},{10,... | collective-permute-start | bytes 98312 | tf_op jit(solution)/shard_map/ppermute | solution.py:58
  19.7 4.3 %collective-permute-start.8 = (f32[64,128]{1,0:T(8,128)S(1)}, f32[64,128]{1,0:T(8,128)S(1)}, u32[]{:S(2)}, u32[]{:S(2)}) collective-permute-start(f32[64,128]{1,0:T(8,128)S(1)} %get-tuple-element.81.refs_12_), channel_id=1, source_target_pairs={{0,1},{1,0},{2,3},{3,2},{4,5},{5,4},{6,7},{7,6},{8,9},{9,8},{10,11... | collective-permute-start | bytes 98312 | tf_op jit(solution)/shard_map/ppermute | solution.py:58
  26.1 0.8 %copy-start.2 = (f32[1024,128]{1,0:T(8,128)}, f32[1024,128]{1,0:T(8,128)S(1)}, u32[]{:S(2)}) copy-start(f32[1024,128]{1,0:T(8,128)S(1)} %get-tuple-element.87.refs_5_) | copy-start | bytes 1572868
  26.9 0.6 %copy-start.4 = (f32[16,128]{1,0:T(8,128)}, f32[16,128]{1,0:T(8,128)S(1)}, u32[]{:S(2)}) copy-start(f32[16,128]{1,0:T(8,128)S(1)} %get-tuple-element.91.refs_5_) | copy-start | bytes 24580
  27.5 13.7 %collective-permute-start.12 = (f32[128,128]{1,0:T(8,128)}, f32[128,128]{1,0:T(8,128)S(1)}, u32[]{:S(2)}, u32[]{:S(2)}) collective-permute-start(f32[128,128]{1,0:T(8,128)} %get-tuple-element.97), channel_id=1, source_target_pairs={{0,4},{4,0},{1,5},{5,1},{2,6},{6,2},{3,7},{7,3},{8,12},{12,8},{9,1... | collective-permute-start | bytes 196616 | tf_op jit(solution)/shard_map/ppermute | solution.py:58
  29.0 12.2 %all-to-all-start = ((f32[32,1,128]{2,1,0:T(1,128)}), f32[32,1,128]{2,1,0:T(1,128)S(1)}, u32[]{:S(2)}, u32[]{:S(2)}) async-start(f32[32,1,128]{2,1,0:T(1,128)} %bitcast.6), calls=%async_computation | async-start | bytes 32768 | tf_op jit(solution)/shard_map/all_to_all | solution.py:626
  32.1 8.0 %collective-permute-start.10 = (f32[32,128]{1,0:T(8,128)}, f32[32,128]{1,0:T(8,128)S(1)}, u32[]{:S(2)}, u32[]{:S(2)}) collective-permute-start(f32[32,128]{1,0:T(8,128)} %get-tuple-element.95), channel_id=1, source_target_pairs={{0,8},{8,0},{16,24},{24,16},{1,9},{9,1},{17,25},{25,17},{2,10},{10... | collective-permute-start | bytes 49160 | tf_op jit(solution)/shard_map/ppermute | solution.py:58
  32.4 7.7 %collective-permute-start.11 = (f32[32,128]{1,0:T(8,128)}, f32[32,128]{1,0:T(8,128)S(1)}, u32[]{:S(2)}, u32[]{:S(2)}) collective-permute-start(f32[32,128]{1,0:T(8,128)} %get-tuple-element.96), channel_id=1, source_target_pairs={{0,24},{8,16},{16,8},{24,0},{1,25},{9,17},{17,9},{25,1},{2,26},{10... | collective-permute-start | bytes 49160 | tf_op jit(solution)/shard_map/ppermute | solution.py:58
  34.0 6.0 %collective-permute-start.14 = (f32[32,128]{1,0:T(8,128)S(1)}, f32[32,128]{1,0:T(8,128)S(1)}, u32[]{:S(2)}, u32[]{:S(2)}) collective-permute-start(f32[32,128]{1,0:T(8,128)S(1)} %get-tuple-element.94.refs_8_), channel_id=1, source_target_pairs={{0,3},{1,2},{2,1},{3,0},{4,7},{5,6},{6,5},{7,4},{8,11},{9,10},{10,... | collective-permute-start | bytes 49160 | tf_op jit(solution)/shard_map/ppermute | solution.py:58
  37.4 3.7 %collective-permute-start.13 = (f32[32,128]{1,0:T(8,128)S(1)}, f32[32,128]{1,0:T(8,128)S(1)}, u32[]{:S(2)}, u32[]{:S(2)}) collective-permute-start(f32[32,128]{1,0:T(8,128)S(1)} %get-tuple-element.94.refs_8_), channel_id=1, source_target_pairs={{0,1},{1,0},{2,3},{3,2},{4,5},{5,4},{6,7},{7,6},{8,9},{9,8},{10,11... | collective-permute-start | bytes 49160 | tf_op jit(solution)/shard_map/ppermute | solution.py:58
  37.4 1.0 %copy-start.3 = (f32[1024,128]{1,0:T(8,128)S(1)}, f32[1024,128]{1,0:T(8,128)}, u32[]{:S(2)}) copy-start(f32[1024,128]{1,0:T(8,128)} %copy-done.2) | copy-start | bytes 1572868
  41.1 0.7 %copy-start.5 = (f32[16,128]{1,0:T(8,128)S(1)}, f32[16,128]{1,0:T(8,128)}, u32[]{:S(2)}) copy-start(f32[16,128]{1,0:T(8,128)} %copy-done.4) | copy-start | bytes 24580

commit v3 on v2

--- a/solution.py
+++ b/solution.py
@@ -42,20 +42,35 @@
     return k, l, (m_const, m)
 
 
-def swap_pairs(count, kind):
-    if kind == 0:
-        return [(i, i ^ 1) for i in range(count)]
-    return [(i, (i + 1) % count if i % 2 else (i - 1) % count) for i in range(count)]
+SPARE = {"gx": 0, "gz": 0, "gy": 2}
+
+
+def swap_pairs(counts, axis, kind):
+    pairs = []
+    for at in np.ndindex(*counts):
+        to = list(at)
+        i = at[axis]
+        to[axis] = i ^ 1 if kind == 0 else (i + 1 if i % 2 else i - 1)
+        if not 0 <= to[axis] < counts[axis]:
+            to[axis] = i
+            spare = SPARE[AXES[axis]]
+            if spare == axis:
+                to[axis] = counts[axis] - 1 - i
+            else:
+                to[spare] = at[spare] ^ 1
+        pairs.append(tuple(int(np.ravel_multi_index(v, counts)) for v in (at, to)))
+    return pairs
 
 
 def swaps(count):
     return {1: 0, 2: 1}.get(count, 2)
 
 
-def exchange(payloads, axis):
-    count = lax.axis_size(axis)
-    assert count == 1 or count % 2 == 0
-    return [lax.ppermute(p, axis, swap_pairs(count, kind)) for kind, p in enumerate(payloads)]
+def exchange(payloads, counts, axis):
+    assert counts[axis] == 1 or counts[axis] % 2 == 0
+    return [
+        lax.ppermute(p, AXES, swap_pairs(counts, axis, kind)) for kind, p in enumerate(payloads)
+    ]
 
 
 class Side:
@@ -124,12 +139,13 @@
 
 
 class Own:
-    def __init__(self, dims, counts, refs):
+    def __init__(self, dims, counts, refs, scratch=None):
         self.nx, self.ny = dims
         self.counts = counts
-        self.x, self.y, self.z = refs[:3]
+        self.x, self.y = scratch or refs[:2]
+        self.z, *out = refs if scratch else refs[2:]
         a = swaps(counts[0])
-        self.out = (refs[3 : 3 + a], refs[3 + a :])
+        self.out = (out[:a], out[a:])
 
     def rows(self, f, x, value):
         self.y[0, pl.ds(f * self.nx + x, 1), :] = value[:1, :]
@@ -159,8 +175,8 @@
     a = swaps(counts[0])
     payloads = (own[3 : 3 + a], own[3 + a :], [own[2]] * swaps(counts[2]))
     got = []
-    for payload, axis in zip(payloads, AXES):
-        got += exchange(payload, axis)
+    for axis, payload in enumerate(payloads):
+        got += exchange(payload, counts, axis)
     return got
 
 
@@ -398,8 +414,8 @@
     faces = Faces(dims, counts, refs[10:13], refs[13 : 13 + ngot])
     mt_ref, ms_ref, sense_ref, sums_ref = refs[13 + ngot : 17 + ngot]
     meet = refs[17 + ngot : 20 + ngot]
-    own = Own(dims, counts, refs[20 + ngot : -1])
-    rows_ref = refs[-1]
+    own = Own(dims, counts, refs[20 + ngot : -3], refs[-2:])
+    rows_ref = refs[-3]
     row, lane = grid_iota(ny)
     edge = (lane == 0) | (lane == LANES - 1)
 
@@ -479,14 +495,16 @@
 def third_inner_kernel(dims, unroll, *refs):
     nx, ny = dims
     t_ref, k_ref, mt_ref, ms_ref, w_ref, sense_ref = refs[:6]
-    out_ref = refs[6]
+    out_ref, x_ref, y_ref = refs[6:]
     row, lane = grid_iota(ny)
+    x_ref[0], x_ref[1] = mt_ref[pl.ds(0, ny), :], mt_ref[pl.ds((nx - 1) * ny, ny), :]
 
     def plane(x, carry):
         t, k, mt, ms, from_prev = carry
         here = pl.ds(x * ny, ny)
         then = pl.ds(jnp.minimum(x + 1, nx - 1) * ny, ny)
         tn, kn, mtn, msn = [r[then, :] for r in (t_ref, k_ref, mt_ref, ms_ref)]
+        y_ref[0, pl.ds(x, 1), :], y_ref[1, pl.ds(x, 1), :] = mt[:1, :], mt[ny - 1 :, :]
         total = from_prev - (6.0 * SUGAR_WEIGHT) * ms
         total = total + jnp.where(x == nx - 1, 0.0, crossing(k, t, mt, kn, tn, mtn, msn))
         to_next = crossing(kn, tn, mtn, k, t, mt, ms)
@@ -545,7 +563,7 @@
 SM = pl.BlockSpec(memory_space=pltpu.SMEM)
 
 
-def call(kernel, out, args, name, scratch=(), in_specs=None, out_specs=None, vmem=32, flops=0):
+def call(kernel, out, args, name, scratch=(), in_specs=None, out_specs=None, vmem=32, flops=0, aliases={}):
     size = sum(int(np.prod(a.shape)) * a.dtype.itemsize for a in args)
     return pl.pallas_call(
         kernel,
@@ -554,6 +572,7 @@
         out_specs=out_specs or [VM] * len(out),
         scratch_shapes=list(scratch),
         name=name,
+        input_output_aliases=aliases,
         cost_estimate=pl.CostEstimate(flops=flops, bytes_accessed=size, transcendentals=0),
         compiler_params=pltpu.CompilerParams(vmem_limit_bytes=vmem << 20),
     )(*args)
@@ -594,7 +613,7 @@
         flops=work,
     )
     res = call(
-        functools.partial(first_edge_kernel, dims, counts, 32),
+        functools.partial(first_edge_kernel, dims, counts, 64),
         [field] * 3 + own_shapes(dims, counts, 4),
         (tp, sp, hp, k1, kpack, *own[:3], *got),
         "first_edge",
@@ -614,27 +633,28 @@
     line = ((devices, LANES), F32)
     meet_shapes = own_shapes(dims, counts, 1)[:3]
     res = call(
-        functools.partial(second_edge_kernel, dims, counts, 32),
-        [field] * 3 + [line] + meet_shapes + own_shapes(dims, counts, 2),
+        functools.partial(second_edge_kernel, dims, counts, 64),
+        [field] * 3 + [line] + meet_shapes + own_shapes(dims, counts, 2)[2:],
         (h0, l1, w, v, g, *inner, *own1[:3], *got1),
         "second_edge",
-        [pltpu.VMEM((2, 3 * nx, nz), F32)],
+        [pltpu.VMEM(v, F32) for v in ((2, 3 * nx, nz), (2, 2 * ny, nz), (2, 2 * nx, nz))],
     )
     mt, ms, sense, sums = res[:4]
-    meet, own2 = res[4:7], res[7:]
-    got2 = send_faces(own2, counts)
+    meet, sent = res[4:7], res[7:]
+    got2 = send_faces((None, None, *sent), counts)
     sums = lax.all_to_all(sums, AXES, 0, 0, tiled=True)
-    (sense,) = call(
-        functools.partial(third_inner_kernel, dims, 8),
-        [field],
+    sense, *kept = call(
+        functools.partial(third_inner_kernel, dims, 16),
+        [field] + meet_shapes[:2],
         (t1, k1, mt, ms, w, sense),
         "third_inner",
+        aliases={5: 0},
         flops=work,
     )
     sens, misfit, gradient = call(
         functools.partial(finish_kernel, dims, counts, float(cells * nz * devices), 64),
         [field, ((1, 1), F32), ((1, 1), F32)],
-        (w, sense, sums, *meet, *own2[:3], *got2),
+        (w, sense, sums, *meet, *kept, sent[0], *got2),
         "finish",
         [pltpu.VMEM((2, nx, nz), F32)],
         out_specs=[VM, SM, SM],

time: 43.2 us -> 35.7 us (0.83)
  waiting for transfers between devices: 5.39 us -> 0.93 us
  local copies, waits for them, and re-layouts: 3.14 us -> 0.01 us
  starting transfers between devices: 21.1 us -> 21.9 us
  Pallas kernels: 12.5 us -> 11.8 us
    ppermute x15, waiting for transfers between devices: 5.39 us -> 0.5 us  [exchange(): lax.ppermute(p, AXES, swap_pairs(counts, axis, kind))]
    unnamed x12 -> x4, local copies, waits for them, and re-layouts: 3.14 us -> 0.01 us
    all_to_all x1, starting transfers between devices: 3.12 us -> 4.07 us  [per_device(): sums = lax.all_to_all(sums, AXES, 0, 0, tiled=True)]
    pallas_call x7, Pallas kernels: 12.5 us -> 11.8 us  [call(): pl.pallas_call(kernel, out_shape=[jax.ShapeDtypeStruct(s, d) for s, d in...]
  transfers between devices with their start and end apart: 16 -> 16, of which waited for: 5 -> 3; matrix products, arithmetic and copies ran while one was open for 0% -> 0% of each run, Pallas kernels for 12% -> 14%
where the time goes in v3:
time: 35.7 us; the launch traced here: 35.5 us
  starting transfers between devices  21.9 us (61%)
  Pallas kernels  11.8 us (33%)
  waiting for transfers between devices  0.93 us (3%)
  between operations  0.79 us (2%)
    ppermute x15, starting transfers between devices, exchange(): lax.ppermute(p, AXES, swap_pairs(counts, axis, kind))  17.9 us
    pallas_call x7, Pallas kernels, call(): pl.pallas_call(kernel, out_shape=[jax.ShapeDtypeStruct(s, d) for s, d in...  11.8 us
    all_to_all x1, starting transfers between devices, per_device(): sums = lax.all_to_all(sums, AXES, 0, 0, tiled=True)  4.07 us
  transfers between devices with their start and end apart: 16, of which 3 were waited for; matrix products, arithmetic and copies ran while one was open for 0% of the time, Pallas kernels for 14%

profile of v3, /device:TPU:0, one launch (start us, length us, event | category | flops | bytes accessed | tf_op | source)
XLA Modules:
  0.0 35.5 jit_solution(1730246947178580190)
XLA Ops:
  0.6 2.9 %prepare.1 = (f32[1024,128]{1,0:T(8,128)S(1)}, f32[1024,128]{1,0:T(8,128)S(1)}, f32[1024,128]{1,0:T(8,128)S(1)}, f32[1024,128]{1,0:T(8,128)S(1)}, f32[1024,128]{...) custom-call(f32[8,1024,128]{2,1,0:T(8,128)} %bitcast.17, ...), custom_call_target="tpu_custom_call" | custom-call | bytes 5242880 | tf_op jit(solution)/shard_map/prepare/pallas_call | solution.py:568
  3.6 0.0 copy-start.1
  3.6 3.0 %collective-permute-start.2 = (f32[192,128]{1,0:T(8,128)S(1)}, f32[192,128]{1,0:T(8,128)S(1)}, u32[]{:S(2)}, u32[]{:S(2)}) collective-permute-start(f32[192,128]{1,0:T(8,128)S(1)} %get-tuple-element.69), channel_id=1, source_target_pairs={{0,4},{1,5},{2,6},{3,7},{4,0},{5,1},{6,2},{7,3},{8,12},{9,13},{10,... | collective-permute-start | bytes 294920 | tf_op jit(solution)/shard_map/ppermute | solution.py:72
  6.6 1.6 %collective-permute-start.1 = (f32[48,128]{1,0:T(8,128)S(1)}, f32[48,128]{1,0:T(8,128)S(1)}, u32[]{:S(2)}, u32[]{:S(2)}) collective-permute-start(f32[48,128]{1,0:T(8,128)S(1)} %get-tuple-element.68), channel_id=1, source_target_pairs={{0,24},{1,25},{2,26},{3,27},{4,28},{5,29},{6,30},{7,31},{8,16},{9,... | collective-permute-start | bytes 73736 | tf_op jit(solution)/shard_map/ppermute | solution.py:72
  8.2 3.1 %collective-permute-start.3 = (f32[48,128]{1,0:T(8,128)S(1)}, f32[48,128]{1,0:T(8,128)S(1)}, u32[]{:S(2)}, u32[]{:S(2)}) collective-permute-start(f32[48,128]{1,0:T(8,128)S(1)} %get-tuple-element.66.refs_7_), channel_id=1, source_target_pairs={{0,1},{1,0},{2,3},{3,2},{4,5},{5,4},{6,7},{7,6},{8,9},{9,8},{10,11... | collective-permute-start | bytes 73736 | tf_op jit(solution)/shard_map/ppermute | solution.py:72
  11.4 1.6 %first_inner.1 = (f32[1024,128]{1,0:T(8,128)S(1)}, f32[1024,128]{1,0:T(8,128)S(1)}, f32[1024,128]{1,0:T(8,128)S(1)}, f32[1024,128]{1,0:T(8,128)S(1)}, f32[1024,1...) custom-call(f32[1024,128]{1,0:T(8,128)S(1)} %get-tuple-element.53.refs_0_, ...), custom_call_target="tpu_custom_call" | custom-call | flops 13107200 | bytes 3145728 | tf_op jit(solution)/shard_map/first_inner/pallas_call | solution.py:568
  13.0 0.2 collective-permute-done.3.refs_11_
  13.2 0.9 %first_edge.1 = (f32[1024,128]{1,0:T(8,128)S(1)}, f32[1024,128]{1,0:T(8,128)S(1)}, f32[1024,128]{1,0:T(8,128)S(1)}, f32[2,64,128]{2,1,0:T(8,128)S(1)}, f32[2,256...) custom-call(f32[1024,128]{1,0:T(8,128)S(1)} %get-tuple-element.59.re, ...), custom_call_target="tpu_custom_call" | custom-call | bytes 2572288 | tf_op jit(solution)/shard_map/first_edge/pallas_call | solution.py:568
  14.0 0.6 %collective-permute-start.7 = (f32[256,128]{1,0:T(8,128)S(1)}, f32[256,128]{1,0:T(8,128)S(1)}, u32[]{:S(2)}, u32[]{:S(2)}) collective-permute-start(f32[256,128]{1,0:T(8,128)S(1)} %get-tuple-element.85), channel_id=1, source_target_pairs={{0,4},{1,5},{2,6},{3,7},{4,0},{5,1},{6,2},{7,3},{8,12},{9,13},{10,... | collective-permute-start | bytes 393224 | tf_op jit(solution)/shard_map/ppermute | solution.py:72
  14.6 0.6 %collective-permute-start.6 = (f32[64,128]{1,0:T(8,128)S(1)}, f32[64,128]{1,0:T(8,128)S(1)}, u32[]{:S(2)}, u32[]{:S(2)}) collective-permute-start(f32[64,128]{1,0:T(8,128)S(1)} %get-tuple-element.84), channel_id=1, source_target_pairs={{0,24},{1,25},{2,26},{3,27},{4,28},{5,29},{6,30},{7,31},{8,16},{9,... | collective-permute-start | bytes 98312 | tf_op jit(solution)/shard_map/ppermute | solution.py:72
  15.3 0.0 collective-permute-start.9
  15.3 2.5 %collective-permute-start.8 = (f32[64,128]{1,0:T(8,128)S(1)}, f32[64,128]{1,0:T(8,128)S(1)}, u32[]{:S(2)}, u32[]{:S(2)}) collective-permute-start(f32[64,128]{1,0:T(8,128)S(1)} %get-tuple-element.82.refs_12_), channel_id=1, source_target_pairs={{0,1},{1,0},{2,3},{3,2},{4,5},{5,4},{6,7},{7,6},{8,9},{9,8},{10,11... | collective-permute-start | bytes 98312 | tf_op jit(solution)/shard_map/ppermute | solution.py:72
  17.7 2.1 %second_inner.1 = (f32[1024,128]{1,0:T(8,128)S(1)}, f32[1024,128]{1,0:T(8,128)S(1)}, f32[1024,128]{1,0:T(8,128)S(1)}, f32[1024,128]{1,0:T(8,128)S(1)}, f32[1024,128]{1,0:T(8,128)S(1)}) custom-call(f32[1024,128]{1,0:T(8,128)S(1)} %get-tuple-element.70.refs_0_, f32[1024,128]{1,0:T(8,128)S(1)} %get-tuple-element.74.refs_1_, ...), custom_call_target="tpu_custom_call" | custom-call | flops 13107200 | bytes 3670016 | tf_op jit(solution)/shard_map/second_inner/pallas_call | solution.py:568
  19.9 1.8 %second_edge.1 = (f32[1024,128]{1,0:T(8,128)S(1)}, f32[1024,128]{1,0:T(8,128)S(1)}, f32[1024,128]{1,0:T(8,128)S(1)}, f32[32,128]{1,0:T(8,128)}, f32[2,16,128]{2,...) custom-call(f32[1024,128]{1,0:T(8,128)S(1)} %get-tuple-element.71.re, ...), custom_call_target="tpu_custom_call" | custom-call | bytes 5865472 | tf_op jit(solution)/shard_map/second_edge/pallas_call | solution.py:568
  21.7 1.5 %collective-permute-start.12 = (f32[128,128]{1,0:T(8,128)S(1)}, f32[128,128]{1,0:T(8,128)S(1)}, u32[]{:S(2)}, u32[]{:S(2)}) collective-permute-start(f32[128,128]{1,0:T(8,128)S(1)} %get-tuple-element.99), channel_id=1, source_target_pairs={{0,4},{1,5},{2,6},{3,7},{4,0},{5,1},{6,2},{7,3},{8,12},{9,13},{10,... | collective-permute-start | bytes 196616 | tf_op jit(solution)/shard_map/ppermute | solution.py:72
  23.2 4.1 %all-to-all-start = ((f32[32,1,128]{2,1,0:T(1,128)}), f32[32,1,128]{2,1,0:T(1,128)S(1)}, u32[]{:S(2)}, u32[]{:S(2)}) async-start(f32[32,1,128]{2,1,0:T(1,128)} %bitcast.6), calls=%async_computation | async-start | bytes 32768 | tf_op jit(solution)/shard_map/all_to_all | solution.py:645
  27.3 0.3 collective-permute-start.10
  27.6 1.6 %collective-permute-start.11 = (f32[32,128]{1,0:T(8,128)}, f32[32,128]{1,0:T(8,128)S(1)}, u32[]{:S(2)}, u32[]{:S(2)}) collective-permute-start(f32[32,128]{1,0:T(8,128)} %get-tuple-element.98), channel_id=1, source_target_pairs={{0,24},{1,25},{2,26},{3,27},{4,28},{5,29},{6,30},{7,31},{8,16},{9,... | collective-permute-start | bytes 49160 | tf_op jit(solution)/shard_map/ppermute | solution.py:72
  29.3 0.2 collective-permute-start.14
  29.4 2.8 %collective-permute-start.13 = (f32[32,128]{1,0:T(8,128)S(1)}, f32[32,128]{1,0:T(8,128)S(1)}, u32[]{:S(2)}, u32[]{:S(2)}) collective-permute-start(f32[32,128]{1,0:T(8,128)S(1)} %get-tuple-element.96.refs_8_), channel_id=1, source_target_pairs={{0,1},{1,0},{2,3},{3,2},{4,5},{5,4},{6,7},{7,6},{8,9},{9,8},{10,11... | collective-permute-start | bytes 49160 | tf_op jit(solution)/shard_map/ppermute | solution.py:72
  32.2 1.4 %third_inner.1 = (f32[1024,128]{1,0:T(8,128)S(1)}, f32[2,16,128]{2,1,0:T(8,128)S(1)}, f32[2,64,128]{2,1,0:T(8,128)S(1)}) custom-call(f32[1024,128]{1,0:T(8,128)S(1)} %get-tuple-element.70.refs_0_, f32[1024,128]{1,0:T(8,128)S(1)} %get-tuple-element.62.refs_3_.refs_2_.refs_1_, ...), custom_call_target="tpu_custom_call", output_to_operand_aliasing={{0}: (5, {})} | custom-call | flops 13107200 | bytes 3145728 | tf_op jit(solution)/shard_map/third_inner/pallas_call | solution.py:568
  33.6 0.3 collective-permute-done.13.refs_12_
  33.9 0.4 %all-to-all-done = f32[32,1,128]{2,1,0:T(1,128)S(1)} async-done(((f32[32,1,128]{2,1,0:T(1,128)}), f32[32,1,128]{2,1,0:T(1,128)S(1)}, u32[]{:S(2)}, u32[]{:S(2)}) %all-to-all-start) | async-done | bytes 16416 | tf_op jit(solution)/shard_map/all_to_all | solution.py:645
  34.3 1.1 %finish.1 = (f32[1024,128]{1,0:T(8,128)}, f32[1,1]{1,0:T(1,128)}, f32[1,1]{1,0:T(1,128)}) custom-call(f32[1024,128]{1,0:T(8,128)S(1)} %get-tuple-element.58.refs_2_.refs_4_.refs_0_, f32[1024,128]{1,0:T(8,128)S(1)} %get-tuple-element.89.refs_1_, f32[32,128]{1,0:T(8,128)S(1)} %bitcast.16, f32[2,16,128]{2,1,0:T(8,128)S(1)} %get-tuple-element.91.refs_3_, ...), custom_call_target="tpu_custom_call" | custom-call | bytes 1384448 | tf_op jit(solution)/shard_map/finish/pallas_call | solution.py:568
  (19 shorter events, 0.0 us)
Async XLA Ops:
  0.6 10.7 %copy-start = (f32[64,16,128]{2,1,0:T(8,128)S(1)}, f32[64,16,128]{2,1,0:T(8,128)}, u32[]{:S(2)}) copy-start(f32[64,16,128]{2,1,0:T(8,128)} %param.8) | copy-start | bytes 1572868
  3.6 14.2 %copy-start.1 = (bf16[2,64,16,128]{3,2,1,0:T(8,128)(2,1)S(1)}, bf16[2,64,16,128]{3,2,1,0:T(8,128)(2,1)}, u32[]{:S(2)}) copy-start(bf16[2,64,16,128]{3,2,1,0:T(8,128)(2,1)} %param.9) | copy-start | bytes 1572868
  3.6 9.6 %collective-permute-start.2 = (f32[192,128]{1,0:T(8,128)S(1)}, f32[192,128]{1,0:T(8,128)S(1)}, u32[]{:S(2)}, u32[]{:S(2)}) collective-permute-start(f32[192,128]{1,0:T(8,128)S(1)} %get-tuple-element.69), channel_id=1, source_target_pairs={{0,4},{1,5},{2,6},{3,7},{4,0},{5,1},{6,2},{7,3},{8,12},{9,13},{10,... | collective-permute-start | bytes 294920 | tf_op jit(solution)/shard_map/ppermute | solution.py:72
  6.6 6.4 %collective-permute-start = (f32[48,128]{1,0:T(8,128)S(1)}, f32[48,128]{1,0:T(8,128)S(1)}, u32[]{:S(2)}, u32[]{:S(2)}) collective-permute-start(f32[48,128]{1,0:T(8,128)S(1)} %get-tuple-element.67), channel_id=1, source_target_pairs={{0,8},{1,9},{2,10},{3,11},{4,12},{5,13},{6,14},{7,15},{8,0},{9,1},... | collective-permute-start | bytes 73736 | tf_op jit(solution)/shard_map/ppermute | solution.py:72
  6.6 6.4 %collective-permute-start.1 = (f32[48,128]{1,0:T(8,128)S(1)}, f32[48,128]{1,0:T(8,128)S(1)}, u32[]{:S(2)}, u32[]{:S(2)}) collective-permute-start(f32[48,128]{1,0:T(8,128)S(1)} %get-tuple-element.68), channel_id=1, source_target_pairs={{0,24},{1,25},{2,26},{3,27},{4,28},{5,29},{6,30},{7,31},{8,16},{9,... | collective-permute-start | bytes 73736 | tf_op jit(solution)/shard_map/ppermute | solution.py:72
  8.2 4.8 %collective-permute-start.4 = (f32[48,128]{1,0:T(8,128)S(1)}, f32[48,128]{1,0:T(8,128)S(1)}, u32[]{:S(2)}, u32[]{:S(2)}) collective-permute-start(f32[48,128]{1,0:T(8,128)S(1)} %get-tuple-element.66.refs_7_), channel_id=1, source_target_pairs={{0,8},{1,2},{2,1},{3,11},{4,12},{5,6},{6,5},{7,15},{8,0},{9,10},{1... | collective-permute-start | bytes 73736 | tf_op jit(solution)/shard_map/ppermute | solution.py:72
  8.2 5.0 %collective-permute-start.3 = (f32[48,128]{1,0:T(8,128)S(1)}, f32[48,128]{1,0:T(8,128)S(1)}, u32[]{:S(2)}, u32[]{:S(2)}) collective-permute-start(f32[48,128]{1,0:T(8,128)S(1)} %get-tuple-element.66.refs_7_), channel_id=1, source_target_pairs={{0,1},{1,0},{2,3},{3,2},{4,5},{5,4},{6,7},{7,6},{8,9},{9,8},{10,11... | collective-permute-start | bytes 73736 | tf_op jit(solution)/shard_map/ppermute | solution.py:72
  14.0 5.9 %collective-permute-start.7 = (f32[256,128]{1,0:T(8,128)S(1)}, f32[256,128]{1,0:T(8,128)S(1)}, u32[]{:S(2)}, u32[]{:S(2)}) collective-permute-start(f32[256,128]{1,0:T(8,128)S(1)} %get-tuple-element.85), channel_id=1, source_target_pairs={{0,4},{1,5},{2,6},{3,7},{4,0},{5,1},{6,2},{7,3},{8,12},{9,13},{10,... | collective-permute-start | bytes 393224 | tf_op jit(solution)/shard_map/ppermute | solution.py:72
  14.6 5.2 %collective-permute-start.5 = (f32[64,128]{1,0:T(8,128)S(1)}, f32[64,128]{1,0:T(8,128)S(1)}, u32[]{:S(2)}, u32[]{:S(2)}) collective-permute-start(f32[64,128]{1,0:T(8,128)S(1)} %get-tuple-element.83), channel_id=1, source_target_pairs={{0,8},{1,9},{2,10},{3,11},{4,12},{5,13},{6,14},{7,15},{8,0},{9,1},... | collective-permute-start | bytes 98312 | tf_op jit(solution)/shard_map/ppermute | solution.py:72
  14.6 5.2 %collective-permute-start.6 = (f32[64,128]{1,0:T(8,128)S(1)}, f32[64,128]{1,0:T(8,128)S(1)}, u32[]{:S(2)}, u32[]{:S(2)}) collective-permute-start(f32[64,128]{1,0:T(8,128)S(1)} %get-tuple-element.84), channel_id=1, source_target_pairs={{0,24},{1,25},{2,26},{3,27},{4,28},{5,29},{6,30},{7,31},{8,16},{9,... | collective-permute-start | bytes 98312 | tf_op jit(solution)/shard_map/ppermute | solution.py:72
  15.3 4.6 %collective-permute-start.9 = (f32[64,128]{1,0:T(8,128)S(1)}, f32[64,128]{1,0:T(8,128)S(1)}, u32[]{:S(2)}, u32[]{:S(2)}) collective-permute-start(f32[64,128]{1,0:T(8,128)S(1)} %get-tuple-element.82.refs_12_), channel_id=1, source_target_pairs={{0,8},{1,2},{2,1},{3,11},{4,12},{5,6},{6,5},{7,15},{8,0},{9,10},{1... | collective-permute-start | bytes 98312 | tf_op jit(solution)/shard_map/ppermute | solution.py:72
  15.3 4.6 %collective-permute-start.8 = (f32[64,128]{1,0:T(8,128)S(1)}, f32[64,128]{1,0:T(8,128)S(1)}, u32[]{:S(2)}, u32[]{:S(2)}) collective-permute-start(f32[64,128]{1,0:T(8,128)S(1)} %get-tuple-element.82.refs_12_), channel_id=1, source_target_pairs={{0,1},{1,0},{2,3},{3,2},{4,5},{5,4},{6,7},{7,6},{8,9},{9,8},{10,11... | collective-permute-start | bytes 98312 | tf_op jit(solution)/shard_map/ppermute | solution.py:72
  21.7 12.6 %collective-permute-start.12 = (f32[128,128]{1,0:T(8,128)S(1)}, f32[128,128]{1,0:T(8,128)S(1)}, u32[]{:S(2)}, u32[]{:S(2)}) collective-permute-start(f32[128,128]{1,0:T(8,128)S(1)} %get-tuple-element.99), channel_id=1, source_target_pairs={{0,4},{1,5},{2,6},{3,7},{4,0},{5,1},{6,2},{7,3},{8,12},{9,13},{10,... | collective-permute-start | bytes 196616 | tf_op jit(solution)/shard_map/ppermute | solution.py:72
  23.2 11.1 %all-to-all-start = ((f32[32,1,128]{2,1,0:T(1,128)}), f32[32,1,128]{2,1,0:T(1,128)S(1)}, u32[]{:S(2)}, u32[]{:S(2)}) async-start(f32[32,1,128]{2,1,0:T(1,128)} %bitcast.6), calls=%async_computation | async-start | bytes 32768 | tf_op jit(solution)/shard_map/all_to_all | solution.py:645
  27.3 6.3 %collective-permute-start.10 = (f32[32,128]{1,0:T(8,128)}, f32[32,128]{1,0:T(8,128)S(1)}, u32[]{:S(2)}, u32[]{:S(2)}) collective-permute-start(f32[32,128]{1,0:T(8,128)} %get-tuple-element.97), channel_id=1, source_target_pairs={{0,8},{1,9},{2,10},{3,11},{4,12},{5,13},{6,14},{7,15},{8,0},{9,1},... | collective-permute-start | bytes 49160 | tf_op jit(solution)/shard_map/ppermute | solution.py:72
  27.6 6.0 %collective-permute-start.11 = (f32[32,128]{1,0:T(8,128)}, f32[32,128]{1,0:T(8,128)S(1)}, u32[]{:S(2)}, u32[]{:S(2)}) collective-permute-start(f32[32,128]{1,0:T(8,128)} %get-tuple-element.98), channel_id=1, source_target_pairs={{0,24},{1,25},{2,26},{3,27},{4,28},{5,29},{6,30},{7,31},{8,16},{9,... | collective-permute-start | bytes 49160 | tf_op jit(solution)/shard_map/ppermute | solution.py:72
  29.3 4.4 %collective-permute-start.14 = (f32[32,128]{1,0:T(8,128)S(1)}, f32[32,128]{1,0:T(8,128)S(1)}, u32[]{:S(2)}, u32[]{:S(2)}) collective-permute-start(f32[32,128]{1,0:T(8,128)S(1)} %get-tuple-element.96.refs_8_), channel_id=1, source_target_pairs={{0,8},{1,2},{2,1},{3,11},{4,12},{5,6},{6,5},{7,15},{8,0},{9,10},{1... | collective-permute-start | bytes 49160 | tf_op jit(solution)/shard_map/ppermute | solution.py:72
  29.4 4.5 %collective-permute-start.13 = (f32[32,128]{1,0:T(8,128)S(1)}, f32[32,128]{1,0:T(8,128)S(1)}, u32[]{:S(2)}, u32[]{:S(2)}) collective-permute-start(f32[32,128]{1,0:T(8,128)S(1)} %get-tuple-element.96.refs_8_), channel_id=1, source_target_pairs={{0,1},{1,0},{2,3},{3,2},{4,5},{5,4},{6,7},{7,6},{8,9},{9,8},{10,11... | collective-permute-start | bytes 49160 | tf_op jit(solution)/shard_map/ppermute | solution.py:72

commit v4 on v3

--- a/solution.py
+++ b/solution.py
@@ -186,7 +186,27 @@
 
 def at_rows(x, ref, f, nx, row, ny):
     part = pl.ds(f * nx + x, 1)
-    return jnp.where(row == 0, ref[0, part, :], jnp.where(row == ny - 1, ref[1, part, :], 0.0))
+    first, last = ref[0, part, :], ref[1, part, :]
+    if ny < 16:
+        return jnp.where(row == 0, first, jnp.where(row == ny - 1, last, 0.0))
+    parts = [jnp.where(row[:8] == 0, first, 0.0), jnp.where(row[:8] == 7, last, 0.0)]
+    if ny > 16:
+        parts.insert(1, jnp.zeros((ny - 16, LANES), F32))
+    return jnp.concatenate(parts, axis=0)
+
+
+def pack_edges(pair_x, pair_y, nx, ny):
+    _, lane = grid_iota(ny)
+    acc = jnp.zeros((ny, LANES), F32)
+    for side, x in ((0, 0), (1, nx - 1)):
+        acc = acc + pack_z(jnp.zeros_like(acc), pair_x[side], x, lane)
+    x, lane = grid_iota(nx)
+    row, _ = grid_iota(ny)
+    for side, y in ((0, 0), (1, ny - 1)):
+        moved = pltpu.roll(pair_y[side], 1, 1, stride=2, stride_axis=0)
+        line = jnp.sum(jnp.where(lane // 2 == x, moved, 0.0), axis=0, keepdims=True)
+        acc = acc + jnp.where(row == y, line, 0.0)
+    return acc
 
 
 def ready_z(value):
@@ -279,11 +299,11 @@
 def first_inner_kernel(dims, unroll, *refs):
     nx, ny = dims
     t_ref, s_ref, k_ref, l_ref, m_ref, g_ref = refs[:6]
-    t1, s1, h0, k1, l1, w0, v0, kpack = refs[6:]
+    t1, s1, h0, k1, l1, w0, v0, packs = refs[6:]
     row, lane = grid_iota(ny)
 
     def plane(x, carry):
-        t, s, k, s_prev, flux_prev, acc = carry
+        t, s, k, s_prev, flux_prev, accs = carry
         here = pl.ds(x * ny, ny)
         then = pl.ds(jnp.minimum(x + 1, nx - 1) * ny, ny)
         tn, sn, kn = t_ref[then, :], s_ref[then, :], k_ref[then, :]
@@ -299,24 +319,25 @@
         soft, _ = softplus_parts(SOLIDIFY_POINT - LOWERING_COEF * s - t)
         w, v = soft * l, soft * m
         frost = g * w
-        t1[here, :] = t + WARMTH_ADVANCE * heat + HIDDEN_WARMTH * frost
-        s1[here, :] = s + STEP_SOLUTE * diff + REJECT * frost
-        h0[here, :] = heat
+        new_t = t + WARMTH_ADVANCE * heat + HIDDEN_WARMTH * frost
+        new_s = s + STEP_SOLUTE * diff + REJECT * frost
         new_k = k + frost
-        k1[here, :] = new_k
+        t1[here, :], s1[here, :], h0[here, :], k1[here, :] = new_t, new_s, heat, new_k
         l1[here, :], w0[here, :], v0[here, :] = l + g * v, w, v
-        return tn, sn, kn, s, flux, pack_z(acc, new_k, x, lane)
+        accs = tuple(pack_z(a, z, x, lane) for a, z in zip(accs, (new_t, new_s, new_k, heat)))
+        return tn, sn, kn, s, flux, accs
 
     top = pl.ds(0, ny)
     zero = jnp.zeros((ny, LANES), F32)
-    carry = (t_ref[top, :], s_ref[top, :], k_ref[top, :], zero, zero, zero)
-    kpack[...] = lax.fori_loop(0, nx, plane, carry, unroll=unroll)[-1]
+    carry = (t_ref[top, :], s_ref[top, :], k_ref[top, :], zero, zero, (zero,) * 4)
+    for f, acc in enumerate(lax.fori_loop(0, nx, plane, carry, unroll=unroll)[-1]):
+        packs[pl.ds(f * ny, ny), :] = acc
 
 
 def first_edge_kernel(dims, counts, unroll, *refs):
     nx, ny = dims
     ngot = sum(swaps(n) for n in counts)
-    tp_ref, sp_ref, hp_ref, k1_ref, kpack_ref = refs[:5]
+    tp_ref, sp_ref, hp_ref, k1_ref, packs_ref = refs[:5]
     faces = Faces(dims, counts, refs[5:8], refs[8 : 8 + ngot])
     t1, s1, h0 = refs[8 + ngot : 11 + ngot]
     own = Own(dims, counts, refs[11 + ngot : -1])
@@ -339,7 +360,7 @@
     heat_z, sugar_z = flux_in(2)
     in_heat, in_sugar = ready_z(heat_z), ready_z(sugar_z)
 
-    def plane(x, accs):
+    def plane(x, _):
         here = pl.ds(x * ny, ny)
         heat = at_plane(x, nx, heat_x) + at_rows(x, rows_ref, 0, nx, row, ny)
         diff = at_plane(x, nx, sugar_x) + at_rows(x, rows_ref, 1, nx, row, ny)
@@ -354,24 +375,22 @@
         t1[here, :], s1[here, :], h0[here, :] = new_t, new_s, new_h
         for f, v in enumerate((new_t, new_s, k1_ref[here, :], new_h)):
             own.rows(f, x, v)
-        return tuple(pack_z(a, v, x, lane) for a, v in zip(accs, (some_t, some_s, some_h)))
-
-    accs = tuple(jnp.zeros((ny, LANES), F32) for _ in range(3))
-    accs = lax.fori_loop(0, nx, plane, accs, unroll=unroll)
-    heat_z, sugar_z = turn_z(heat_z), turn_z(sugar_z)
-    packs = (
-        accs[0] + WARMTH_ADVANCE * heat_z,
-        accs[1] + STEP_SOLUTE * sugar_z,
-        kpack_ref[...],
-        accs[2] + heat_z,
-    )
+        return 0
+
+    lax.fori_loop(0, nx, plane, 0, unroll=unroll)
+    heat = turn_z(heat_z) + pack_edges(heat_x, heat_y, nx, ny)
+    sugar = turn_z(sugar_z) + pack_edges(sugar_x, sugar_y, nx, ny)
+    packs = [packs_ref[pl.ds(f * ny, ny), :] for f in range(4)]
+    packs[0] = packs[0] + WARMTH_ADVANCE * heat
+    packs[1] = packs[1] + STEP_SOLUTE * sugar
+    packs[3] = packs[3] + heat
     own.finish((t1, s1, k1_ref, h0), packs)
 
 
 def second_inner_kernel(dims, unroll, *refs):
     nx, ny = dims
-    t_ref, s_ref, k_ref, h_ref, l_ref, g_ref, r_ref = refs[:7]
-    mt_ref, ms_ref, inner_ref, soft_ref, slope_ref = refs[7:]
+    t_ref, s_ref, k_ref, h_ref, l_ref, w_ref, v_ref, g_ref, r_ref = refs[:9]
+    mt_ref, ms_ref, by_pull_ref, with_miss_ref, with_pull_ref = refs[9:]
     row, lane = grid_iota(ny)
 
     def plane(x, carry):
@@ -396,8 +415,12 @@
             t + WARMTH_ADVANCE * heat + HIDDEN_WARMTH * frost - r_ref[0, here, :].astype(F32)
         )
         ms_ref[here, :] = s + STEP_SOLUTE * diff + REJECT * frost - r_ref[1, here, :].astype(F32)
-        inner_ref[here, :] = heat + WARMTH_ADVANCE * again
-        soft_ref[here, :], slope_ref[here, :] = soft, slope
+        below = g * l * slope
+        by_pull_ref[here, :] = soft * (l + g * v_ref[here, :]) + w_ref[here, :] * (
+            1.0 - (HIDDEN_WARMTH + REJECT * LOWERING_COEF) * below
+        )
+        with_miss_ref[here, :] = heat + WARMTH_ADVANCE * again + h
+        with_pull_ref[here, :] = below * h
         return tn, sn, kn, hn, s, flux, other
 
     top = pl.ds(0, ny)
@@ -409,12 +432,11 @@
 def second_edge_kernel(dims, counts, unroll, *refs):
     nx, ny = dims
     ngot = sum(swaps(n) for n in counts)
-    h_ref, l_ref, w_ref, v_ref, g_ref = refs[:5]
-    mtp_ref, msp_ref, inner_ref, soft_ref, slope_ref = refs[5:10]
-    faces = Faces(dims, counts, refs[10:13], refs[13 : 13 + ngot])
-    mt_ref, ms_ref, sense_ref, sums_ref = refs[13 + ngot : 17 + ngot]
-    meet = refs[17 + ngot : 20 + ngot]
-    own = Own(dims, counts, refs[20 + ngot : -3], refs[-2:])
+    mtp_ref, msp_ref, with_miss_ref, with_pull_ref = refs[:4]
+    faces = Faces(dims, counts, refs[4:7], refs[7 : 7 + ngot])
+    mt_ref, ms_ref, sums_ref = refs[7 + ngot : 10 + ngot]
+    meet = refs[10 + ngot : 13 + ngot]
+    own = Own(dims, counts, refs[13 + ngot : -3], refs[-2:])
     rows_ref = refs[-3]
     row, lane = grid_iota(ny)
     edge = (lane == 0) | (lane == LANES - 1)
@@ -431,9 +453,10 @@
         return heat, sn, [half_flux(*v) for v in zip(ko, ho, kn, hn)]
 
     heat_x, sugar_x, again_x = flux_in(0)
-    for f, pair in enumerate(flux_in(1)):
-        for side in (0, 1):
-            rows_ref[side, pl.ds(f * nx, nx), :] = pair[side]
+    heat_y, sugar_y, again_y = flux_in(1)
+    for side in (0, 1):
+        rows_ref[side, pl.ds(0, nx), :] = heat_y[side]
+        rows_ref[side, pl.ds(nx, nx), :] = sugar_y[side]
     heat_z, sugar_z, again_z = flux_in(2)
     in_heat, in_sugar = ready_z(heat_z), ready_z(sugar_z)
 
@@ -444,25 +467,14 @@
         diff = at_plane(x, nx, sugar_x) + at_rows(x, rows_ref, 1, nx, row, ny)
         some_t = mtp_ref[here, :] + WARMTH_ADVANCE * heat
         some_s = msp_ref[here, :] + STEP_SOLUTE * diff
-        heat_in = jnp.where(edge, unpack_z(in_heat, x), 0.0)
+        heat = jnp.where(edge, unpack_z(in_heat, x), 0.0)
         diff = jnp.where(edge, unpack_z(in_sugar, x), 0.0)
-        heat = heat + heat_in
-        again = at_plane(x, nx, again_x) + at_rows(x, rows_ref, 2, nx, row, ny)
-        mt = some_t + WARMTH_ADVANCE * heat_in
+        mt = some_t + WARMTH_ADVANCE * heat
         ms = some_s + STEP_SOLUTE * diff
-        h, l, soft, g = h_ref[here, :], l_ref[here, :], soft_ref[here, :], g_ref[here, :]
+        mt_ref[here, :], ms_ref[here, :] = mt, ms
+        misfit = misfit + (mt * mt + ms * ms)
         pull = HIDDEN_WARMTH * mt + REJECT * ms
-        by_speed = pull * l
-        below = by_speed * g * slope_ref[here, :]
-        part_t = mt - below
-        pull_0 = HIDDEN_WARMTH * part_t + REJECT * (ms - LOWERING_COEF * below)
-        mt_ref[here, :], ms_ref[here, :] = mt, ms
-        sense_ref[here, :] = (
-            by_speed * soft + pull_0 * w_ref[here, :] + g * soft * pull * v_ref[here, :]
-        )
-        misfit = misfit + (mt * mt + ms * ms)
-        inner = inner_ref[here, :] + heat + WARMTH_ADVANCE * again
-        part = part + (mt * inner + part_t * h)
+        part = part + (mt * with_miss_ref[here, :] - pull * with_pull_ref[here, :])
         for f, v in enumerate((mt, ms)):
             own.rows(f, x, v)
         accs = tuple(pack_z(a, z, x, lane) for a, z in zip(accs, (some_t, some_s)))
@@ -477,7 +489,16 @@
         accs[1] + STEP_SOLUTE * turn_z(sugar_z),
     )
     own.finish((mt_ref, ms_ref), packs)
-    part = part + WARMTH_ADVANCE * turn_z(packs[0]) * again_z
+    part = part + turn_z(packs[0]) * (heat_z + WARMTH_ADVANCE * again_z)
+    rows = None
+    for side in (0, 1):
+        part = part + own.x[side, pl.ds(0, ny), :] * (
+            heat_x[side] + WARMTH_ADVANCE * again_x[side]
+        )
+        line = own.y[side, pl.ds(0, nx), :] * (heat_y[side] + WARMTH_ADVANCE * again_y[side])
+        rows = line if rows is None else rows + line
+    for first in range(0, nx, ny):
+        part = part + rows[first : first + ny]
     lane_row = lax.broadcasted_iota(jnp.int32, (1, LANES), 1)
     line = jnp.where(lane_row == 0, 0.5 * jnp.sum(misfit), 0.0)
     line = jnp.where(lane_row == 1, WARMTH_ADVANCE * jnp.sum(part), line)
@@ -494,7 +515,7 @@
 
 def third_inner_kernel(dims, unroll, *refs):
     nx, ny = dims
-    t_ref, k_ref, mt_ref, ms_ref, w_ref, sense_ref = refs[:6]
+    t_ref, k_ref, mt_ref, ms_ref, w_ref, by_pull_ref = refs[:6]
     out_ref, x_ref, y_ref = refs[6:]
     row, lane = grid_iota(ny)
     x_ref[0], x_ref[1] = mt_ref[pl.ds(0, ny), :], mt_ref[pl.ds((nx - 1) * ny, ny), :]
@@ -515,7 +536,8 @@
             down = crossing(ka, ta, mta, k, t, mt, ms)
             total = total + jnp.where(index == size - 1, 0.0, up)
             total = total + jnp.where(index == 0, 0.0, pltpu.roll(down, 1, axis))
-        out_ref[here, :] = sense_ref[here, :] + w_ref[here, :] * total
+        pull = HIDDEN_WARMTH * mt + REJECT * ms
+        out_ref[here, :] = by_pull_ref[here, :] * pull + w_ref[here, :] * total
         return tn, kn, mtn, msn, to_next
 
     top = pl.ds(0, ny)
@@ -523,13 +545,13 @@
     lax.fori_loop(0, nx, plane, (*start, jnp.zeros((ny, LANES), F32)), unroll=unroll)
 
 
-def finish_kernel(dims, counts, cells, unroll, *refs):
+def finish_kernel(dims, counts, unroll, *refs):
     nx, ny = dims
     ngot = sum(swaps(n) for n in counts)
-    w_ref, sense_ref, sums_ref = refs[:3]
-    meet = refs[3:6]
-    faces = Faces(dims, counts, refs[6:9], refs[9 : 9 + ngot])
-    out_ref, misfit_ref, gradient_ref, rows_ref = refs[9 + ngot :]
+    w_ref, sense_ref = refs[:2]
+    meet = refs[2:5]
+    faces = Faces(dims, counts, refs[5:8], refs[8 : 8 + ngot])
+    out_ref, rows_ref = refs[8 + ngot :]
     row, lane = grid_iota(ny)
     edge = (lane == 0) | (lane == LANES - 1)
 
@@ -553,6 +575,9 @@
         return 0
 
     lax.fori_loop(0, nx, plane, 0, unroll=unroll)
+
+
+def totals_kernel(cells, sums_ref, misfit_ref, gradient_ref):
     sums = sums_ref[...]
     which = lax.broadcasted_iota(jnp.int32, sums.shape, 1)
     misfit_ref[0, 0] = jnp.sum(jnp.where(which == 0, sums, 0.0)) / cells
@@ -604,8 +629,8 @@
     k, l, m, t, s = res[:5]
     own = res[5:]
     got = send_faces(own, counts)
-    pack = ((ny, nz), F32)
-    tp, sp, hp, k1, l1, w, v, kpack = call(
+    pack = ((4 * ny, nz), F32)
+    tp, sp, hp, k1, l1, w, v, packs = call(
         functools.partial(first_inner_kernel, dims, 8),
         [field] * 7 + [pack],
         (t, s, k, l, m, g),
@@ -615,17 +640,17 @@
     res = call(
         functools.partial(first_edge_kernel, dims, counts, 64),
         [field] * 3 + own_shapes(dims, counts, 4),
-        (tp, sp, hp, k1, kpack, *own[:3], *got),
+        (tp, sp, hp, k1, packs, *own[:3], *got),
         "first_edge",
         [pltpu.VMEM((2, 2 * nx, nz), F32)],
     )
     t1, s1, h0 = res[:3]
     own1 = res[3:]
     got1 = send_faces(own1, counts)
-    inner = call(
+    mtp, msp, by_pull, *inner = call(
         functools.partial(second_inner_kernel, dims, 8),
         [field] * 5,
-        (t1, s1, k1, h0, l1, g, r),
+        (t1, s1, k1, h0, l1, w, v, g, r),
         "second_inner",
         flops=work,
     )
@@ -634,30 +659,38 @@
     meet_shapes = own_shapes(dims, counts, 1)[:3]
     res = call(
         functools.partial(second_edge_kernel, dims, counts, 64),
-        [field] * 3 + [line] + meet_shapes + own_shapes(dims, counts, 2)[2:],
-        (h0, l1, w, v, g, *inner, *own1[:3], *got1),
+        [field] * 2 + [line] + meet_shapes + own_shapes(dims, counts, 2)[2:],
+        (mtp, msp, *inner, *own1[:3], *got1),
         "second_edge",
-        [pltpu.VMEM(v, F32) for v in ((2, 3 * nx, nz), (2, 2 * ny, nz), (2, 2 * nx, nz))],
-    )
-    mt, ms, sense, sums = res[:4]
-    meet, sent = res[4:7], res[7:]
+        [pltpu.VMEM(v, F32) for v in ((2, 2 * nx, nz), (2, 2 * ny, nz), (2, 2 * nx, nz))],
+    )
+    mt, ms, sums = res[:3]
+    meet, sent = res[3:6], res[6:]
     got2 = send_faces((None, None, *sent), counts)
     sums = lax.all_to_all(sums, AXES, 0, 0, tiled=True)
     sense, *kept = call(
         functools.partial(third_inner_kernel, dims, 16),
         [field] + meet_shapes[:2],
-        (t1, k1, mt, ms, w, sense),
+        (t1, k1, mt, ms, w, by_pull),
         "third_inner",
         aliases={5: 0},
         flops=work,
     )
-    sens, misfit, gradient = call(
-        functools.partial(finish_kernel, dims, counts, float(cells * nz * devices), 64),
-        [field, ((1, 1), F32), ((1, 1), F32)],
-        (w, sense, sums, *meet, *kept, sent[0], *got2),
+    (sens,) = call(
+        functools.partial(finish_kernel, dims, counts, 64),
+        [field],
+        (w, sense, *meet, *kept, sent[0], *got2),
         "finish",
         [pltpu.VMEM((2, nx, nz), F32)],
-        out_specs=[VM, SM, SM],
+        flops=work,
+    )
+    sums, sens = lax.optimization_barrier((sums, sens))
+    misfit, gradient = call(
+        functools.partial(totals_kernel, float(cells * nz * devices)),
+        [((1, 1), F32), ((1, 1), F32)],
+        (sums,),
+        "totals",
+        out_specs=[SM, SM],
     )
     return sens.reshape(nx, ny, nz), misfit.reshape(()), gradient.reshape(())
 

time: 35.7 us -> 33.5 us (0.938)
  starting transfers between devices: 21.9 us -> 18.4 us
  Pallas kernels: 11.8 us -> 13.1 us
    ppermute x15, starting transfers between devices: 17.9 us -> 15.5 us  [exchange(): lax.ppermute(p, AXES, swap_pairs(counts, axis, kind))]
    pallas_call x7 -> x8, Pallas kernels: 11.8 us -> 13.1 us  [call(): pl.pallas_call(kernel, out_shape=[jax.ShapeDtypeStruct(s, d) for s, d in...]
    all_to_all x1, starting transfers between devices: 4.07 us -> 2.89 us  [per_device(): sums = lax.all_to_all(sums, AXES, 0, 0, tiled=True)]
  transfers between devices with their start and end apart: 16 -> 16, of which waited for: 3 -> 2; matrix products, arithmetic and copies ran while one was open for 0% -> 0% of each run, Pallas kernels for 14% -> 22%
where the time goes in v4:
time: 33.5 us; the launch traced here: 33.4 us
  starting transfers between devices  18.4 us (55%)
  Pallas kernels  13.1 us (39%)
  waiting for transfers between devices  1.07 us (3%)
  between operations  0.8 us (2%)
    ppermute x15, starting transfers between devices, exchange(): lax.ppermute(p, AXES, swap_pairs(counts, axis, kind))  15.5 us
    pallas_call x8, Pallas kernels, call(): pl.pallas_call(kernel, out_shape=[jax.ShapeDtypeStruct(s, d) for s, d in...  13.1 us
    all_to_all x1, starting transfers between devices, per_device(): sums = lax.all_to_all(sums, AXES, 0, 0, tiled=True)  2.89 us
    ppermute x15, waiting for transfers between devices, exchange(): lax.ppermute(p, AXES, swap_pairs(counts, axis, kind))  0.79 us
  transfers between devices with their start and end apart: 16, of which 2 were waited for; matrix products, arithmetic and copies ran while one was open for 0% of the time, Pallas kernels for 22%

profile of v4, /device:TPU:0, one launch (start us, length us, event | category | flops | bytes accessed | tf_op | source)
XLA Modules:
  0.0 33.4 jit_solution(13138753655442566926)
XLA Ops:
  0.6 2.9 %prepare.1 = (f32[1024,128]{1,0:T(8,128)S(1)}, f32[1024,128]{1,0:T(8,128)S(1)}, f32[1024,128]{1,0:T(8,128)S(1)}, f32[1024,128]{1,0:T(8,128)S(1)}, f32[1024,128]{...) custom-call(f32[8,1024,128]{2,1,0:T(8,128)} %bitcast.16, ...), custom_call_target="tpu_custom_call" | custom-call | bytes 5242880 | tf_op jit(solution)/shard_map/prepare/pallas_call | solution.py:593
  3.6 0.0 copy-start.1
  3.6 3.0 %collective-permute-start.2 = (f32[192,128]{1,0:T(8,128)S(1)}, f32[192,128]{1,0:T(8,128)S(1)}, u32[]{:S(2)}, u32[]{:S(2)}) collective-permute-start(f32[192,128]{1,0:T(8,128)S(1)} %get-tuple-element.68), channel_id=1, source_target_pairs={{0,4},{1,5},{2,6},{3,7},{4,0},{5,1},{6,2},{7,3},{8,12},{9,13},{10,... | collective-permute-start | bytes 294920 | tf_op jit(solution)/shard_map/ppermute | solution.py:72
  6.6 1.6 %collective-permute-start.3 = (f32[48,128]{1,0:T(8,128)S(1)}, f32[48,128]{1,0:T(8,128)S(1)}, u32[]{:S(2)}, u32[]{:S(2)}) collective-permute-start(f32[48,128]{1,0:T(8,128)S(1)} %get-tuple-element.65.refs_7_), channel_id=1, source_target_pairs={{0,1},{1,0},{2,3},{3,2},{4,5},{5,4},{6,7},{7,6},{8,9},{9,8},{10,11... | collective-permute-start | bytes 73736 | tf_op jit(solution)/shard_map/ppermute | solution.py:72
  8.2 0.5 %collective-permute-start = (f32[48,128]{1,0:T(8,128)S(1)}, f32[48,128]{1,0:T(8,128)S(1)}, u32[]{:S(2)}, u32[]{:S(2)}) collective-permute-start(f32[48,128]{1,0:T(8,128)S(1)} %get-tuple-element.66), channel_id=1, source_target_pairs={{0,8},{1,9},{2,10},{3,11},{4,12},{5,13},{6,14},{7,15},{8,0},{9,1},... | collective-permute-start | bytes 73736 | tf_op jit(solution)/shard_map/ppermute | solution.py:72
  8.7 1.1 %collective-permute-start.1 = (f32[48,128]{1,0:T(8,128)S(1)}, f32[48,128]{1,0:T(8,128)S(1)}, u32[]{:S(2)}, u32[]{:S(2)}) collective-permute-start(f32[48,128]{1,0:T(8,128)S(1)} %get-tuple-element.67), channel_id=1, source_target_pairs={{0,24},{1,25},{2,26},{3,27},{4,28},{5,29},{6,30},{7,31},{8,16},{9,... | collective-permute-start | bytes 73736 | tf_op jit(solution)/shard_map/ppermute | solution.py:72
  9.8 2.5 %first_inner.1 = (f32[1024,128]{1,0:T(8,128)S(1)}, f32[1024,128]{1,0:T(8,128)S(1)}, f32[1024,128]{1,0:T(8,128)S(1)}, f32[1024,128]{1,0:T(8,128)S(1)}, f32[1024,1...) custom-call(f32[1024,128]{1,0:T(8,128)S(1)} %get-tuple-element.53.refs_0_, ...), custom_call_target="tpu_custom_call" | custom-call | flops 13107200 | bytes 3145728 | tf_op jit(solution)/shard_map/first_inner/pallas_call | solution.py:593
  12.4 0.7 %first_edge.1 = (f32[1024,128]{1,0:T(8,128)S(1)}, f32[1024,128]{1,0:T(8,128)S(1)}, f32[1024,128]{1,0:T(8,128)S(1)}, f32[2,64,128]{2,1,0:T(8,128)S(1)}, f32[2,256...) custom-call(f32[1024,128]{1,0:T(8,128)S(1)} %get-tuple-element.58.re, ...), custom_call_target="tpu_custom_call" | custom-call | bytes 2596864 | tf_op jit(solution)/shard_map/first_edge/pallas_call | solution.py:593
  13.0 0.6 %collective-permute-start.7 = (f32[256,128]{1,0:T(8,128)S(1)}, f32[256,128]{1,0:T(8,128)S(1)}, u32[]{:S(2)}, u32[]{:S(2)}) collective-permute-start(f32[256,128]{1,0:T(8,128)S(1)} %get-tuple-element.84), channel_id=1, source_target_pairs={{0,4},{1,5},{2,6},{3,7},{4,0},{5,1},{6,2},{7,3},{8,12},{9,13},{10,... | collective-permute-start | bytes 393224 | tf_op jit(solution)/shard_map/ppermute | solution.py:72
  13.6 0.2 collective-permute-start.5
  13.9 1.0 %collective-permute-start.6 = (f32[64,128]{1,0:T(8,128)S(1)}, f32[64,128]{1,0:T(8,128)S(1)}, u32[]{:S(2)}, u32[]{:S(2)}) collective-permute-start(f32[64,128]{1,0:T(8,128)S(1)} %get-tuple-element.83), channel_id=1, source_target_pairs={{0,24},{1,25},{2,26},{3,27},{4,28},{5,29},{6,30},{7,31},{8,16},{9,... | collective-permute-start | bytes 98312 | tf_op jit(solution)/shard_map/ppermute | solution.py:72
  14.9 2.6 %collective-permute-start.8 = (f32[64,128]{1,0:T(8,128)S(1)}, f32[64,128]{1,0:T(8,128)S(1)}, u32[]{:S(2)}, u32[]{:S(2)}) collective-permute-start(f32[64,128]{1,0:T(8,128)S(1)} %get-tuple-element.81.refs_6_), channel_id=1, source_target_pairs={{0,1},{1,0},{2,3},{3,2},{4,5},{5,4},{6,7},{7,6},{8,9},{9,8},{10,11... | collective-permute-start | bytes 98312 | tf_op jit(solution)/shard_map/ppermute | solution.py:72
  17.5 2.2 %second_inner.1 = (f32[1024,128]{1,0:T(8,128)S(1)}, f32[1024,128]{1,0:T(8,128)S(1)}, f32[1024,128]{1,0:T(8,128)S(1)}, f32[1024,128]{1,0:T(8,128)S(1)}, f32[1024,128]{1,0:T(8,128)S(1)}) custom-call(f32[1024,128]{1,0:T(8,128)S(1)} %get-tuple-element.69.refs_0_, f32[1024,128]{1,0:T(8,128)S(1)} %get-tuple-element.70.refs_1_, ...), custom_call_target="tpu_custom_call" | custom-call | flops 13107200 | bytes 4718592 | tf_op jit(solution)/shard_map/second_inner/pallas_call | solution.py:593
  19.8 1.4 %second_edge.1 = (f32[1024,128]{1,0:T(8,128)S(1)}, f32[1024,128]{1,0:T(8,128)S(1)}, f32[32,128]{1,0:T(8,128)}, f32[2,16,128]{2,1,0:T(8,128)S(1)}, f32[2,64,128]{...) custom-call(f32[1024,128]{1,0:T(8,128)S(1)} %get-tuple-element.75.re, ...), custom_call_target="tpu_custom_call" | custom-call | bytes 2719744 | tf_op jit(solution)/shard_map/second_edge/pallas_call | solution.py:593
  21.2 1.5 %collective-permute-start.12 = (f32[128,128]{1,0:T(8,128)S(1)}, f32[128,128]{1,0:T(8,128)S(1)}, u32[]{:S(2)}, u32[]{:S(2)}) collective-permute-start(f32[128,128]{1,0:T(8,128)S(1)} %get-tuple-element.98), channel_id=1, source_target_pairs={{0,4},{1,5},{2,6},{3,7},{4,0},{5,1},{6,2},{7,3},{8,12},{9,13},{10,... | collective-permute-start | bytes 196616 | tf_op jit(solution)/shard_map/ppermute | solution.py:72
  22.7 2.9 %all-to-all-start = ((f32[32,1,128]{2,1,0:T(1,128)}), f32[32,1,128]{2,1,0:T(1,128)S(1)}, u32[]{:S(2)}, u32[]{:S(2)}) async-start(f32[32,1,128]{2,1,0:T(1,128)} %bitcast.6), calls=%async_computation | async-start | bytes 32768 | tf_op jit(solution)/shard_map/all_to_all | solution.py:670
  25.6 0.3 collective-permute-start.10
  25.9 1.6 %collective-permute-start.11 = (f32[32,128]{1,0:T(8,128)S(1)}, f32[32,128]{1,0:T(8,128)S(1)}, u32[]{:S(2)}, u32[]{:S(2)}) collective-permute-start(f32[32,128]{1,0:T(8,128)S(1)} %get-tuple-element.97), channel_id=1, source_target_pairs={{0,24},{1,25},{2,26},{3,27},{4,28},{5,29},{6,30},{7,31},{8,16},{9,... | collective-permute-start | bytes 49160 | tf_op jit(solution)/shard_map/ppermute | solution.py:72
  27.5 1.5 %collective-permute-start.13 = (f32[32,128]{1,0:T(8,128)S(1)}, f32[32,128]{1,0:T(8,128)S(1)}, u32[]{:S(2)}, u32[]{:S(2)}) collective-permute-start(f32[32,128]{1,0:T(8,128)S(1)} %get-tuple-element.95.refs_7_), channel_id=1, source_target_pairs={{0,1},{1,0},{2,3},{3,2},{4,5},{5,4},{6,7},{7,6},{8,9},{9,8},{10,11... | collective-permute-start | bytes 49160 | tf_op jit(solution)/shard_map/ppermute | solution.py:72
  29.0 1.5 %third_inner.1 = (f32[1024,128]{1,0:T(8,128)S(1)}, f32[2,16,128]{2,1,0:T(8,128)S(1)}, f32[2,64,128]{2,1,0:T(8,128)S(1)}) custom-call(f32[1024,128]{1,0:T(8,128)S(1)} %get-tuple-element.69.refs_0_, f32[1024,128]{1,0:T(8,128)S(1)} %get-tuple-element.61.refs_3_.refs_2_.refs_1_, ...), custom_call_target="tpu_custom_call", output_to_operand_aliasing={{0}: (5, {})} | custom-call | flops 13107200 | bytes 3145728 | tf_op jit(solution)/shard_map/third_inner/pallas_call | solution.py:593
  30.5 0.8 %collective-permute-done.13.refs_11_ = f32[32,128]{1,0:T(8,128)S(1)} collective-permute-done((f32[32,128]{1,0:T(8,128)S(1)}, f32[32,128]{1,0:T(8,128)S(1)}, u32[]{:S(2)}, u32[]{:S(2)}) %collective-permute-start.13) | collective-permute-done | bytes 16416 | tf_op jit(solution)/shard_map/ppermute | solution.py:72
  31.3 1.1 %finish.1 = f32[1024,128]{1,0:T(8,128)} custom-call(f32[1024,128]{1,0:T(8,128)S(1)} %get-tuple-element.73.refs_5_.refs_4_.refs_0_, f32[1024,128]{1,0:T(8,128)S(1)} %get-tuple-element.89.refs_1_, f32[2,16,128]{2,1,0:T(8,128)S(1)} %get-tuple-element.90.refs_2_, f32[2,64,128]{2,1,0:T(8,128)S(1)} %get-tuple-element.91.refs_3_, ...), custom_call_target="tpu_custom_call" | custom-call | flops 13107200 | bytes 1368064 | tf_op jit(solution)/shard_map/finish/pallas_call | solution.py:593
  32.4 0.3 all-to-all-done
  32.7 0.6 %totals.1 = (f32[1,1]{1,0:T(1,128)}, f32[1,1]{1,0:T(1,128)}) custom-call(f32[32,128]{1,0:T(8,128)S(1)} %bitcast.15), custom_call_target="tpu_custom_call" | custom-call | bytes 16384 | tf_op jit(solution)/shard_map/totals/pallas_call | solution.py:593
  (20 shorter events, 0.1 us)
Async XLA Ops:
  0.6 9.2 %copy-start = (f32[64,16,128]{2,1,0:T(8,128)S(1)}, f32[64,16,128]{2,1,0:T(8,128)}, u32[]{:S(2)}) copy-start(f32[64,16,128]{2,1,0:T(8,128)} %param.8) | copy-start | bytes 1572868
  3.6 13.9 %copy-start.1 = (bf16[2,64,16,128]{3,2,1,0:T(8,128)(2,1)S(1)}, bf16[2,64,16,128]{3,2,1,0:T(8,128)(2,1)}, u32[]{:S(2)}) copy-start(bf16[2,64,16,128]{3,2,1,0:T(8,128)(2,1)} %param.9) | copy-start | bytes 1572868
  3.6 8.8 %collective-permute-start.2 = (f32[192,128]{1,0:T(8,128)S(1)}, f32[192,128]{1,0:T(8,128)S(1)}, u32[]{:S(2)}, u32[]{:S(2)}) collective-permute-start(f32[192,128]{1,0:T(8,128)S(1)} %get-tuple-element.68), channel_id=1, source_target_pairs={{0,4},{1,5},{2,6},{3,7},{4,0},{5,1},{6,2},{7,3},{8,12},{9,13},{10,... | collective-permute-start | bytes 294920 | tf_op jit(solution)/shard_map/ppermute | solution.py:72
  6.6 5.7 %collective-permute-start.3 = (f32[48,128]{1,0:T(8,128)S(1)}, f32[48,128]{1,0:T(8,128)S(1)}, u32[]{:S(2)}, u32[]{:S(2)}) collective-permute-start(f32[48,128]{1,0:T(8,128)S(1)} %get-tuple-element.65.refs_7_), channel_id=1, source_target_pairs={{0,1},{1,0},{2,3},{3,2},{4,5},{5,4},{6,7},{7,6},{8,9},{9,8},{10,11... | collective-permute-start | bytes 73736 | tf_op jit(solution)/shard_map/ppermute | solution.py:72
  8.1 4.2 %collective-permute-start.4 = (f32[48,128]{1,0:T(8,128)S(1)}, f32[48,128]{1,0:T(8,128)S(1)}, u32[]{:S(2)}, u32[]{:S(2)}) collective-permute-start(f32[48,128]{1,0:T(8,128)S(1)} %get-tuple-element.65.refs_7_), channel_id=1, source_target_pairs={{0,8},{1,2},{2,1},{3,11},{4,12},{5,6},{6,5},{7,15},{8,0},{9,10},{1... | collective-permute-start | bytes 73736 | tf_op jit(solution)/shard_map/ppermute | solution.py:72
  8.2 4.2 %collective-permute-start = (f32[48,128]{1,0:T(8,128)S(1)}, f32[48,128]{1,0:T(8,128)S(1)}, u32[]{:S(2)}, u32[]{:S(2)}) collective-permute-start(f32[48,128]{1,0:T(8,128)S(1)} %get-tuple-element.66), channel_id=1, source_target_pairs={{0,8},{1,9},{2,10},{3,11},{4,12},{5,13},{6,14},{7,15},{8,0},{9,1},... | collective-permute-start | bytes 73736 | tf_op jit(solution)/shard_map/ppermute | solution.py:72
  8.7 3.7 %collective-permute-start.1 = (f32[48,128]{1,0:T(8,128)S(1)}, f32[48,128]{1,0:T(8,128)S(1)}, u32[]{:S(2)}, u32[]{:S(2)}) collective-permute-start(f32[48,128]{1,0:T(8,128)S(1)} %get-tuple-element.67), channel_id=1, source_target_pairs={{0,24},{1,25},{2,26},{3,27},{4,28},{5,29},{6,30},{7,31},{8,16},{9,... | collective-permute-start | bytes 73736 | tf_op jit(solution)/shard_map/ppermute | solution.py:72
  13.0 6.7 %collective-permute-start.7 = (f32[256,128]{1,0:T(8,128)S(1)}, f32[256,128]{1,0:T(8,128)S(1)}, u32[]{:S(2)}, u32[]{:S(2)}) collective-permute-start(f32[256,128]{1,0:T(8,128)S(1)} %get-tuple-element.84), channel_id=1, source_target_pairs={{0,4},{1,5},{2,6},{3,7},{4,0},{5,1},{6,2},{7,3},{8,12},{9,13},{10,... | collective-permute-start | bytes 393224 | tf_op jit(solution)/shard_map/ppermute | solution.py:72
  13.6 6.1 %collective-permute-start.5 = (f32[64,128]{1,0:T(8,128)S(1)}, f32[64,128]{1,0:T(8,128)S(1)}, u32[]{:S(2)}, u32[]{:S(2)}) collective-permute-start(f32[64,128]{1,0:T(8,128)S(1)} %get-tuple-element.82), channel_id=1, source_target_pairs={{0,8},{1,9},{2,10},{3,11},{4,12},{5,13},{6,14},{7,15},{8,0},{9,1},... | collective-permute-start | bytes 98312 | tf_op jit(solution)/shard_map/ppermute | solution.py:72
  13.9 5.9 %collective-permute-start.6 = (f32[64,128]{1,0:T(8,128)S(1)}, f32[64,128]{1,0:T(8,128)S(1)}, u32[]{:S(2)}, u32[]{:S(2)}) collective-permute-start(f32[64,128]{1,0:T(8,128)S(1)} %get-tuple-element.83), channel_id=1, source_target_pairs={{0,24},{1,25},{2,26},{3,27},{4,28},{5,29},{6,30},{7,31},{8,16},{9,... | collective-permute-start | bytes 98312 | tf_op jit(solution)/shard_map/ppermute | solution.py:72
  14.9 4.8 %collective-permute-start.8 = (f32[64,128]{1,0:T(8,128)S(1)}, f32[64,128]{1,0:T(8,128)S(1)}, u32[]{:S(2)}, u32[]{:S(2)}) collective-permute-start(f32[64,128]{1,0:T(8,128)S(1)} %get-tuple-element.81.refs_6_), channel_id=1, source_target_pairs={{0,1},{1,0},{2,3},{3,2},{4,5},{5,4},{6,7},{7,6},{8,9},{9,8},{10,11... | collective-permute-start | bytes 98312 | tf_op jit(solution)/shard_map/ppermute | solution.py:72
  17.5 2.3 %collective-permute-start.9 = (f32[64,128]{1,0:T(8,128)S(1)}, f32[64,128]{1,0:T(8,128)S(1)}, u32[]{:S(2)}, u32[]{:S(2)}) collective-permute-start(f32[64,128]{1,0:T(8,128)S(1)} %get-tuple-element.81.refs_6_), channel_id=1, source_target_pairs={{0,8},{1,2},{2,1},{3,11},{4,12},{5,6},{6,5},{7,15},{8,0},{9,10},{1... | collective-permute-start | bytes 98312 | tf_op jit(solution)/shard_map/ppermute | solution.py:72
  21.2 10.1 %collective-permute-start.12 = (f32[128,128]{1,0:T(8,128)S(1)}, f32[128,128]{1,0:T(8,128)S(1)}, u32[]{:S(2)}, u32[]{:S(2)}) collective-permute-start(f32[128,128]{1,0:T(8,128)S(1)} %get-tuple-element.98), channel_id=1, source_target_pairs={{0,4},{1,5},{2,6},{3,7},{4,0},{5,1},{6,2},{7,3},{8,12},{9,13},{10,... | collective-permute-start | bytes 196616 | tf_op jit(solution)/shard_map/ppermute | solution.py:72
  22.7 10.0 %all-to-all-start = ((f32[32,1,128]{2,1,0:T(1,128)}), f32[32,1,128]{2,1,0:T(1,128)S(1)}, u32[]{:S(2)}, u32[]{:S(2)}) async-start(f32[32,1,128]{2,1,0:T(1,128)} %bitcast.6), calls=%async_computation | async-start | bytes 32768 | tf_op jit(solution)/shard_map/all_to_all | solution.py:670
  25.6 4.9 %collective-permute-start.10 = (f32[32,128]{1,0:T(8,128)S(1)}, f32[32,128]{1,0:T(8,128)S(1)}, u32[]{:S(2)}, u32[]{:S(2)}) collective-permute-start(f32[32,128]{1,0:T(8,128)S(1)} %get-tuple-element.96), channel_id=1, source_target_pairs={{0,8},{1,9},{2,10},{3,11},{4,12},{5,13},{6,14},{7,15},{8,0},{9,1},... | collective-permute-start | bytes 49160 | tf_op jit(solution)/shard_map/ppermute | solution.py:72
  25.9 4.6 %collective-permute-start.11 = (f32[32,128]{1,0:T(8,128)S(1)}, f32[32,128]{1,0:T(8,128)S(1)}, u32[]{:S(2)}, u32[]{:S(2)}) collective-permute-start(f32[32,128]{1,0:T(8,128)S(1)} %get-tuple-element.97), channel_id=1, source_target_pairs={{0,24},{1,25},{2,26},{3,27},{4,28},{5,29},{6,30},{7,31},{8,16},{9,... | collective-permute-start | bytes 49160 | tf_op jit(solution)/shard_map/ppermute | solution.py:72
  27.5 3.7 %collective-permute-start.13 = (f32[32,128]{1,0:T(8,128)S(1)}, f32[32,128]{1,0:T(8,128)S(1)}, u32[]{:S(2)}, u32[]{:S(2)}) collective-permute-start(f32[32,128]{1,0:T(8,128)S(1)} %get-tuple-element.95.refs_7_), channel_id=1, source_target_pairs={{0,1},{1,0},{2,3},{3,2},{4,5},{5,4},{6,7},{7,6},{8,9},{9,8},{10,11... | collective-permute-start | bytes 49160 | tf_op jit(solution)/shard_map/ppermute | solution.py:72
  29.0 2.3 %collective-permute-start.14 = (f32[32,128]{1,0:T(8,128)S(1)}, f32[32,128]{1,0:T(8,128)S(1)}, u32[]{:S(2)}, u32[]{:S(2)}) collective-permute-start(f32[32,128]{1,0:T(8,128)S(1)} %get-tuple-element.95.refs_7_), channel_id=1, source_target_pairs={{0,8},{1,2},{2,1},{3,11},{4,12},{5,6},{6,5},{7,15},{8,0},{9,10},{1... | collective-permute-start | bytes 49160 | tf_op jit(solution)/shard_map/ppermute | solution.py:72

commit v5 on v4

--- a/solution.py
+++ b/solution.py
@@ -164,6 +164,11 @@
                 o[...] = v
 
 
+def choose_kernel(counts, rows_ref, *outs):
+    for o, v in zip(outs, Side(AXES[1], counts[1]).outgoing(rows_ref[0], rows_ref[1])):
+        o[...] = v
+
+
 def own_shapes(dims, counts, fields):
     nx, ny = dims
     x, y = (fields * ny, LANES), (fields * nx, LANES)
@@ -222,10 +227,15 @@
     return 0.5 * (k + kn) * (tn - t)
 
 
-def divergence(flux_up, axis, index):
-    size = flux_up.shape[axis]
-    flux_up = jnp.where(index == size - 1, 0.0, flux_up)
-    return flux_up - pltpu.roll(flux_up, 1, axis)
+def behind(value, axis):
+    return pltpu.roll(value, 1, axis)
+
+
+def divergence(k, fields, axis, index):
+    last = index == k.shape[axis] - 1
+    up, down = 0.5 * (k + ahead(k, axis)), 0.5 * (k + behind(k, axis))
+    up, down = jnp.where(last, 0.0, up), jnp.where(index == 0, 0.0, down)
+    return [up * (ahead(v, axis) - v) + down * (behind(v, axis) - v) for v in fields]
 
 
 def ahead(value, axis):
@@ -303,15 +313,14 @@
     row, lane = grid_iota(ny)
 
     def plane(x, carry):
-        t, s, k, s_prev, flux_prev, accs = carry
+        t, s, k, s_prev, flux_prev = carry
         here = pl.ds(x * ny, ny)
         then = pl.ds(jnp.minimum(x + 1, nx - 1) * ny, ny)
         tn, sn, kn = t_ref[then, :], s_ref[then, :], k_ref[then, :]
         flux = half_flux(k, t, kn, tn)
-        heat = (flux - flux_prev) + divergence(
-            half_flux(k, t, ahead(k, 0), ahead(t, 0)), 0, row
-        )
-        heat = heat + divergence(half_flux(k, t, ahead(k, 1), ahead(t, 1)), 1, lane)
+        heat = flux - flux_prev
+        for axis, index in ((0, row), (1, lane)):
+            heat = heat + divergence(k, (t,), axis, index)[0]
         s_next = jnp.where(x == nx - 1, 0.0, sn)
         diff = (s_prev + s_next) + neighbour_sum(s, 0, row)
         diff = diff + neighbour_sum(s, 1, lane) - 6.0 * s
@@ -324,13 +333,19 @@
         new_k = k + frost
         t1[here, :], s1[here, :], h0[here, :], k1[here, :] = new_t, new_s, heat, new_k
         l1[here, :], w0[here, :], v0[here, :] = l + g * v, w, v
-        accs = tuple(pack_z(a, z, x, lane) for a, z in zip(accs, (new_t, new_s, new_k, heat)))
-        return tn, sn, kn, s, flux, accs
+        return tn, sn, kn, s, flux
 
     top = pl.ds(0, ny)
     zero = jnp.zeros((ny, LANES), F32)
-    carry = (t_ref[top, :], s_ref[top, :], k_ref[top, :], zero, zero, (zero,) * 4)
-    for f, acc in enumerate(lax.fori_loop(0, nx, plane, carry, unroll=unroll)[-1]):
+    carry = (t_ref[top, :], s_ref[top, :], k_ref[top, :], zero, zero)
+    lax.fori_loop(0, nx, plane, carry, unroll=unroll)
+    fields = (t1, s1, k1, h0)
+
+    def pack(x, accs):
+        here = pl.ds(x * ny, ny)
+        return tuple(pack_z(a, r[here, :], x, lane) for a, r in zip(accs, fields))
+
+    for f, acc in enumerate(lax.fori_loop(0, nx, pack, (zero,) * 4, unroll=64)):
         packs[pl.ds(f * ny, ny), :] = acc
 
 
@@ -402,9 +417,8 @@
         flux, other = both * (tn - t), both * (hn - h)
         heat, again = flux - flux_prev, other - other_prev
         for axis, index in ((0, row), (1, lane)):
-            both = 0.5 * (k + ahead(k, axis))
-            heat = heat + divergence(both * (ahead(t, axis) - t), axis, index)
-            again = again + divergence(both * (ahead(h, axis) - h), axis, index)
+            more, other_more = divergence(k, (t, h), axis, index)
+            heat, again = heat + more, again + other_more
         s_next = jnp.where(x == nx - 1, 0.0, sn)
         diff = (s_prev + s_next) + neighbour_sum(s, 0, row)
         diff = diff + neighbour_sum(s, 1, lane) - 6.0 * s
@@ -436,8 +450,8 @@
     faces = Faces(dims, counts, refs[4:7], refs[7 : 7 + ngot])
     mt_ref, ms_ref, sums_ref = refs[7 + ngot : 10 + ngot]
     meet = refs[10 + ngot : 13 + ngot]
-    own = Own(dims, counts, refs[13 + ngot : -3], refs[-2:])
-    rows_ref = refs[-3]
+    own = Own(dims, counts, refs[13 + ngot : -3], (refs[-1], refs[-3]))
+    rows_ref = refs[-2]
     row, lane = grid_iota(ny)
     edge = (lane == 0) | (lane == LANES - 1)
 
@@ -657,17 +671,26 @@
     devices = int(np.prod(counts))
     line = ((devices, LANES), F32)
     meet_shapes = own_shapes(dims, counts, 1)[:3]
+    second_own = own_shapes(dims, counts, 2)
+    second_own = second_own[2 : 3 + swaps(counts[0])] + [second_own[1]]
     res = call(
         functools.partial(second_edge_kernel, dims, counts, 64),
-        [field] * 2 + [line] + meet_shapes + own_shapes(dims, counts, 2)[2:],
+        [field] * 2 + [line] + meet_shapes + second_own,
         (mtp, msp, *inner, *own1[:3], *got1),
         "second_edge",
-        [pltpu.VMEM(v, F32) for v in ((2, 2 * nx, nz), (2, 2 * ny, nz), (2, 2 * nx, nz))],
+        [pltpu.VMEM(v, F32) for v in ((2, 2 * nx, nz), (2, 2 * ny, nz))],
     )
     mt, ms, sums = res[:3]
-    meet, sent = res[3:6], res[6:]
+    meet, sent = res[3:6], list(res[6:])
+    sums = lax.all_to_all(sums, AXES, 0, 0, tiled=True)
+    a = swaps(counts[0])
+    sent[1 + a :] = call(
+        functools.partial(choose_kernel, counts),
+        own_shapes(dims, counts, 2)[3 + a :],
+        (sent[1 + a],),
+        "choose",
+    )
     got2 = send_faces((None, None, *sent), counts)
-    sums = lax.all_to_all(sums, AXES, 0, 0, tiled=True)
     sense, *kept = call(
         functools.partial(third_inner_kernel, dims, 16),
         [field] + meet_shapes[:2],

time: 33.5 us -> 33.4 us (level)
  Pallas kernels: 13.1 us -> 12.7 us
    ppermute x15, starting transfers between devices: 15.5 us -> 16 us  [exchange(): lax.ppermute(p, AXES, swap_pairs(counts, axis, kind))]
    pallas_call x8 -> x9, Pallas kernels: 13.1 us -> 12.7 us  [call(): pl.pallas_call(kernel, out_shape=[jax.ShapeDtypeStruct(s, d) for s, d in...]
  transfers between devices with their start and end apart: 16 -> 16, of which waited for: 2 -> 2; matrix products, arithmetic and copies ran while one was open for 0% -> 0% of each run, Pallas kernels for 22% -> 21%
where the time goes in v5:
time: 33.4 us; the launch traced here: 33.2 us
  starting transfers between devices  18.7 us (56%)
  Pallas kernels  12.7 us (38%)
  waiting for transfers between devices  1.07 us (3%)
  between operations  0.8 us (2%)
    ppermute x15, starting transfers between devices, exchange(): lax.ppermute(p, AXES, swap_pairs(counts, axis, kind))  16 us
    pallas_call x9, Pallas kernels, call(): pl.pallas_call(kernel, out_shape=[jax.ShapeDtypeStruct(s, d) for s, d in...  12.7 us
    all_to_all x1, starting transfers between devices, per_device(): sums = lax.all_to_all(sums, AXES, 0, 0, tiled=True)  2.74 us
    ppermute x15, waiting for transfers between devices, exchange(): lax.ppermute(p, AXES, swap_pairs(counts, axis, kind))  0.79 us
  transfers between devices with their start and end apart: 16, of which 2 were waited for; matrix products, arithmetic and copies ran while one was open for 0% of the time, Pallas kernels for 21%

profile of v5, /device:TPU:0, one launch (start us, length us, event | category | flops | bytes accessed | tf_op | source)
XLA Modules:
  0.0 33.2 jit_solution(3582519113788233292)
XLA Ops:
  0.6 2.9 %prepare.1 = (f32[1024,128]{1,0:T(8,128)S(1)}, f32[1024,128]{1,0:T(8,128)S(1)}, f32[1024,128]{1,0:T(8,128)S(1)}, f32[1024,128]{1,0:T(8,128)S(1)}, f32[1024,128]{...) custom-call(f32[8,1024,128]{2,1,0:T(8,128)} %bitcast.16, ...), custom_call_target="tpu_custom_call" | custom-call | bytes 5242880 | tf_op jit(solution)/shard_map/prepare/pallas_call | solution.py:607
  3.6 0.0 copy-start.1
  3.6 3.0 %collective-permute-start.2 = (f32[192,128]{1,0:T(8,128)S(1)}, f32[192,128]{1,0:T(8,128)S(1)}, u32[]{:S(2)}, u32[]{:S(2)}) collective-permute-start(f32[192,128]{1,0:T(8,128)S(1)} %get-tuple-element.68), channel_id=1, source_target_pairs={{0,4},{1,5},{2,6},{3,7},{4,0},{5,1},{6,2},{7,3},{8,12},{9,13},{10,... | collective-permute-start | bytes 294920 | tf_op jit(solution)/shard_map/ppermute | solution.py:72
  6.6 1.6 %collective-permute-start.3 = (f32[48,128]{1,0:T(8,128)S(1)}, f32[48,128]{1,0:T(8,128)S(1)}, u32[]{:S(2)}, u32[]{:S(2)}) collective-permute-start(f32[48,128]{1,0:T(8,128)S(1)} %get-tuple-element.65.refs_7_), channel_id=1, source_target_pairs={{0,1},{1,0},{2,3},{3,2},{4,5},{5,4},{6,7},{7,6},{8,9},{9,8},{10,11... | collective-permute-start | bytes 73736 | tf_op jit(solution)/shard_map/ppermute | solution.py:72
  8.2 0.5 %collective-permute-start = (f32[48,128]{1,0:T(8,128)S(1)}, f32[48,128]{1,0:T(8,128)S(1)}, u32[]{:S(2)}, u32[]{:S(2)}) collective-permute-start(f32[48,128]{1,0:T(8,128)S(1)} %get-tuple-element.66), channel_id=1, source_target_pairs={{0,8},{1,9},{2,10},{3,11},{4,12},{5,13},{6,14},{7,15},{8,0},{9,1},... | collective-permute-start | bytes 73736 | tf_op jit(solution)/shard_map/ppermute | solution.py:72
  8.7 1.1 %collective-permute-start.1 = (f32[48,128]{1,0:T(8,128)S(1)}, f32[48,128]{1,0:T(8,128)S(1)}, u32[]{:S(2)}, u32[]{:S(2)}) collective-permute-start(f32[48,128]{1,0:T(8,128)S(1)} %get-tuple-element.67), channel_id=1, source_target_pairs={{0,24},{1,25},{2,26},{3,27},{4,28},{5,29},{6,30},{7,31},{8,16},{9,... | collective-permute-start | bytes 73736 | tf_op jit(solution)/shard_map/ppermute | solution.py:72
  9.8 2.2 %first_inner.1 = (f32[1024,128]{1,0:T(8,128)S(1)}, f32[1024,128]{1,0:T(8,128)S(1)}, f32[1024,128]{1,0:T(8,128)S(1)}, f32[1024,128]{1,0:T(8,128)S(1)}, f32[1024,1...) custom-call(f32[1024,128]{1,0:T(8,128)S(1)} %get-tuple-element.53.refs_0_, ...), custom_call_target="tpu_custom_call" | custom-call | flops 13107200 | bytes 3145728 | tf_op jit(solution)/shard_map/first_inner/pallas_call | solution.py:607
  12.0 0.7 %first_edge.1 = (f32[1024,128]{1,0:T(8,128)S(1)}, f32[1024,128]{1,0:T(8,128)S(1)}, f32[1024,128]{1,0:T(8,128)S(1)}, f32[2,64,128]{2,1,0:T(8,128)S(1)}, f32[2,256...) custom-call(f32[1024,128]{1,0:T(8,128)S(1)} %get-tuple-element.58.re, ...), custom_call_target="tpu_custom_call" | custom-call | bytes 2596864 | tf_op jit(solution)/shard_map/first_edge/pallas_call | solution.py:607
  12.7 0.6 %collective-permute-start.7 = (f32[256,128]{1,0:T(8,128)S(1)}, f32[256,128]{1,0:T(8,128)S(1)}, u32[]{:S(2)}, u32[]{:S(2)}) collective-permute-start(f32[256,128]{1,0:T(8,128)S(1)} %get-tuple-element.84), channel_id=1, source_target_pairs={{0,4},{1,5},{2,6},{3,7},{4,0},{5,1},{6,2},{7,3},{8,12},{9,13},{10,... | collective-permute-start | bytes 393224 | tf_op jit(solution)/shard_map/ppermute | solution.py:72
  13.3 0.2 collective-permute-start.5
  13.5 1.4 %collective-permute-start.6 = (f32[64,128]{1,0:T(8,128)S(1)}, f32[64,128]{1,0:T(8,128)S(1)}, u32[]{:S(2)}, u32[]{:S(2)}) collective-permute-start(f32[64,128]{1,0:T(8,128)S(1)} %get-tuple-element.83), channel_id=1, source_target_pairs={{0,24},{1,25},{2,26},{3,27},{4,28},{5,29},{6,30},{7,31},{8,16},{9,... | collective-permute-start | bytes 98312 | tf_op jit(solution)/shard_map/ppermute | solution.py:72
  14.9 2.6 %collective-permute-start.8 = (f32[64,128]{1,0:T(8,128)S(1)}, f32[64,128]{1,0:T(8,128)S(1)}, u32[]{:S(2)}, u32[]{:S(2)}) collective-permute-start(f32[64,128]{1,0:T(8,128)S(1)} %get-tuple-element.81.refs_6_), channel_id=1, source_target_pairs={{0,1},{1,0},{2,3},{3,2},{4,5},{5,4},{6,7},{7,6},{8,9},{9,8},{10,11... | collective-permute-start | bytes 98312 | tf_op jit(solution)/shard_map/ppermute | solution.py:72
  17.5 2.2 %second_inner.1 = (f32[1024,128]{1,0:T(8,128)S(1)}, f32[1024,128]{1,0:T(8,128)S(1)}, f32[1024,128]{1,0:T(8,128)S(1)}, f32[1024,128]{1,0:T(8,128)S(1)}, f32[1024,128]{1,0:T(8,128)S(1)}) custom-call(f32[1024,128]{1,0:T(8,128)S(1)} %get-tuple-element.69.refs_0_, f32[1024,128]{1,0:T(8,128)S(1)} %get-tuple-element.70.refs_1_, ...), custom_call_target="tpu_custom_call" | custom-call | flops 13107200 | bytes 4718592 | tf_op jit(solution)/shard_map/second_inner/pallas_call | solution.py:607
  19.7 1.4 %second_edge.1 = (f32[1024,128]{1,0:T(8,128)S(1)}, f32[1024,128]{1,0:T(8,128)S(1)}, f32[32,128]{1,0:T(8,128)}, f32[2,16,128]{2,1,0:T(8,128)S(1)}, f32[2,64,128]{...) custom-call(f32[1024,128]{1,0:T(8,128)S(1)} %get-tuple-element.75.re, ...), custom_call_target="tpu_custom_call" | custom-call | bytes 2719744 | tf_op jit(solution)/shard_map/second_edge/pallas_call | solution.py:607
  21.2 1.6 %collective-permute-start.12 = (f32[128,128]{1,0:T(8,128)S(1)}, f32[128,128]{1,0:T(8,128)S(1)}, u32[]{:S(2)}, u32[]{:S(2)}) collective-permute-start(f32[128,128]{1,0:T(8,128)S(1)} %choose.1), channel_id=1, source_target_pairs={{0,4},{1,5},{2,6},{3,7},{4,0},{5,1},{6,2},{7,3},{8,12},{9,13},{10,... | collective-permute-start | bytes 196616 | tf_op jit(solution)/shard_map/ppermute | solution.py:72
  22.7 2.7 %all-to-all-start = ((f32[32,1,128]{2,1,0:T(1,128)}), f32[32,1,128]{2,1,0:T(1,128)S(1)}, u32[]{:S(2)}, u32[]{:S(2)}) async-start(f32[32,1,128]{2,1,0:T(1,128)} %bitcast.6), calls=%async_computation | async-start | bytes 32768 | tf_op jit(solution)/shard_map/all_to_all | solution.py:685
  25.5 0.3 collective-permute-start.10
  25.8 1.6 %collective-permute-start.11 = (f32[32,128]{1,0:T(8,128)S(1)}, f32[32,128]{1,0:T(8,128)S(1)}, u32[]{:S(2)}, u32[]{:S(2)}) collective-permute-start(f32[32,128]{1,0:T(8,128)S(1)} %get-tuple-element.97), channel_id=1, source_target_pairs={{0,24},{1,25},{2,26},{3,27},{4,28},{5,29},{6,30},{7,31},{8,16},{9,... | collective-permute-start | bytes 49160 | tf_op jit(solution)/shard_map/ppermute | solution.py:72
  27.4 1.5 %collective-permute-start.13 = (f32[32,128]{1,0:T(8,128)S(1)}, f32[32,128]{1,0:T(8,128)S(1)}, u32[]{:S(2)}, u32[]{:S(2)}) collective-permute-start(f32[32,128]{1,0:T(8,128)S(1)} %get-tuple-element.95.refs_7_), channel_id=1, source_target_pairs={{0,1},{1,0},{2,3},{3,2},{4,5},{5,4},{6,7},{7,6},{8,9},{9,8},{10,11... | collective-permute-start | bytes 49160 | tf_op jit(solution)/shard_map/ppermute | solution.py:72
  28.9 1.5 %third_inner.1 = (f32[1024,128]{1,0:T(8,128)S(1)}, f32[2,16,128]{2,1,0:T(8,128)S(1)}, f32[2,64,128]{2,1,0:T(8,128)S(1)}) custom-call(f32[1024,128]{1,0:T(8,128)S(1)} %get-tuple-element.69.refs_0_, f32[1024,128]{1,0:T(8,128)S(1)} %get-tuple-element.61.refs_3_.refs_2_.refs_1_, ...), custom_call_target="tpu_custom_call", output_to_operand_aliasing={{0}: (5, {})} | custom-call | flops 13107200 | bytes 3145728 | tf_op jit(solution)/shard_map/third_inner/pallas_call | solution.py:607
  30.4 0.8 %collective-permute-done.13.refs_11_ = f32[32,128]{1,0:T(8,128)S(1)} collective-permute-done((f32[32,128]{1,0:T(8,128)S(1)}, f32[32,128]{1,0:T(8,128)S(1)}, u32[]{:S(2)}, u32[]{:S(2)}) %collective-permute-start.13) | collective-permute-done | bytes 16416 | tf_op jit(solution)/shard_map/ppermute | solution.py:72
  31.2 1.1 %finish.1 = f32[1024,128]{1,0:T(8,128)} custom-call(f32[1024,128]{1,0:T(8,128)S(1)} %get-tuple-element.73.refs_5_.refs_4_.refs_0_, f32[1024,128]{1,0:T(8,128)S(1)} %get-tuple-element.89.refs_1_, f32[2,16,128]{2,1,0:T(8,128)S(1)} %get-tuple-element.90.refs_2_, f32[2,64,128]{2,1,0:T(8,128)S(1)} %get-tuple-element.91.refs_3_, ...), custom_call_target="tpu_custom_call" | custom-call | flops 13107200 | bytes 1368064 | tf_op jit(solution)/shard_map/finish/pallas_call | solution.py:607
  32.3 0.3 all-to-all-done
  32.6 0.6 %totals.1 = (f32[1,1]{1,0:T(1,128)}, f32[1,1]{1,0:T(1,128)}) custom-call(f32[32,128]{1,0:T(8,128)S(1)} %bitcast.15), custom_call_target="tpu_custom_call" | custom-call | bytes 16384 | tf_op jit(solution)/shard_map/totals/pallas_call | solution.py:607
  (21 shorter events, 0.1 us)
Async XLA Ops:
  0.6 9.2 %copy-start = (f32[64,16,128]{2,1,0:T(8,128)S(1)}, f32[64,16,128]{2,1,0:T(8,128)}, u32[]{:S(2)}) copy-start(f32[64,16,128]{2,1,0:T(8,128)} %param.8) | copy-start | bytes 1572868
  3.6 13.9 %copy-start.1 = (bf16[2,64,16,128]{3,2,1,0:T(8,128)(2,1)S(1)}, bf16[2,64,16,128]{3,2,1,0:T(8,128)(2,1)}, u32[]{:S(2)}) copy-start(bf16[2,64,16,128]{3,2,1,0:T(8,128)(2,1)} %param.9) | copy-start | bytes 1572868
  3.6 8.4 %collective-permute-start.2 = (f32[192,128]{1,0:T(8,128)S(1)}, f32[192,128]{1,0:T(8,128)S(1)}, u32[]{:S(2)}, u32[]{:S(2)}) collective-permute-start(f32[192,128]{1,0:T(8,128)S(1)} %get-tuple-element.68), channel_id=1, source_target_pairs={{0,4},{1,5},{2,6},{3,7},{4,0},{5,1},{6,2},{7,3},{8,12},{9,13},{10,... | collective-permute-start | bytes 294920 | tf_op jit(solution)/shard_map/ppermute | solution.py:72
  6.6 5.4 %collective-permute-start.3 = (f32[48,128]{1,0:T(8,128)S(1)}, f32[48,128]{1,0:T(8,128)S(1)}, u32[]{:S(2)}, u32[]{:S(2)}) collective-permute-start(f32[48,128]{1,0:T(8,128)S(1)} %get-tuple-element.65.refs_7_), channel_id=1, source_target_pairs={{0,1},{1,0},{2,3},{3,2},{4,5},{5,4},{6,7},{7,6},{8,9},{9,8},{10,11... | collective-permute-start | bytes 73736 | tf_op jit(solution)/shard_map/ppermute | solution.py:72
  8.1 3.8 %collective-permute-start.4 = (f32[48,128]{1,0:T(8,128)S(1)}, f32[48,128]{1,0:T(8,128)S(1)}, u32[]{:S(2)}, u32[]{:S(2)}) collective-permute-start(f32[48,128]{1,0:T(8,128)S(1)} %get-tuple-element.65.refs_7_), channel_id=1, source_target_pairs={{0,8},{1,2},{2,1},{3,11},{4,12},{5,6},{6,5},{7,15},{8,0},{9,10},{1... | collective-permute-start | bytes 73736 | tf_op jit(solution)/shard_map/ppermute | solution.py:72
  8.2 3.8 %collective-permute-start = (f32[48,128]{1,0:T(8,128)S(1)}, f32[48,128]{1,0:T(8,128)S(1)}, u32[]{:S(2)}, u32[]{:S(2)}) collective-permute-start(f32[48,128]{1,0:T(8,128)S(1)} %get-tuple-element.66), channel_id=1, source_target_pairs={{0,8},{1,9},{2,10},{3,11},{4,12},{5,13},{6,14},{7,15},{8,0},{9,1},... | collective-permute-start | bytes 73736 | tf_op jit(solution)/shard_map/ppermute | solution.py:72
  8.7 3.3 %collective-permute-start.1 = (f32[48,128]{1,0:T(8,128)S(1)}, f32[48,128]{1,0:T(8,128)S(1)}, u32[]{:S(2)}, u32[]{:S(2)}) collective-permute-start(f32[48,128]{1,0:T(8,128)S(1)} %get-tuple-element.67), channel_id=1, source_target_pairs={{0,24},{1,25},{2,26},{3,27},{4,28},{5,29},{6,30},{7,31},{8,16},{9,... | collective-permute-start | bytes 73736 | tf_op jit(solution)/shard_map/ppermute | solution.py:72
  12.7 7.0 %collective-permute-start.7 = (f32[256,128]{1,0:T(8,128)S(1)}, f32[256,128]{1,0:T(8,128)S(1)}, u32[]{:S(2)}, u32[]{:S(2)}) collective-permute-start(f32[256,128]{1,0:T(8,128)S(1)} %get-tuple-element.84), channel_id=1, source_target_pairs={{0,4},{1,5},{2,6},{3,7},{4,0},{5,1},{6,2},{7,3},{8,12},{9,13},{10,... | collective-permute-start | bytes 393224 | tf_op jit(solution)/shard_map/ppermute | solution.py:72
  13.3 6.4 %collective-permute-start.5 = (f32[64,128]{1,0:T(8,128)S(1)}, f32[64,128]{1,0:T(8,128)S(1)}, u32[]{:S(2)}, u32[]{:S(2)}) collective-permute-start(f32[64,128]{1,0:T(8,128)S(1)} %get-tuple-element.82), channel_id=1, source_target_pairs={{0,8},{1,9},{2,10},{3,11},{4,12},{5,13},{6,14},{7,15},{8,0},{9,1},... | collective-permute-start | bytes 98312 | tf_op jit(solution)/shard_map/ppermute | solution.py:72
  13.5 6.2 %collective-permute-start.6 = (f32[64,128]{1,0:T(8,128)S(1)}, f32[64,128]{1,0:T(8,128)S(1)}, u32[]{:S(2)}, u32[]{:S(2)}) collective-permute-start(f32[64,128]{1,0:T(8,128)S(1)} %get-tuple-element.83), channel_id=1, source_target_pairs={{0,24},{1,25},{2,26},{3,27},{4,28},{5,29},{6,30},{7,31},{8,16},{9,... | collective-permute-start | bytes 98312 | tf_op jit(solution)/shard_map/ppermute | solution.py:72
  14.9 4.8 %collective-permute-start.8 = (f32[64,128]{1,0:T(8,128)S(1)}, f32[64,128]{1,0:T(8,128)S(1)}, u32[]{:S(2)}, u32[]{:S(2)}) collective-permute-start(f32[64,128]{1,0:T(8,128)S(1)} %get-tuple-element.81.refs_6_), channel_id=1, source_target_pairs={{0,1},{1,0},{2,3},{3,2},{4,5},{5,4},{6,7},{7,6},{8,9},{9,8},{10,11... | collective-permute-start | bytes 98312 | tf_op jit(solution)/shard_map/ppermute | solution.py:72
  17.5 2.3 %collective-permute-start.9 = (f32[64,128]{1,0:T(8,128)S(1)}, f32[64,128]{1,0:T(8,128)S(1)}, u32[]{:S(2)}, u32[]{:S(2)}) collective-permute-start(f32[64,128]{1,0:T(8,128)S(1)} %get-tuple-element.81.refs_6_), channel_id=1, source_target_pairs={{0,8},{1,2},{2,1},{3,11},{4,12},{5,6},{6,5},{7,15},{8,0},{9,10},{1... | collective-permute-start | bytes 98312 | tf_op jit(solution)/shard_map/ppermute | solution.py:72
  21.2 10.0 %collective-permute-start.12 = (f32[128,128]{1,0:T(8,128)S(1)}, f32[128,128]{1,0:T(8,128)S(1)}, u32[]{:S(2)}, u32[]{:S(2)}) collective-permute-start(f32[128,128]{1,0:T(8,128)S(1)} %choose.1), channel_id=1, source_target_pairs={{0,4},{1,5},{2,6},{3,7},{4,0},{5,1},{6,2},{7,3},{8,12},{9,13},{10,... | collective-permute-start | bytes 196616 | tf_op jit(solution)/shard_map/ppermute | solution.py:72
  22.7 9.9 %all-to-all-start = ((f32[32,1,128]{2,1,0:T(1,128)}), f32[32,1,128]{2,1,0:T(1,128)S(1)}, u32[]{:S(2)}, u32[]{:S(2)}) async-start(f32[32,1,128]{2,1,0:T(1,128)} %bitcast.6), calls=%async_computation | async-start | bytes 32768 | tf_op jit(solution)/shard_map/all_to_all | solution.py:685
  25.5 4.9 %collective-permute-start.10 = (f32[32,128]{1,0:T(8,128)S(1)}, f32[32,128]{1,0:T(8,128)S(1)}, u32[]{:S(2)}, u32[]{:S(2)}) collective-permute-start(f32[32,128]{1,0:T(8,128)S(1)} %get-tuple-element.96), channel_id=1, source_target_pairs={{0,8},{1,9},{2,10},{3,11},{4,12},{5,13},{6,14},{7,15},{8,0},{9,1},... | collective-permute-start | bytes 49160 | tf_op jit(solution)/shard_map/ppermute | solution.py:72
  25.8 4.6 %collective-permute-start.11 = (f32[32,128]{1,0:T(8,128)S(1)}, f32[32,128]{1,0:T(8,128)S(1)}, u32[]{:S(2)}, u32[]{:S(2)}) collective-permute-start(f32[32,128]{1,0:T(8,128)S(1)} %get-tuple-element.97), channel_id=1, source_target_pairs={{0,24},{1,25},{2,26},{3,27},{4,28},{5,29},{6,30},{7,31},{8,16},{9,... | collective-permute-start | bytes 49160 | tf_op jit(solution)/shard_map/ppermute | solution.py:72
  27.4 3.7 %collective-permute-start.13 = (f32[32,128]{1,0:T(8,128)S(1)}, f32[32,128]{1,0:T(8,128)S(1)}, u32[]{:S(2)}, u32[]{:S(2)}) collective-permute-start(f32[32,128]{1,0:T(8,128)S(1)} %get-tuple-element.95.refs_7_), channel_id=1, source_target_pairs={{0,1},{1,0},{2,3},{3,2},{4,5},{5,4},{6,7},{7,6},{8,9},{9,8},{10,11... | collective-permute-start | bytes 49160 | tf_op jit(solution)/shard_map/ppermute | solution.py:72
  28.9 2.3 %collective-permute-start.14 = (f32[32,128]{1,0:T(8,128)S(1)}, f32[32,128]{1,0:T(8,128)S(1)}, u32[]{:S(2)}, u32[]{:S(2)}) collective-permute-start(f32[32,128]{1,0:T(8,128)S(1)} %get-tuple-element.95.refs_7_), channel_id=1, source_target_pairs={{0,8},{1,2},{2,1},{3,11},{4,12},{5,6},{6,5},{7,15},{8,0},{9,10},{1... | collective-permute-start | bytes 49160 | tf_op jit(solution)/shard_map/ppermute | solution.py:72

commit v6 on v5

--- a/solution.py
+++ b/solution.py
@@ -266,13 +266,13 @@
     k_ref, l_ref, m_ref, t_ref, s_ref = refs[3:8]
     own = Own(dims, counts, refs[8:-2])
     c_ref, sems = refs[-2:]
-    rows = nx * ny // chunks
     copies = [
         pltpu.make_async_copy(t_hbm, t_ref, sems.at[chunks]),
         pltpu.make_async_copy(s_hbm, s_ref, sems.at[chunks + 1]),
     ]
+    ends = [nx * i // 16 for i in (0, 2, 6, 10, 14, 16)]
     for j in range(chunks):
-        part = pl.ds(j * rows, rows)
+        part = pl.ds(ends[j] * ny, (ends[j + 1] - ends[j]) * ny)
         copies.append(pltpu.make_async_copy(c_hbm.at[:, part, :], c_ref.at[:, part, :], sems.at[j]))
     for copy in copies:
         copy.start()
@@ -299,10 +299,9 @@
         return tuple(pack_z(a, v, x, lane) for a, v in zip(accs, faces))
 
     accs = tuple(jnp.zeros((ny, LANES), F32) for _ in range(3))
-    planes = nx // chunks
     for j in range(chunks):
         copies[2 + j].wait()
-        accs = lax.fori_loop(j * planes, (j + 1) * planes, plane, accs, unroll=8)
+        accs = lax.fori_loop(ends[j], ends[j + 1], plane, accs, unroll=min(8, ends[j + 1] - ends[j]))
     own.finish((t_ref, s_ref, k_ref), accs)
 
 
@@ -630,7 +629,7 @@
     hbm = pl.BlockSpec(memory_space=pl.ANY)
     work = cells * nz * 100
 
-    chunks = 8
+    chunks = 5
     res = call(
         functools.partial(prepare_kernel, dims, counts, bins, chunks),
         [field] * 5 + own_shapes(dims, counts, 3),

time: 33.4 us -> 33.6 us (level)
  no operation moved by 1% of the time
where the time goes in v6:
time: 33.6 us; the launch traced here: 33.4 us
  starting transfers between devices  18.7 us (56%)
  Pallas kernels  12.8 us (38%)
  waiting for transfers between devices  1.07 us (3%)
  between operations  0.8 us (2%)
    ppermute x15, starting transfers between devices, exchange(): lax.ppermute(p, AXES, swap_pairs(counts, axis, kind))  16 us
    pallas_call x9, Pallas kernels, call(): pl.pallas_call(kernel, out_shape=[jax.ShapeDtypeStruct(s, d) for s, d in...  12.8 us
    all_to_all x1, starting transfers between devices, per_device(): sums = lax.all_to_all(sums, AXES, 0, 0, tiled=True)  2.74 us
    ppermute x15, waiting for transfers between devices, exchange(): lax.ppermute(p, AXES, swap_pairs(counts, axis, kind))  0.79 us
  transfers between devices with their start and end apart: 16, of which 2 were waited for; matrix products, arithmetic and copies ran while one was open for 0% of the time, Pallas kernels for 21%

profile of v6, /device:TPU:0, one launch (start us, length us, event | category | flops | bytes accessed | tf_op | source)
XLA Modules:
  0.0 33.4 jit_solution(12854210226532386660)
XLA Ops:
  0.6 3.1 %prepare.1 = (f32[1024,128]{1,0:T(8,128)S(1)}, f32[1024,128]{1,0:T(8,128)S(1)}, f32[1024,128]{1,0:T(8,128)S(1)}, f32[1024,128]{1,0:T(8,128)S(1)}, f32[1024,128]{...) custom-call(f32[8,1024,128]{2,1,0:T(8,128)} %bitcast.16, ...), custom_call_target="tpu_custom_call" | custom-call | bytes 5242880 | tf_op jit(solution)/shard_map/prepare/pallas_call | solution.py:606
  3.7 0.0 copy-start.1
  3.7 3.0 %collective-permute-start.2 = (f32[192,128]{1,0:T(8,128)S(1)}, f32[192,128]{1,0:T(8,128)S(1)}, u32[]{:S(2)}, u32[]{:S(2)}) collective-permute-start(f32[192,128]{1,0:T(8,128)S(1)} %get-tuple-element.68), channel_id=1, source_target_pairs={{0,4},{1,5},{2,6},{3,7},{4,0},{5,1},{6,2},{7,3},{8,12},{9,13},{10,... | collective-permute-start | bytes 294920 | tf_op jit(solution)/shard_map/ppermute | solution.py:72
  6.7 1.6 %collective-permute-start.3 = (f32[48,128]{1,0:T(8,128)S(1)}, f32[48,128]{1,0:T(8,128)S(1)}, u32[]{:S(2)}, u32[]{:S(2)}) collective-permute-start(f32[48,128]{1,0:T(8,128)S(1)} %get-tuple-element.65.refs_7_), channel_id=1, source_target_pairs={{0,1},{1,0},{2,3},{3,2},{4,5},{5,4},{6,7},{7,6},{8,9},{9,8},{10,11... | collective-permute-start | bytes 73736 | tf_op jit(solution)/shard_map/ppermute | solution.py:72
  8.3 0.5 %collective-permute-start = (f32[48,128]{1,0:T(8,128)S(1)}, f32[48,128]{1,0:T(8,128)S(1)}, u32[]{:S(2)}, u32[]{:S(2)}) collective-permute-start(f32[48,128]{1,0:T(8,128)S(1)} %get-tuple-element.66), channel_id=1, source_target_pairs={{0,8},{1,9},{2,10},{3,11},{4,12},{5,13},{6,14},{7,15},{8,0},{9,1},... | collective-permute-start | bytes 73736 | tf_op jit(solution)/shard_map/ppermute | solution.py:72
  8.8 1.1 %collective-permute-start.1 = (f32[48,128]{1,0:T(8,128)S(1)}, f32[48,128]{1,0:T(8,128)S(1)}, u32[]{:S(2)}, u32[]{:S(2)}) collective-permute-start(f32[48,128]{1,0:T(8,128)S(1)} %get-tuple-element.67), channel_id=1, source_target_pairs={{0,24},{1,25},{2,26},{3,27},{4,28},{5,29},{6,30},{7,31},{8,16},{9,... | collective-permute-start | bytes 73736 | tf_op jit(solution)/shard_map/ppermute | solution.py:72
  9.9 2.2 %first_inner.1 = (f32[1024,128]{1,0:T(8,128)S(1)}, f32[1024,128]{1,0:T(8,128)S(1)}, f32[1024,128]{1,0:T(8,128)S(1)}, f32[1024,128]{1,0:T(8,128)S(1)}, f32[1024,1...) custom-call(f32[1024,128]{1,0:T(8,128)S(1)} %get-tuple-element.53.refs_0_, ...), custom_call_target="tpu_custom_call" | custom-call | flops 13107200 | bytes 3145728 | tf_op jit(solution)/shard_map/first_inner/pallas_call | solution.py:606
  12.2 0.7 %first_edge.1 = (f32[1024,128]{1,0:T(8,128)S(1)}, f32[1024,128]{1,0:T(8,128)S(1)}, f32[1024,128]{1,0:T(8,128)S(1)}, f32[2,64,128]{2,1,0:T(8,128)S(1)}, f32[2,256...) custom-call(f32[1024,128]{1,0:T(8,128)S(1)} %get-tuple-element.58.re, ...), custom_call_target="tpu_custom_call" | custom-call | bytes 2596864 | tf_op jit(solution)/shard_map/first_edge/pallas_call | solution.py:606
  12.8 0.6 %collective-permute-start.7 = (f32[256,128]{1,0:T(8,128)S(1)}, f32[256,128]{1,0:T(8,128)S(1)}, u32[]{:S(2)}, u32[]{:S(2)}) collective-permute-start(f32[256,128]{1,0:T(8,128)S(1)} %get-tuple-element.84), channel_id=1, source_target_pairs={{0,4},{1,5},{2,6},{3,7},{4,0},{5,1},{6,2},{7,3},{8,12},{9,13},{10,... | collective-permute-start | bytes 393224 | tf_op jit(solution)/shard_map/ppermute | solution.py:72
  13.4 0.2 collective-permute-start.5
  13.7 1.4 %collective-permute-start.6 = (f32[64,128]{1,0:T(8,128)S(1)}, f32[64,128]{1,0:T(8,128)S(1)}, u32[]{:S(2)}, u32[]{:S(2)}) collective-permute-start(f32[64,128]{1,0:T(8,128)S(1)} %get-tuple-element.83), channel_id=1, source_target_pairs={{0,24},{1,25},{2,26},{3,27},{4,28},{5,29},{6,30},{7,31},{8,16},{9,... | collective-permute-start | bytes 98312 | tf_op jit(solution)/shard_map/ppermute | solution.py:72
  15.0 2.6 %collective-permute-start.8 = (f32[64,128]{1,0:T(8,128)S(1)}, f32[64,128]{1,0:T(8,128)S(1)}, u32[]{:S(2)}, u32[]{:S(2)}) collective-permute-start(f32[64,128]{1,0:T(8,128)S(1)} %get-tuple-element.81.refs_6_), channel_id=1, source_target_pairs={{0,1},{1,0},{2,3},{3,2},{4,5},{5,4},{6,7},{7,6},{8,9},{9,8},{10,11... | collective-permute-start | bytes 98312 | tf_op jit(solution)/shard_map/ppermute | solution.py:72
  17.6 2.2 %second_inner.1 = (f32[1024,128]{1,0:T(8,128)S(1)}, f32[1024,128]{1,0:T(8,128)S(1)}, f32[1024,128]{1,0:T(8,128)S(1)}, f32[1024,128]{1,0:T(8,128)S(1)}, f32[1024,128]{1,0:T(8,128)S(1)}) custom-call(f32[1024,128]{1,0:T(8,128)S(1)} %get-tuple-element.69.refs_0_, f32[1024,128]{1,0:T(8,128)S(1)} %get-tuple-element.70.refs_1_, ...), custom_call_target="tpu_custom_call" | custom-call | flops 13107200 | bytes 4718592 | tf_op jit(solution)/shard_map/second_inner/pallas_call | solution.py:606
  19.9 1.4 %second_edge.1 = (f32[1024,128]{1,0:T(8,128)S(1)}, f32[1024,128]{1,0:T(8,128)S(1)}, f32[32,128]{1,0:T(8,128)}, f32[2,16,128]{2,1,0:T(8,128)S(1)}, f32[2,64,128]{...) custom-call(f32[1024,128]{1,0:T(8,128)S(1)} %get-tuple-element.75.re, ...), custom_call_target="tpu_custom_call" | custom-call | bytes 2719744 | tf_op jit(solution)/shard_map/second_edge/pallas_call | solution.py:606
  21.3 1.6 %collective-permute-start.12 = (f32[128,128]{1,0:T(8,128)S(1)}, f32[128,128]{1,0:T(8,128)S(1)}, u32[]{:S(2)}, u32[]{:S(2)}) collective-permute-start(f32[128,128]{1,0:T(8,128)S(1)} %choose.1), channel_id=1, source_target_pairs={{0,4},{1,5},{2,6},{3,7},{4,0},{5,1},{6,2},{7,3},{8,12},{9,13},{10,... | collective-permute-start | bytes 196616 | tf_op jit(solution)/shard_map/ppermute | solution.py:72
  22.9 2.7 %all-to-all-start = ((f32[32,1,128]{2,1,0:T(1,128)}), f32[32,1,128]{2,1,0:T(1,128)S(1)}, u32[]{:S(2)}, u32[]{:S(2)}) async-start(f32[32,1,128]{2,1,0:T(1,128)} %bitcast.6), calls=%async_computation | async-start | bytes 32768 | tf_op jit(solution)/shard_map/all_to_all | solution.py:684
  25.6 0.3 collective-permute-start.10
  25.9 1.6 %collective-permute-start.11 = (f32[32,128]{1,0:T(8,128)S(1)}, f32[32,128]{1,0:T(8,128)S(1)}, u32[]{:S(2)}, u32[]{:S(2)}) collective-permute-start(f32[32,128]{1,0:T(8,128)S(1)} %get-tuple-element.97), channel_id=1, source_target_pairs={{0,24},{1,25},{2,26},{3,27},{4,28},{5,29},{6,30},{7,31},{8,16},{9,... | collective-permute-start | bytes 49160 | tf_op jit(solution)/shard_map/ppermute | solution.py:72
  27.6 1.5 %collective-permute-start.13 = (f32[32,128]{1,0:T(8,128)S(1)}, f32[32,128]{1,0:T(8,128)S(1)}, u32[]{:S(2)}, u32[]{:S(2)}) collective-permute-start(f32[32,128]{1,0:T(8,128)S(1)} %get-tuple-element.95.refs_7_), channel_id=1, source_target_pairs={{0,1},{1,0},{2,3},{3,2},{4,5},{5,4},{6,7},{7,6},{8,9},{9,8},{10,11... | collective-permute-start | bytes 49160 | tf_op jit(solution)/shard_map/ppermute | solution.py:72
  29.0 1.5 %third_inner.1 = (f32[1024,128]{1,0:T(8,128)S(1)}, f32[2,16,128]{2,1,0:T(8,128)S(1)}, f32[2,64,128]{2,1,0:T(8,128)S(1)}) custom-call(f32[1024,128]{1,0:T(8,128)S(1)} %get-tuple-element.69.refs_0_, f32[1024,128]{1,0:T(8,128)S(1)} %get-tuple-element.61.refs_3_.refs_2_.refs_1_, ...), custom_call_target="tpu_custom_call", output_to_operand_aliasing={{0}: (5, {})} | custom-call | flops 13107200 | bytes 3145728 | tf_op jit(solution)/shard_map/third_inner/pallas_call | solution.py:606
  30.6 0.8 %collective-permute-done.13.refs_11_ = f32[32,128]{1,0:T(8,128)S(1)} collective-permute-done((f32[32,128]{1,0:T(8,128)S(1)}, f32[32,128]{1,0:T(8,128)S(1)}, u32[]{:S(2)}, u32[]{:S(2)}) %collective-permute-start.13) | collective-permute-done | bytes 16416 | tf_op jit(solution)/shard_map/ppermute | solution.py:72
  31.3 1.1 %finish.1 = f32[1024,128]{1,0:T(8,128)} custom-call(f32[1024,128]{1,0:T(8,128)S(1)} %get-tuple-element.73.refs_5_.refs_4_.refs_0_, f32[1024,128]{1,0:T(8,128)S(1)} %get-tuple-element.89.refs_1_, f32[2,16,128]{2,1,0:T(8,128)S(1)} %get-tuple-element.90.refs_2_, f32[2,64,128]{2,1,0:T(8,128)S(1)} %get-tuple-element.91.refs_3_, ...), custom_call_target="tpu_custom_call" | custom-call | flops 13107200 | bytes 1368064 | tf_op jit(solution)/shard_map/finish/pallas_call | solution.py:606
  32.5 0.3 all-to-all-done
  32.7 0.6 %totals.1 = (f32[1,1]{1,0:T(1,128)}, f32[1,1]{1,0:T(1,128)}) custom-call(f32[32,128]{1,0:T(8,128)S(1)} %bitcast.15), custom_call_target="tpu_custom_call" | custom-call | bytes 16384 | tf_op jit(solution)/shard_map/totals/pallas_call | solution.py:606
  (21 shorter events, 0.1 us)
Async XLA Ops:
  0.6 9.3 %copy-start = (f32[64,16,128]{2,1,0:T(8,128)S(1)}, f32[64,16,128]{2,1,0:T(8,128)}, u32[]{:S(2)}) copy-start(f32[64,16,128]{2,1,0:T(8,128)} %param.8) | copy-start | bytes 1572868
  3.7 13.9 %copy-start.1 = (bf16[2,64,16,128]{3,2,1,0:T(8,128)(2,1)S(1)}, bf16[2,64,16,128]{3,2,1,0:T(8,128)(2,1)}, u32[]{:S(2)}) copy-start(bf16[2,64,16,128]{3,2,1,0:T(8,128)(2,1)} %param.9) | copy-start | bytes 1572868
  3.7 8.4 %collective-permute-start.2 = (f32[192,128]{1,0:T(8,128)S(1)}, f32[192,128]{1,0:T(8,128)S(1)}, u32[]{:S(2)}, u32[]{:S(2)}) collective-permute-start(f32[192,128]{1,0:T(8,128)S(1)} %get-tuple-element.68), channel_id=1, source_target_pairs={{0,4},{1,5},{2,6},{3,7},{4,0},{5,1},{6,2},{7,3},{8,12},{9,13},{10,... | collective-permute-start | bytes 294920 | tf_op jit(solution)/shard_map/ppermute | solution.py:72
  6.7 5.4 %collective-permute-start.3 = (f32[48,128]{1,0:T(8,128)S(1)}, f32[48,128]{1,0:T(8,128)S(1)}, u32[]{:S(2)}, u32[]{:S(2)}) collective-permute-start(f32[48,128]{1,0:T(8,128)S(1)} %get-tuple-element.65.refs_7_), channel_id=1, source_target_pairs={{0,1},{1,0},{2,3},{3,2},{4,5},{5,4},{6,7},{7,6},{8,9},{9,8},{10,11... | collective-permute-start | bytes 73736 | tf_op jit(solution)/shard_map/ppermute | solution.py:72
  8.3 3.8 %collective-permute-start.4 = (f32[48,128]{1,0:T(8,128)S(1)}, f32[48,128]{1,0:T(8,128)S(1)}, u32[]{:S(2)}, u32[]{:S(2)}) collective-permute-start(f32[48,128]{1,0:T(8,128)S(1)} %get-tuple-element.65.refs_7_), channel_id=1, source_target_pairs={{0,8},{1,2},{2,1},{3,11},{4,12},{5,6},{6,5},{7,15},{8,0},{9,10},{1... | collective-permute-start | bytes 73736 | tf_op jit(solution)/shard_map/ppermute | solution.py:72
  8.3 3.8 %collective-permute-start = (f32[48,128]{1,0:T(8,128)S(1)}, f32[48,128]{1,0:T(8,128)S(1)}, u32[]{:S(2)}, u32[]{:S(2)}) collective-permute-start(f32[48,128]{1,0:T(8,128)S(1)} %get-tuple-element.66), channel_id=1, source_target_pairs={{0,8},{1,9},{2,10},{3,11},{4,12},{5,13},{6,14},{7,15},{8,0},{9,1},... | collective-permute-start | bytes 73736 | tf_op jit(solution)/shard_map/ppermute | solution.py:72
  8.8 3.3 %collective-permute-start.1 = (f32[48,128]{1,0:T(8,128)S(1)}, f32[48,128]{1,0:T(8,128)S(1)}, u32[]{:S(2)}, u32[]{:S(2)}) collective-permute-start(f32[48,128]{1,0:T(8,128)S(1)} %get-tuple-element.67), channel_id=1, source_target_pairs={{0,24},{1,25},{2,26},{3,27},{4,28},{5,29},{6,30},{7,31},{8,16},{9,... | collective-permute-start | bytes 73736 | tf_op jit(solution)/shard_map/ppermute | solution.py:72
  12.8 7.0 %collective-permute-start.7 = (f32[256,128]{1,0:T(8,128)S(1)}, f32[256,128]{1,0:T(8,128)S(1)}, u32[]{:S(2)}, u32[]{:S(2)}) collective-permute-start(f32[256,128]{1,0:T(8,128)S(1)} %get-tuple-element.84), channel_id=1, source_target_pairs={{0,4},{1,5},{2,6},{3,7},{4,0},{5,1},{6,2},{7,3},{8,12},{9,13},{10,... | collective-permute-start | bytes 393224 | tf_op jit(solution)/shard_map/ppermute | solution.py:72
  13.4 6.4 %collective-permute-start.5 = (f32[64,128]{1,0:T(8,128)S(1)}, f32[64,128]{1,0:T(8,128)S(1)}, u32[]{:S(2)}, u32[]{:S(2)}) collective-permute-start(f32[64,128]{1,0:T(8,128)S(1)} %get-tuple-element.82), channel_id=1, source_target_pairs={{0,8},{1,9},{2,10},{3,11},{4,12},{5,13},{6,14},{7,15},{8,0},{9,1},... | collective-permute-start | bytes 98312 | tf_op jit(solution)/shard_map/ppermute | solution.py:72
  13.7 6.2 %collective-permute-start.6 = (f32[64,128]{1,0:T(8,128)S(1)}, f32[64,128]{1,0:T(8,128)S(1)}, u32[]{:S(2)}, u32[]{:S(2)}) collective-permute-start(f32[64,128]{1,0:T(8,128)S(1)} %get-tuple-element.83), channel_id=1, source_target_pairs={{0,24},{1,25},{2,26},{3,27},{4,28},{5,29},{6,30},{7,31},{8,16},{9,... | collective-permute-start | bytes 98312 | tf_op jit(solution)/shard_map/ppermute | solution.py:72
  15.0 4.8 %collective-permute-start.8 = (f32[64,128]{1,0:T(8,128)S(1)}, f32[64,128]{1,0:T(8,128)S(1)}, u32[]{:S(2)}, u32[]{:S(2)}) collective-permute-start(f32[64,128]{1,0:T(8,128)S(1)} %get-tuple-element.81.refs_6_), channel_id=1, source_target_pairs={{0,1},{1,0},{2,3},{3,2},{4,5},{5,4},{6,7},{7,6},{8,9},{9,8},{10,11... | collective-permute-start | bytes 98312 | tf_op jit(solution)/shard_map/ppermute | solution.py:72
  17.6 2.3 %collective-permute-start.9 = (f32[64,128]{1,0:T(8,128)S(1)}, f32[64,128]{1,0:T(8,128)S(1)}, u32[]{:S(2)}, u32[]{:S(2)}) collective-permute-start(f32[64,128]{1,0:T(8,128)S(1)} %get-tuple-element.81.refs_6_), channel_id=1, source_target_pairs={{0,8},{1,2},{2,1},{3,11},{4,12},{5,6},{6,5},{7,15},{8,0},{9,10},{1... | collective-permute-start | bytes 98312 | tf_op jit(solution)/shard_map/ppermute | solution.py:72
  21.3 10.0 %collective-permute-start.12 = (f32[128,128]{1,0:T(8,128)S(1)}, f32[128,128]{1,0:T(8,128)S(1)}, u32[]{:S(2)}, u32[]{:S(2)}) collective-permute-start(f32[128,128]{1,0:T(8,128)S(1)} %choose.1), channel_id=1, source_target_pairs={{0,4},{1,5},{2,6},{3,7},{4,0},{5,1},{6,2},{7,3},{8,12},{9,13},{10,... | collective-permute-start | bytes 196616 | tf_op jit(solution)/shard_map/ppermute | solution.py:72
  22.9 9.9 %all-to-all-start = ((f32[32,1,128]{2,1,0:T(1,128)}), f32[32,1,128]{2,1,0:T(1,128)S(1)}, u32[]{:S(2)}, u32[]{:S(2)}) async-start(f32[32,1,128]{2,1,0:T(1,128)} %bitcast.6), calls=%async_computation | async-start | bytes 32768 | tf_op jit(solution)/shard_map/all_to_all | solution.py:684
  25.6 4.9 %collective-permute-start.10 = (f32[32,128]{1,0:T(8,128)S(1)}, f32[32,128]{1,0:T(8,128)S(1)}, u32[]{:S(2)}, u32[]{:S(2)}) collective-permute-start(f32[32,128]{1,0:T(8,128)S(1)} %get-tuple-element.96), channel_id=1, source_target_pairs={{0,8},{1,9},{2,10},{3,11},{4,12},{5,13},{6,14},{7,15},{8,0},{9,1},... | collective-permute-start | bytes 49160 | tf_op jit(solution)/shard_map/ppermute | solution.py:72
  25.9 4.6 %collective-permute-start.11 = (f32[32,128]{1,0:T(8,128)S(1)}, f32[32,128]{1,0:T(8,128)S(1)}, u32[]{:S(2)}, u32[]{:S(2)}) collective-permute-start(f32[32,128]{1,0:T(8,128)S(1)} %get-tuple-element.97), channel_id=1, source_target_pairs={{0,24},{1,25},{2,26},{3,27},{4,28},{5,29},{6,30},{7,31},{8,16},{9,... | collective-permute-start | bytes 49160 | tf_op jit(solution)/shard_map/ppermute | solution.py:72
  27.6 3.7 %collective-permute-start.13 = (f32[32,128]{1,0:T(8,128)S(1)}, f32[32,128]{1,0:T(8,128)S(1)}, u32[]{:S(2)}, u32[]{:S(2)}) collective-permute-start(f32[32,128]{1,0:T(8,128)S(1)} %get-tuple-element.95.refs_7_), channel_id=1, source_target_pairs={{0,1},{1,0},{2,3},{3,2},{4,5},{5,4},{6,7},{7,6},{8,9},{9,8},{10,11... | collective-permute-start | bytes 49160 | tf_op jit(solution)/shard_map/ppermute | solution.py:72
  29.0 2.3 %collective-permute-start.14 = (f32[32,128]{1,0:T(8,128)S(1)}, f32[32,128]{1,0:T(8,128)S(1)}, u32[]{:S(2)}, u32[]{:S(2)}) collective-permute-start(f32[32,128]{1,0:T(8,128)S(1)} %get-tuple-element.95.refs_7_), channel_id=1, source_target_pairs={{0,8},{1,2},{2,1},{3,11},{4,12},{5,6},{6,5},{7,15},{8,0},{9,10},{1... | collective-permute-start | bytes 49160 | tf_op jit(solution)/shard_map/ppermute | solution.py:72

commit v7 on v5

--- a/solution.py
+++ b/solution.py
@@ -233,7 +233,8 @@
 
 def divergence(k, fields, axis, index):
     last = index == k.shape[axis] - 1
-    up, down = 0.5 * (k + ahead(k, axis)), 0.5 * (k + behind(k, axis))
+    half = 0.5 * k
+    up, down = half + ahead(half, axis), half + behind(half, axis)
     up, down = jnp.where(last, 0.0, up), jnp.where(index == 0, 0.0, down)
     return [up * (ahead(v, axis) - v) + down * (behind(v, axis) - v) for v in fields]
 
@@ -248,15 +249,15 @@
     return up + jnp.where(index == 0, 0.0, pltpu.roll(value, 1, axis))
 
 
-def log1p_of(e, u, inv):
-    return jnp.log(u) + (e - (u - 1.0)) * inv
+def log1p_of(e, u):
+    return jnp.log(u) + (e - (u - 1.0))
 
 
 def softplus_parts(v):
     e = jnp.exp(-jnp.abs(v))
     u = 1.0 + e
     inv = 1.0 / u
-    soft = jnp.maximum(v, 0.0) + log1p_of(e, u, inv)
+    soft = jnp.maximum(v, 0.0) + log1p_of(e, u)
     return soft, jnp.where(v >= 0, inv, e * inv)
 
 

time: 33.4 us -> 33.4 us (level)
  no operation moved by 1% of the time
where the time goes in v7:
time: 33.4 us; the launch traced here: 33.2 us
  starting transfers between devices  18.7 us (56%)
  Pallas kernels  12.6 us (38%)
  waiting for transfers between devices  1.1 us (3%)
  between operations  0.78 us (2%)
    ppermute x15, starting transfers between devices, exchange(): lax.ppermute(p, AXES, swap_pairs(counts, axis, kind))  16 us
    pallas_call x9, Pallas kernels, call(): pl.pallas_call(kernel, out_shape=[jax.ShapeDtypeStruct(s, d) for s, d in...  12.6 us
    all_to_all x1, starting transfers between devices, per_device(): sums = lax.all_to_all(sums, AXES, 0, 0, tiled=True)  2.75 us
    ppermute x15, waiting for transfers between devices, exchange(): lax.ppermute(p, AXES, swap_pairs(counts, axis, kind))  0.82 us
  transfers between devices with their start and end apart: 16, of which 2 were waited for; matrix products, arithmetic and copies ran while one was open for 0% of the time, Pallas kernels for 21%

profile of v7, /device:TPU:0, one launch (start us, length us, event | category | flops | bytes accessed | tf_op | source)
XLA Modules:
  0.0 33.2 jit_solution(14348898434538256702)
XLA Ops:
  0.6 2.9 %prepare.1 = (f32[1024,128]{1,0:T(8,128)S(1)}, f32[1024,128]{1,0:T(8,128)S(1)}, f32[1024,128]{1,0:T(8,128)S(1)}, f32[1024,128]{1,0:T(8,128)S(1)}, f32[1024,128]{...) custom-call(f32[8,1024,128]{2,1,0:T(8,128)} %bitcast.16, ...), custom_call_target="tpu_custom_call" | custom-call | bytes 5242880 | tf_op jit(solution)/shard_map/prepare/pallas_call | solution.py:608
  3.6 3.0 %collective-permute-start.2 = (f32[192,128]{1,0:T(8,128)S(1)}, f32[192,128]{1,0:T(8,128)S(1)}, u32[]{:S(2)}, u32[]{:S(2)}) collective-permute-start(f32[192,128]{1,0:T(8,128)S(1)} %get-tuple-element.68), channel_id=1, source_target_pairs={{0,4},{1,5},{2,6},{3,7},{4,0},{5,1},{6,2},{7,3},{8,12},{9,13},{10,... | collective-permute-start | bytes 294920 | tf_op jit(solution)/shard_map/ppermute | solution.py:72
  6.6 1.6 %collective-permute-start.3 = (f32[48,128]{1,0:T(8,128)S(1)}, f32[48,128]{1,0:T(8,128)S(1)}, u32[]{:S(2)}, u32[]{:S(2)}) collective-permute-start(f32[48,128]{1,0:T(8,128)S(1)} %get-tuple-element.65.refs_7_), channel_id=1, source_target_pairs={{0,1},{1,0},{2,3},{3,2},{4,5},{5,4},{6,7},{7,6},{8,9},{9,8},{10,11... | collective-permute-start | bytes 73736 | tf_op jit(solution)/shard_map/ppermute | solution.py:72
  8.2 0.5 %collective-permute-start = (f32[48,128]{1,0:T(8,128)S(1)}, f32[48,128]{1,0:T(8,128)S(1)}, u32[]{:S(2)}, u32[]{:S(2)}) collective-permute-start(f32[48,128]{1,0:T(8,128)S(1)} %get-tuple-element.66), channel_id=1, source_target_pairs={{0,8},{1,9},{2,10},{3,11},{4,12},{5,13},{6,14},{7,15},{8,0},{9,1},... | collective-permute-start | bytes 73736 | tf_op jit(solution)/shard_map/ppermute | solution.py:72
  8.7 1.1 %collective-permute-start.1 = (f32[48,128]{1,0:T(8,128)S(1)}, f32[48,128]{1,0:T(8,128)S(1)}, u32[]{:S(2)}, u32[]{:S(2)}) collective-permute-start(f32[48,128]{1,0:T(8,128)S(1)} %get-tuple-element.67), channel_id=1, source_target_pairs={{0,24},{1,25},{2,26},{3,27},{4,28},{5,29},{6,30},{7,31},{8,16},{9,... | collective-permute-start | bytes 73736 | tf_op jit(solution)/shard_map/ppermute | solution.py:72
  9.8 2.1 %first_inner.1 = (f32[1024,128]{1,0:T(8,128)S(1)}, f32[1024,128]{1,0:T(8,128)S(1)}, f32[1024,128]{1,0:T(8,128)S(1)}, f32[1024,128]{1,0:T(8,128)S(1)}, f32[1024,1...) custom-call(f32[1024,128]{1,0:T(8,128)S(1)} %get-tuple-element.53.refs_0_, ...), custom_call_target="tpu_custom_call" | custom-call | flops 13107200 | bytes 3145728 | tf_op jit(solution)/shard_map/first_inner/pallas_call | solution.py:608
  12.0 0.0 collective-permute-done.1.refs_9_
  12.0 0.7 %first_edge.1 = (f32[1024,128]{1,0:T(8,128)S(1)}, f32[1024,128]{1,0:T(8,128)S(1)}, f32[1024,128]{1,0:T(8,128)S(1)}, f32[2,64,128]{2,1,0:T(8,128)S(1)}, f32[2,256...) custom-call(f32[1024,128]{1,0:T(8,128)S(1)} %get-tuple-element.58.re, ...), custom_call_target="tpu_custom_call" | custom-call | bytes 2596864 | tf_op jit(solution)/shard_map/first_edge/pallas_call | solution.py:608
  12.7 0.6 %collective-permute-start.7 = (f32[256,128]{1,0:T(8,128)S(1)}, f32[256,128]{1,0:T(8,128)S(1)}, u32[]{:S(2)}, u32[]{:S(2)}) collective-permute-start(f32[256,128]{1,0:T(8,128)S(1)} %get-tuple-element.84), channel_id=1, source_target_pairs={{0,4},{1,5},{2,6},{3,7},{4,0},{5,1},{6,2},{7,3},{8,12},{9,13},{10,... | collective-permute-start | bytes 393224 | tf_op jit(solution)/shard_map/ppermute | solution.py:72
  13.3 0.2 collective-permute-start.5
  13.5 1.4 %collective-permute-start.6 = (f32[64,128]{1,0:T(8,128)S(1)}, f32[64,128]{1,0:T(8,128)S(1)}, u32[]{:S(2)}, u32[]{:S(2)}) collective-permute-start(f32[64,128]{1,0:T(8,128)S(1)} %get-tuple-element.83), channel_id=1, source_target_pairs={{0,24},{1,25},{2,26},{3,27},{4,28},{5,29},{6,30},{7,31},{8,16},{9,... | collective-permute-start | bytes 98312 | tf_op jit(solution)/shard_map/ppermute | solution.py:72
  14.9 2.6 %collective-permute-start.8 = (f32[64,128]{1,0:T(8,128)S(1)}, f32[64,128]{1,0:T(8,128)S(1)}, u32[]{:S(2)}, u32[]{:S(2)}) collective-permute-start(f32[64,128]{1,0:T(8,128)S(1)} %get-tuple-element.81.refs_6_), channel_id=1, source_target_pairs={{0,1},{1,0},{2,3},{3,2},{4,5},{5,4},{6,7},{7,6},{8,9},{9,8},{10,11... | collective-permute-start | bytes 98312 | tf_op jit(solution)/shard_map/ppermute | solution.py:72
  17.5 2.2 %second_inner.1 = (f32[1024,128]{1,0:T(8,128)S(1)}, f32[1024,128]{1,0:T(8,128)S(1)}, f32[1024,128]{1,0:T(8,128)S(1)}, f32[1024,128]{1,0:T(8,128)S(1)}, f32[1024,128]{1,0:T(8,128)S(1)}) custom-call(f32[1024,128]{1,0:T(8,128)S(1)} %get-tuple-element.69.refs_0_, f32[1024,128]{1,0:T(8,128)S(1)} %get-tuple-element.70.refs_1_, ...), custom_call_target="tpu_custom_call" | custom-call | flops 13107200 | bytes 4718592 | tf_op jit(solution)/shard_map/second_inner/pallas_call | solution.py:608
  19.7 1.4 %second_edge.1 = (f32[1024,128]{1,0:T(8,128)S(1)}, f32[1024,128]{1,0:T(8,128)S(1)}, f32[32,128]{1,0:T(8,128)}, f32[2,16,128]{2,1,0:T(8,128)S(1)}, f32[2,64,128]{...) custom-call(f32[1024,128]{1,0:T(8,128)S(1)} %get-tuple-element.75.re, ...), custom_call_target="tpu_custom_call" | custom-call | bytes 2719744 | tf_op jit(solution)/shard_map/second_edge/pallas_call | solution.py:608
  21.2 1.6 %collective-permute-start.12 = (f32[128,128]{1,0:T(8,128)S(1)}, f32[128,128]{1,0:T(8,128)S(1)}, u32[]{:S(2)}, u32[]{:S(2)}) collective-permute-start(f32[128,128]{1,0:T(8,128)S(1)} %choose.1), channel_id=1, source_target_pairs={{0,4},{1,5},{2,6},{3,7},{4,0},{5,1},{6,2},{7,3},{8,12},{9,13},{10,... | collective-permute-start | bytes 196616 | tf_op jit(solution)/shard_map/ppermute | solution.py:72
  22.7 2.7 %all-to-all-start = ((f32[32,1,128]{2,1,0:T(1,128)}), f32[32,1,128]{2,1,0:T(1,128)S(1)}, u32[]{:S(2)}, u32[]{:S(2)}) async-start(f32[32,1,128]{2,1,0:T(1,128)} %bitcast.6), calls=%async_computation | async-start | bytes 32768 | tf_op jit(solution)/shard_map/all_to_all | solution.py:686
  25.5 0.3 collective-permute-start.10
  25.8 1.6 %collective-permute-start.11 = (f32[32,128]{1,0:T(8,128)S(1)}, f32[32,128]{1,0:T(8,128)S(1)}, u32[]{:S(2)}, u32[]{:S(2)}) collective-permute-start(f32[32,128]{1,0:T(8,128)S(1)} %get-tuple-element.97), channel_id=1, source_target_pairs={{0,24},{1,25},{2,26},{3,27},{4,28},{5,29},{6,30},{7,31},{8,16},{9,... | collective-permute-start | bytes 49160 | tf_op jit(solution)/shard_map/ppermute | solution.py:72
  27.4 1.5 %collective-permute-start.13 = (f32[32,128]{1,0:T(8,128)S(1)}, f32[32,128]{1,0:T(8,128)S(1)}, u32[]{:S(2)}, u32[]{:S(2)}) collective-permute-start(f32[32,128]{1,0:T(8,128)S(1)} %get-tuple-element.95.refs_7_), channel_id=1, source_target_pairs={{0,1},{1,0},{2,3},{3,2},{4,5},{5,4},{6,7},{7,6},{8,9},{9,8},{10,11... | collective-permute-start | bytes 49160 | tf_op jit(solution)/shard_map/ppermute | solution.py:72
  28.9 1.5 %third_inner.1 = (f32[1024,128]{1,0:T(8,128)S(1)}, f32[2,16,128]{2,1,0:T(8,128)S(1)}, f32[2,64,128]{2,1,0:T(8,128)S(1)}) custom-call(f32[1024,128]{1,0:T(8,128)S(1)} %get-tuple-element.69.refs_0_, f32[1024,128]{1,0:T(8,128)S(1)} %get-tuple-element.61.refs_3_.refs_2_.refs_1_, ...), custom_call_target="tpu_custom_call", output_to_operand_aliasing={{0}: (5, {})} | custom-call | flops 13107200 | bytes 3145728 | tf_op jit(solution)/shard_map/third_inner/pallas_call | solution.py:608
  30.4 0.8 %collective-permute-done.13.refs_11_ = f32[32,128]{1,0:T(8,128)S(1)} collective-permute-done((f32[32,128]{1,0:T(8,128)S(1)}, f32[32,128]{1,0:T(8,128)S(1)}, u32[]{:S(2)}, u32[]{:S(2)}) %collective-permute-start.13) | collective-permute-done | bytes 16416 | tf_op jit(solution)/shard_map/ppermute | solution.py:72
  31.2 1.1 %finish.1 = f32[1024,128]{1,0:T(8,128)} custom-call(f32[1024,128]{1,0:T(8,128)S(1)} %get-tuple-element.73.refs_5_.refs_4_.refs_0_, f32[1024,128]{1,0:T(8,128)S(1)} %get-tuple-element.89.refs_1_, f32[2,16,128]{2,1,0:T(8,128)S(1)} %get-tuple-element.90.refs_2_, f32[2,64,128]{2,1,0:T(8,128)S(1)} %get-tuple-element.91.refs_3_, ...), custom_call_target="tpu_custom_call" | custom-call | flops 13107200 | bytes 1368064 | tf_op jit(solution)/shard_map/finish/pallas_call | solution.py:608
  32.3 0.3 all-to-all-done
  32.6 0.6 %totals.1 = (f32[1,1]{1,0:T(1,128)}, f32[1,1]{1,0:T(1,128)}) custom-call(f32[32,128]{1,0:T(8,128)S(1)} %bitcast.15), custom_call_target="tpu_custom_call" | custom-call | bytes 16384 | tf_op jit(solution)/shard_map/totals/pallas_call | solution.py:608
  (21 shorter events, 0.1 us)
Async XLA Ops:
  0.6 9.2 %copy-start = (f32[64,16,128]{2,1,0:T(8,128)S(1)}, f32[64,16,128]{2,1,0:T(8,128)}, u32[]{:S(2)}) copy-start(f32[64,16,128]{2,1,0:T(8,128)} %param.8) | copy-start | bytes 1572868
  3.6 13.9 %copy-start.1 = (bf16[2,64,16,128]{3,2,1,0:T(8,128)(2,1)S(1)}, bf16[2,64,16,128]{3,2,1,0:T(8,128)(2,1)}, u32[]{:S(2)}) copy-start(bf16[2,64,16,128]{3,2,1,0:T(8,128)(2,1)} %param.9) | copy-start | bytes 1572868
  3.6 8.4 %collective-permute-start.2 = (f32[192,128]{1,0:T(8,128)S(1)}, f32[192,128]{1,0:T(8,128)S(1)}, u32[]{:S(2)}, u32[]{:S(2)}) collective-permute-start(f32[192,128]{1,0:T(8,128)S(1)} %get-tuple-element.68), channel_id=1, source_target_pairs={{0,4},{1,5},{2,6},{3,7},{4,0},{5,1},{6,2},{7,3},{8,12},{9,13},{10,... | collective-permute-start | bytes 294920 | tf_op jit(solution)/shard_map/ppermute | solution.py:72
  6.6 5.4 %collective-permute-start.3 = (f32[48,128]{1,0:T(8,128)S(1)}, f32[48,128]{1,0:T(8,128)S(1)}, u32[]{:S(2)}, u32[]{:S(2)}) collective-permute-start(f32[48,128]{1,0:T(8,128)S(1)} %get-tuple-element.65.refs_7_), channel_id=1, source_target_pairs={{0,1},{1,0},{2,3},{3,2},{4,5},{5,4},{6,7},{7,6},{8,9},{9,8},{10,11... | collective-permute-start | bytes 73736 | tf_op jit(solution)/shard_map/ppermute | solution.py:72
  8.1 3.8 %collective-permute-start.4 = (f32[48,128]{1,0:T(8,128)S(1)}, f32[48,128]{1,0:T(8,128)S(1)}, u32[]{:S(2)}, u32[]{:S(2)}) collective-permute-start(f32[48,128]{1,0:T(8,128)S(1)} %get-tuple-element.65.refs_7_), channel_id=1, source_target_pairs={{0,8},{1,2},{2,1},{3,11},{4,12},{5,6},{6,5},{7,15},{8,0},{9,10},{1... | collective-permute-start | bytes 73736 | tf_op jit(solution)/shard_map/ppermute | solution.py:72
  8.2 3.8 %collective-permute-start = (f32[48,128]{1,0:T(8,128)S(1)}, f32[48,128]{1,0:T(8,128)S(1)}, u32[]{:S(2)}, u32[]{:S(2)}) collective-permute-start(f32[48,128]{1,0:T(8,128)S(1)} %get-tuple-element.66), channel_id=1, source_target_pairs={{0,8},{1,9},{2,10},{3,11},{4,12},{5,13},{6,14},{7,15},{8,0},{9,1},... | collective-permute-start | bytes 73736 | tf_op jit(solution)/shard_map/ppermute | solution.py:72
  8.7 3.3 %collective-permute-start.1 = (f32[48,128]{1,0:T(8,128)S(1)}, f32[48,128]{1,0:T(8,128)S(1)}, u32[]{:S(2)}, u32[]{:S(2)}) collective-permute-start(f32[48,128]{1,0:T(8,128)S(1)} %get-tuple-element.67), channel_id=1, source_target_pairs={{0,24},{1,25},{2,26},{3,27},{4,28},{5,29},{6,30},{7,31},{8,16},{9,... | collective-permute-start | bytes 73736 | tf_op jit(solution)/shard_map/ppermute | solution.py:72
  12.7 7.1 %collective-permute-start.7 = (f32[256,128]{1,0:T(8,128)S(1)}, f32[256,128]{1,0:T(8,128)S(1)}, u32[]{:S(2)}, u32[]{:S(2)}) collective-permute-start(f32[256,128]{1,0:T(8,128)S(1)} %get-tuple-element.84), channel_id=1, source_target_pairs={{0,4},{1,5},{2,6},{3,7},{4,0},{5,1},{6,2},{7,3},{8,12},{9,13},{10,... | collective-permute-start | bytes 393224 | tf_op jit(solution)/shard_map/ppermute | solution.py:72
  13.3 6.4 %collective-permute-start.5 = (f32[64,128]{1,0:T(8,128)S(1)}, f32[64,128]{1,0:T(8,128)S(1)}, u32[]{:S(2)}, u32[]{:S(2)}) collective-permute-start(f32[64,128]{1,0:T(8,128)S(1)} %get-tuple-element.82), channel_id=1, source_target_pairs={{0,8},{1,9},{2,10},{3,11},{4,12},{5,13},{6,14},{7,15},{8,0},{9,1},... | collective-permute-start | bytes 98312 | tf_op jit(solution)/shard_map/ppermute | solution.py:72
  13.5 6.2 %collective-permute-start.6 = (f32[64,128]{1,0:T(8,128)S(1)}, f32[64,128]{1,0:T(8,128)S(1)}, u32[]{:S(2)}, u32[]{:S(2)}) collective-permute-start(f32[64,128]{1,0:T(8,128)S(1)} %get-tuple-element.83), channel_id=1, source_target_pairs={{0,24},{1,25},{2,26},{3,27},{4,28},{5,29},{6,30},{7,31},{8,16},{9,... | collective-permute-start | bytes 98312 | tf_op jit(solution)/shard_map/ppermute | solution.py:72
  14.9 4.8 %collective-permute-start.8 = (f32[64,128]{1,0:T(8,128)S(1)}, f32[64,128]{1,0:T(8,128)S(1)}, u32[]{:S(2)}, u32[]{:S(2)}) collective-permute-start(f32[64,128]{1,0:T(8,128)S(1)} %get-tuple-element.81.refs_6_), channel_id=1, source_target_pairs={{0,1},{1,0},{2,3},{3,2},{4,5},{5,4},{6,7},{7,6},{8,9},{9,8},{10,11... | collective-permute-start | bytes 98312 | tf_op jit(solution)/shard_map/ppermute | solution.py:72
  17.5 2.3 %collective-permute-start.9 = (f32[64,128]{1,0:T(8,128)S(1)}, f32[64,128]{1,0:T(8,128)S(1)}, u32[]{:S(2)}, u32[]{:S(2)}) collective-permute-start(f32[64,128]{1,0:T(8,128)S(1)} %get-tuple-element.81.refs_6_), channel_id=1, source_target_pairs={{0,8},{1,2},{2,1},{3,11},{4,12},{5,6},{6,5},{7,15},{8,0},{9,10},{1... | collective-permute-start | bytes 98312 | tf_op jit(solution)/shard_map/ppermute | solution.py:72
  21.2 10.0 %collective-permute-start.12 = (f32[128,128]{1,0:T(8,128)S(1)}, f32[128,128]{1,0:T(8,128)S(1)}, u32[]{:S(2)}, u32[]{:S(2)}) collective-permute-start(f32[128,128]{1,0:T(8,128)S(1)} %choose.1), channel_id=1, source_target_pairs={{0,4},{1,5},{2,6},{3,7},{4,0},{5,1},{6,2},{7,3},{8,12},{9,13},{10,... | collective-permute-start | bytes 196616 | tf_op jit(solution)/shard_map/ppermute | solution.py:72
  22.7 9.9 %all-to-all-start = ((f32[32,1,128]{2,1,0:T(1,128)}), f32[32,1,128]{2,1,0:T(1,128)S(1)}, u32[]{:S(2)}, u32[]{:S(2)}) async-start(f32[32,1,128]{2,1,0:T(1,128)} %bitcast.6), calls=%async_computation | async-start | bytes 32768 | tf_op jit(solution)/shard_map/all_to_all | solution.py:686
  25.5 4.9 %collective-permute-start.10 = (f32[32,128]{1,0:T(8,128)S(1)}, f32[32,128]{1,0:T(8,128)S(1)}, u32[]{:S(2)}, u32[]{:S(2)}) collective-permute-start(f32[32,128]{1,0:T(8,128)S(1)} %get-tuple-element.96), channel_id=1, source_target_pairs={{0,8},{1,9},{2,10},{3,11},{4,12},{5,13},{6,14},{7,15},{8,0},{9,1},... | collective-permute-start | bytes 49160 | tf_op jit(solution)/shard_map/ppermute | solution.py:72
  25.8 4.6 %collective-permute-start.11 = (f32[32,128]{1,0:T(8,128)S(1)}, f32[32,128]{1,0:T(8,128)S(1)}, u32[]{:S(2)}, u32[]{:S(2)}) collective-permute-start(f32[32,128]{1,0:T(8,128)S(1)} %get-tuple-element.97), channel_id=1, source_target_pairs={{0,24},{1,25},{2,26},{3,27},{4,28},{5,29},{6,30},{7,31},{8,16},{9,... | collective-permute-start | bytes 49160 | tf_op jit(solution)/shard_map/ppermute | solution.py:72
  27.4 3.7 %collective-permute-start.13 = (f32[32,128]{1,0:T(8,128)S(1)}, f32[32,128]{1,0:T(8,128)S(1)}, u32[]{:S(2)}, u32[]{:S(2)}) collective-permute-start(f32[32,128]{1,0:T(8,128)S(1)} %get-tuple-element.95.refs_7_), channel_id=1, source_target_pairs={{0,1},{1,0},{2,3},{3,2},{4,5},{5,4},{6,7},{7,6},{8,9},{9,8},{10,11... | collective-permute-start | bytes 49160 | tf_op jit(solution)/shard_map/ppermute | solution.py:72
  28.9 2.3 %collective-permute-start.14 = (f32[32,128]{1,0:T(8,128)S(1)}, f32[32,128]{1,0:T(8,128)S(1)}, u32[]{:S(2)}, u32[]{:S(2)}) collective-permute-start(f32[32,128]{1,0:T(8,128)S(1)} %get-tuple-element.95.refs_7_), channel_id=1, source_target_pairs={{0,8},{1,2},{2,1},{3,11},{4,12},{5,6},{6,5},{7,15},{8,0},{9,10},{1... | collective-permute-start | bytes 49160 | tf_op jit(solution)/shard_map/ppermute | solution.py:72
